TPU v7x, 512 devices: a whole 4x4x16 slice. The times are simulated.
512 devices in a mesh: seq: 128 (over z, x_hi, y), tp: 4 (over x_lo, core).
Axes of the slice: x: 4 (x_hi: 2, x_lo: 2; x = x_hi * 2 + x_lo), y: 4, z: 16, core: 2. Of those that a mesh axis runs over, the one named last changes fastest.
Arguments:
- latent: bfloat16 [32768, 3072], P(('seq', 'tp')), may hold values from -6 to 6
- queries: bfloat16 [32768, 1536], P('seq', 'tp'), may hold values from -40 to 40
- key_vectors: bfloat16 [32768, 1536], P('seq', 'tp'), may hold values from -40 to 40
- value_vectors: bfloat16 [32768, 1536], P('seq', 'tp'), may hold values from -6 to 6
- proj_weight: bfloat16 [1536, 3072], P('tp'), may hold values from -0.15625 to 0.15625
- gate_scale: float32 [8, 3072], replicated, may hold values from -2 to 2
- text_length: int32 [8], replicated, may hold values from 64 to 128, as said below
- split_table: int32 [8, 16], replicated, may hold values from 64 to 256, as said below
Outputs:
- updated: bfloat16 [32768, 3072], P(('seq', 'tp'))
Inputs may be any that keep to these rules, and one draw needn't show every extreme that they name: `text_length`: some request has exactly 128 text tokens; text tokens are the first positions of a request. `split_table`: live slots of a device are its first ones; some request has an index of its group with all 256 slots live.
All inputs are finite; a program needn't handle non-finite values.
Results may differ from a plain program's by a relative error of at most 0.0075.
Values may be sent and summed in bfloat16 or wider, within the bound.
No kernel may reach another device: no remote copies, remote signals or barrier semaphores. Data moves between devices by JAX's collectives and lax.ppermute only.
A program may use at most 64 MiB of HBM per device.

v0:
```python
import math

import jax
import jax.numpy as jnp
from jax import lax
from jax.sharding import PartitionSpec as P

HEAD_DIM = 128


def shortened(shard):
    return jax.tree.map(lambda a: a.astype(jnp.bfloat16) if a.dtype == jnp.float32 else a, shard)


def from_partner(block, axis, stride):
    count = lax.axis_size(axis)
    route = []
    for low in range(count):
        high = low | 1 << stride
        if high != low and high < count:
            route += [(low, high), (high, low)]
    return lax.ppermute(block, axis, route)


def hop_block(moving, bit_number):
    return jax.tree.map(
        lambda part, own: part.astype(own.dtype),
        from_partner(shortened(moving), "seq", bit_number),
        moving,
    )


def on_device(
    latent, queries, key_vectors, value_vectors, proj_weight, gate_scale, text_length, split_table
):
    group_size = split_table.shape[1]
    tokens = queries.shape[0]
    feature_width = queries.shape[1]
    head_count = feature_width // HEAD_DIM
    seq_index = lax.axis_index("seq")
    item_index = seq_index // group_size
    group_place = seq_index % group_size
    counts = lax.dynamic_index_in_dim(split_table, item_index, 0, keepdims=False)
    members = jnp.arange(group_size, dtype=jnp.int32)
    offset = jnp.sum(jnp.where(members < group_place, counts, 0))
    own_count = jnp.sum(jnp.where(members == group_place, counts, 0))
    slot_index = jnp.arange(tokens, dtype=jnp.int32)
    query_live = slot_index < own_count
    text_count = jnp.sum(
        jnp.where(jnp.arange(text_length.shape[0], dtype=jnp.int32) == item_index, text_length, 0)
    )
    image_mask = query_live & (offset + slot_index >= text_count)
    query_heads = queries.reshape(tokens, head_count, HEAD_DIM)
    score_scale = 1.0 / math.sqrt(HEAD_DIM)

    def absorb(softmax_carry, stacked, key_live):
        running_max, running_sum, running_acc = softmax_carry
        length = stacked.shape[1]
        key_heads = stacked[0].reshape(length, head_count, HEAD_DIM)
        value_heads = stacked[1].reshape(length, head_count, HEAD_DIM)
        scores = (
            jnp.einsum("qhd,khd->qhk", query_heads, key_heads, preferred_element_type=jnp.float32)
            * score_scale
        )
        scores = jnp.where(key_live[None, None, :], scores, -1e30)
        new_max = jnp.maximum(running_max, jnp.max(scores, axis=2))
        shrink = jnp.exp(running_max - new_max)
        weights = jnp.exp(scores - new_max[:, :, None]) * key_live[None, None, :].astype(
            jnp.float32
        )
        running_sum = running_sum * shrink + jnp.sum(weights, axis=2)
        running_acc = running_acc * shrink[:, :, None] + jnp.einsum(
            "qhk,khd->qhd",
            weights.astype(jnp.bfloat16),
            value_heads,
            preferred_element_type=jnp.float32,
        )
        return (new_max, running_sum, running_acc)

    stacked = jnp.stack([key_vectors, value_vectors])
    softmax_carry = (
        jnp.full((tokens, head_count), -1e30, jnp.float32),
        jnp.zeros((tokens, head_count), jnp.float32),
        jnp.zeros((tokens, head_count, HEAD_DIM), jnp.float32),
    )
    softmax_carry = absorb(softmax_carry, stacked, query_live)
    bit_total = group_size.bit_length() - 1

    def make_branch(bit_number):

        def branch(moving):
            return hop_block(moving, bit_number)

        return branch

    branch_list = [make_branch(bit_number) for bit_number in range(bit_total)]

    def cycle_step(step_index, loop_carry):
        inner_carry, moving = loop_carry
        trailing = jnp.int32(0)
        for bit_number in range(bit_total - 1):
            trailing = trailing + (step_index % (2 << bit_number) == 0).astype(jnp.int32)
        moving = lax.switch(trailing, branch_list, moving)
        anchor = jnp.bitwise_xor(group_place, jnp.bitwise_xor(step_index, step_index // 2))
        anchor_count = jnp.sum(jnp.where(members == anchor, counts, 0))
        return (absorb(inner_carry, moving, slot_index < anchor_count), moving)

    softmax_carry, moving = lax.fori_loop(1, group_size, cycle_step, (softmax_carry, stacked))
    running_max, running_sum, running_acc = softmax_carry
    attended = (
        (running_acc / running_sum[:, :, None]).reshape(tokens, feature_width).astype(jnp.bfloat16)
    )
    row_share = tokens // lax.axis_size("tp")
    projected = lax.psum_scatter(
        jnp.dot(attended, proj_weight, preferred_element_type=jnp.float32).astype(jnp.bfloat16),
        "tp",
        scatter_dimension=0,
        tiled=True,
    ).astype(jnp.float32)
    tp_first = lax.axis_index("tp") * row_share
    my_image = lax.dynamic_slice_in_dim(image_mask, tp_first, row_share, 0)
    gate_row = lax.dynamic_index_in_dim(gate_scale, item_index, 0, keepdims=False)
    residual_base = latent.astype(jnp.float32)
    return jnp.where(
        my_image[:, None], residual_base + gate_row[None, :] * projected, residual_base
    ).astype(jnp.bfloat16)


def solution(mesh):
    in_specs = (
        P(("seq", "tp"), None),
        P("seq", "tp"),
        P("seq", "tp"),
        P("seq", "tp"),
        P("tp", None),
        P(),
        P(),
        P(),
    )
    out_specs = P(("seq", "tp"), None)
    return jax.shard_map(
        on_device, mesh=mesh, in_specs=in_specs, out_specs=out_specs, check_vma=False
    )
```

profile of v0, /device:TPU:1, one launch (start us, length us, event | category | flops | bytes accessed | tf_op | source)
XLA Modules:
  0.0 369.8 jit_solution(10075945977083472106)
XLA Ops:
  19.1 285.9 %while.35 = (s32[]{:T(128)}, f32[256,3]{0,1:T(4,128)S(1)}, f32[256,3]{0,1:T(4,128)}, f32[256,3,128]{0,2,1:T(8,128)}, bf16[2,256,384]{2,1,0:T(8,128)(2,1)S(1)}, /...) while((s32[]{:T(128)}, f32[256,3]{0,1:T(4,128)S(1)}, ...), condition=%wide.region_13.14_spmd.clone, body=%wide.region_5.13_spmd.clone.sunk | while | flops 102631520 | bytes 7721172 | solution.py:108
  19.2 9.3 %conditional.3 = (bf16[2,256,384]{2,1,0:T(8,128)(2,1)}) conditional(s32[]{:T(128)} %clamp.13, bf16[2,256,384]{2,1,0:T(8,128)(2,1)S(1)} %get-tuple-element.462, bf16[2,256,384]{2,1,0:T(8,128)(2,1)S(1)} %get-tuple-element.462, bf16[2,256,384]{2,1,0:T(8,128)(2,1)S(1)} %get-tuple-element.462, ...), branch_computations={%region_7.7_spmd, %region_8.8_spmd, %region_9.9_spmd, %region_10.1... | conditional | bytes 1572912 | solution.py:103
  37.5 15.2 %conditional.3 = (bf16[2,256,384]{2,1,0:T(8,128)(2,1)}) conditional(s32[]{:T(128)} %clamp.13, bf16[2,256,384]{2,1,0:T(8,128)(2,1)S(1)} %get-tuple-element.462, bf16[2,256,384]{2,1,0:T(8,128)(2,1)S(1)} %get-tuple-element.462, bf16[2,256,384]{2,1,0:T(8,128)(2,1)S(1)} %get-tuple-element.462, ...), branch_computations={%region_7.7_spmd, %region_8.8_spmd, %region_9.9_spmd, %region_10.1... | conditional | bytes 1572912 | solution.py:103
  37.5 8.3 %collective-permute-start.1 = (bf16[2,256,384]{2,1,0:T(8,128)(2,1)S(1)}, bf16[2,256,384]{2,1,0:T(8,128)(2,1)}, u32[]{:S(2)}, u32[]{:S(2)}) collective-permute-start(bf16[2,256,384]{2,1,0:T(8,128)(2,1)S(1)} %param.1), channel_id=1, source_target_pairs={{0,8},{8,0},{4,12},{12,4},{16,24},{24,16},{20,28},{28,20},{32,40},... | collective-permute-start | bytes 1179656 | tf_op jit(solution)/shard_map/while/body/eval_jaxpr/cond/branch_1_fun/ppermute | solution.py:22
  45.9 6.8 %collective-permute-done.1 = bf16[2,256,384]{2,1,0:T(8,128)(2,1)} collective-permute-done((bf16[2,256,384]{2,1,0:T(8,128)(2,1)S(1)}, bf16[2,256,384]{2,1,0:T(8,128)(2,1)}, u32[]{:S(2)}, u32[]{:S(2)}) %collective-permute-start.1) | collective-permute-done | bytes 393248 | tf_op jit(solution)/shard_map/while/body/eval_jaxpr/cond/branch_1_fun/ppermute | solution.py:22
  61.7 9.1 %conditional.3 = (bf16[2,256,384]{2,1,0:T(8,128)(2,1)}) conditional(s32[]{:T(128)} %clamp.13, bf16[2,256,384]{2,1,0:T(8,128)(2,1)S(1)} %get-tuple-element.462, bf16[2,256,384]{2,1,0:T(8,128)(2,1)S(1)} %get-tuple-element.462, bf16[2,256,384]{2,1,0:T(8,128)(2,1)S(1)} %get-tuple-element.462, ...), branch_computations={%region_7.7_spmd, %region_8.8_spmd, %region_9.9_spmd, %region_10.1... | conditional | bytes 1572912 | solution.py:103
  64.0 6.8 %collective-permute-done = bf16[2,256,384]{2,1,0:T(8,128)(2,1)} collective-permute-done((bf16[2,256,384]{2,1,0:T(8,128)(2,1)S(1)}, bf16[2,256,384]{2,1,0:T(8,128)(2,1)}, u32[]{:S(2)}, u32[]{:S(2)}) %collective-permute-start) | collective-permute-done | bytes 393248 | tf_op jit(solution)/shard_map/while/body/eval_jaxpr/cond/branch_0_fun/ppermute | solution.py:22
  79.9 12.7 %conditional.3 = (bf16[2,256,384]{2,1,0:T(8,128)(2,1)}) conditional(s32[]{:T(128)} %clamp.13, bf16[2,256,384]{2,1,0:T(8,128)(2,1)S(1)} %get-tuple-element.462, bf16[2,256,384]{2,1,0:T(8,128)(2,1)S(1)} %get-tuple-element.462, bf16[2,256,384]{2,1,0:T(8,128)(2,1)S(1)} %get-tuple-element.462, ...), branch_computations={%region_7.7_spmd, %region_8.8_spmd, %region_9.9_spmd, %region_10.1... | conditional | bytes 1572912 | solution.py:103
  79.9 6.5 %collective-permute-start.2 = (bf16[2,256,384]{2,1,0:T(8,128)(2,1)S(1)}, bf16[2,256,384]{2,1,0:T(8,128)(2,1)}, u32[]{:S(2)}, u32[]{:S(2)}) collective-permute-start(bf16[2,256,384]{2,1,0:T(8,128)(2,1)S(1)} %param.2), channel_id=1, source_target_pairs={{0,16},{16,0},{4,20},{20,4},{8,24},{24,8},{12,28},{28,12},{32,48},... | collective-permute-start | bytes 1179656 | tf_op jit(solution)/shard_map/while/body/eval_jaxpr/cond/branch_2_fun/ppermute | solution.py:22
  86.5 6.1 %collective-permute-done.2 = bf16[2,256,384]{2,1,0:T(8,128)(2,1)} collective-permute-done((bf16[2,256,384]{2,1,0:T(8,128)(2,1)S(1)}, bf16[2,256,384]{2,1,0:T(8,128)(2,1)}, u32[]{:S(2)}, u32[]{:S(2)}) %collective-permute-start.2) | collective-permute-done | bytes 393248 | tf_op jit(solution)/shard_map/while/body/eval_jaxpr/cond/branch_2_fun/ppermute | solution.py:22
  101.6 8.6 %conditional.3 = (bf16[2,256,384]{2,1,0:T(8,128)(2,1)}) conditional(s32[]{:T(128)} %clamp.13, bf16[2,256,384]{2,1,0:T(8,128)(2,1)S(1)} %get-tuple-element.462, bf16[2,256,384]{2,1,0:T(8,128)(2,1)S(1)} %get-tuple-element.462, bf16[2,256,384]{2,1,0:T(8,128)(2,1)S(1)} %get-tuple-element.462, ...), branch_computations={%region_7.7_spmd, %region_8.8_spmd, %region_9.9_spmd, %region_10.1... | conditional | bytes 1572912 | solution.py:103
  104.8 5.4 %collective-permute-done = bf16[2,256,384]{2,1,0:T(8,128)(2,1)} collective-permute-done((bf16[2,256,384]{2,1,0:T(8,128)(2,1)S(1)}, bf16[2,256,384]{2,1,0:T(8,128)(2,1)}, u32[]{:S(2)}, u32[]{:S(2)}) %collective-permute-start) | collective-permute-done | bytes 393248 | tf_op jit(solution)/shard_map/while/body/eval_jaxpr/cond/branch_0_fun/ppermute | solution.py:22
  119.3 10.1 %conditional.3 = (bf16[2,256,384]{2,1,0:T(8,128)(2,1)}) conditional(s32[]{:T(128)} %clamp.13, bf16[2,256,384]{2,1,0:T(8,128)(2,1)S(1)} %get-tuple-element.462, bf16[2,256,384]{2,1,0:T(8,128)(2,1)S(1)} %get-tuple-element.462, bf16[2,256,384]{2,1,0:T(8,128)(2,1)S(1)} %get-tuple-element.462, ...), branch_computations={%region_7.7_spmd, %region_8.8_spmd, %region_9.9_spmd, %region_10.1... | conditional | bytes 1572912 | solution.py:103
  124.0 5.4 %collective-permute-done.1 = bf16[2,256,384]{2,1,0:T(8,128)(2,1)} collective-permute-done((bf16[2,256,384]{2,1,0:T(8,128)(2,1)S(1)}, bf16[2,256,384]{2,1,0:T(8,128)(2,1)}, u32[]{:S(2)}, u32[]{:S(2)}) %collective-permute-start.1) | collective-permute-done | bytes 393248 | tf_op jit(solution)/shard_map/while/body/eval_jaxpr/cond/branch_1_fun/ppermute | solution.py:22
  138.4 8.6 %conditional.3 = (bf16[2,256,384]{2,1,0:T(8,128)(2,1)}) conditional(s32[]{:T(128)} %clamp.13, bf16[2,256,384]{2,1,0:T(8,128)(2,1)S(1)} %get-tuple-element.462, bf16[2,256,384]{2,1,0:T(8,128)(2,1)S(1)} %get-tuple-element.462, bf16[2,256,384]{2,1,0:T(8,128)(2,1)S(1)} %get-tuple-element.462, ...), branch_computations={%region_7.7_spmd, %region_8.8_spmd, %region_9.9_spmd, %region_10.1... | conditional | bytes 1572912 | solution.py:103
  141.6 5.4 %collective-permute-done = bf16[2,256,384]{2,1,0:T(8,128)(2,1)} collective-permute-done((bf16[2,256,384]{2,1,0:T(8,128)(2,1)S(1)}, bf16[2,256,384]{2,1,0:T(8,128)(2,1)}, u32[]{:S(2)}, u32[]{:S(2)}) %collective-permute-start) | collective-permute-done | bytes 393248 | tf_op jit(solution)/shard_map/while/body/eval_jaxpr/cond/branch_0_fun/ppermute | solution.py:22
  156.1 8.7 %conditional.3 = (bf16[2,256,384]{2,1,0:T(8,128)(2,1)}) conditional(s32[]{:T(128)} %clamp.13, bf16[2,256,384]{2,1,0:T(8,128)(2,1)S(1)} %get-tuple-element.462, bf16[2,256,384]{2,1,0:T(8,128)(2,1)S(1)} %get-tuple-element.462, bf16[2,256,384]{2,1,0:T(8,128)(2,1)S(1)} %get-tuple-element.462, ...), branch_computations={%region_7.7_spmd, %region_8.8_spmd, %region_9.9_spmd, %region_10.1... | conditional | bytes 1572912 | solution.py:103
  173.9 8.6 %conditional.3 = (bf16[2,256,384]{2,1,0:T(8,128)(2,1)}) conditional(s32[]{:T(128)} %clamp.13, bf16[2,256,384]{2,1,0:T(8,128)(2,1)S(1)} %get-tuple-element.462, bf16[2,256,384]{2,1,0:T(8,128)(2,1)S(1)} %get-tuple-element.462, bf16[2,256,384]{2,1,0:T(8,128)(2,1)S(1)} %get-tuple-element.462, ...), branch_computations={%region_7.7_spmd, %region_8.8_spmd, %region_9.9_spmd, %region_10.1... | conditional | bytes 1572912 | solution.py:103
  177.0 5.5 %collective-permute-done = bf16[2,256,384]{2,1,0:T(8,128)(2,1)} collective-permute-done((bf16[2,256,384]{2,1,0:T(8,128)(2,1)S(1)}, bf16[2,256,384]{2,1,0:T(8,128)(2,1)}, u32[]{:S(2)}, u32[]{:S(2)}) %collective-permute-start) | collective-permute-done | bytes 393248 | tf_op jit(solution)/shard_map/while/body/eval_jaxpr/cond/branch_0_fun/ppermute | solution.py:22
  191.5 10.1 %conditional.3 = (bf16[2,256,384]{2,1,0:T(8,128)(2,1)}) conditional(s32[]{:T(128)} %clamp.13, bf16[2,256,384]{2,1,0:T(8,128)(2,1)S(1)} %get-tuple-element.462, bf16[2,256,384]{2,1,0:T(8,128)(2,1)S(1)} %get-tuple-element.462, bf16[2,256,384]{2,1,0:T(8,128)(2,1)S(1)} %get-tuple-element.462, ...), branch_computations={%region_7.7_spmd, %region_8.8_spmd, %region_9.9_spmd, %region_10.1... | conditional | bytes 1572912 | solution.py:103
  196.3 5.4 %collective-permute-done.1 = bf16[2,256,384]{2,1,0:T(8,128)(2,1)} collective-permute-done((bf16[2,256,384]{2,1,0:T(8,128)(2,1)S(1)}, bf16[2,256,384]{2,1,0:T(8,128)(2,1)}, u32[]{:S(2)}, u32[]{:S(2)}) %collective-permute-start.1) | collective-permute-done | bytes 393248 | tf_op jit(solution)/shard_map/while/body/eval_jaxpr/cond/branch_1_fun/ppermute | solution.py:22
  210.7 8.6 %conditional.3 = (bf16[2,256,384]{2,1,0:T(8,128)(2,1)}) conditional(s32[]{:T(128)} %clamp.13, bf16[2,256,384]{2,1,0:T(8,128)(2,1)S(1)} %get-tuple-element.462, bf16[2,256,384]{2,1,0:T(8,128)(2,1)S(1)} %get-tuple-element.462, bf16[2,256,384]{2,1,0:T(8,128)(2,1)S(1)} %get-tuple-element.462, ...), branch_computations={%region_7.7_spmd, %region_8.8_spmd, %region_9.9_spmd, %region_10.1... | conditional | bytes 1572912 | solution.py:103
  213.8 5.5 %collective-permute-done = bf16[2,256,384]{2,1,0:T(8,128)(2,1)} collective-permute-done((bf16[2,256,384]{2,1,0:T(8,128)(2,1)S(1)}, bf16[2,256,384]{2,1,0:T(8,128)(2,1)}, u32[]{:S(2)}, u32[]{:S(2)}) %collective-permute-start) | collective-permute-done | bytes 393248 | tf_op jit(solution)/shard_map/while/body/eval_jaxpr/cond/branch_0_fun/ppermute | solution.py:22
  228.3 10.1 %conditional.3 = (bf16[2,256,384]{2,1,0:T(8,128)(2,1)}) conditional(s32[]{:T(128)} %clamp.13, bf16[2,256,384]{2,1,0:T(8,128)(2,1)S(1)} %get-tuple-element.462, bf16[2,256,384]{2,1,0:T(8,128)(2,1)S(1)} %get-tuple-element.462, bf16[2,256,384]{2,1,0:T(8,128)(2,1)S(1)} %get-tuple-element.462, ...), branch_computations={%region_7.7_spmd, %region_8.8_spmd, %region_9.9_spmd, %region_10.1... | conditional | bytes 1572912 | solution.py:103
  233.0 5.5 %collective-permute-done.2 = bf16[2,256,384]{2,1,0:T(8,128)(2,1)} collective-permute-done((bf16[2,256,384]{2,1,0:T(8,128)(2,1)S(1)}, bf16[2,256,384]{2,1,0:T(8,128)(2,1)}, u32[]{:S(2)}, u32[]{:S(2)}) %collective-permute-start.2) | collective-permute-done | bytes 393248 | tf_op jit(solution)/shard_map/while/body/eval_jaxpr/cond/branch_2_fun/ppermute | solution.py:22
  247.5 8.6 %conditional.3 = (bf16[2,256,384]{2,1,0:T(8,128)(2,1)}) conditional(s32[]{:T(128)} %clamp.13, bf16[2,256,384]{2,1,0:T(8,128)(2,1)S(1)} %get-tuple-element.462, bf16[2,256,384]{2,1,0:T(8,128)(2,1)S(1)} %get-tuple-element.462, bf16[2,256,384]{2,1,0:T(8,128)(2,1)S(1)} %get-tuple-element.462, ...), branch_computations={%region_7.7_spmd, %region_8.8_spmd, %region_9.9_spmd, %region_10.1... | conditional | bytes 1572912 | solution.py:103
  250.6 5.5 %collective-permute-done = bf16[2,256,384]{2,1,0:T(8,128)(2,1)} collective-permute-done((bf16[2,256,384]{2,1,0:T(8,128)(2,1)S(1)}, bf16[2,256,384]{2,1,0:T(8,128)(2,1)}, u32[]{:S(2)}, u32[]{:S(2)}) %collective-permute-start) | collective-permute-done | bytes 393248 | tf_op jit(solution)/shard_map/while/body/eval_jaxpr/cond/branch_0_fun/ppermute | solution.py:22
  265.1 11.4 %conditional.3 = (bf16[2,256,384]{2,1,0:T(8,128)(2,1)}) conditional(s32[]{:T(128)} %clamp.13, bf16[2,256,384]{2,1,0:T(8,128)(2,1)S(1)} %get-tuple-element.462, bf16[2,256,384]{2,1,0:T(8,128)(2,1)S(1)} %get-tuple-element.462, bf16[2,256,384]{2,1,0:T(8,128)(2,1)S(1)} %get-tuple-element.462, ...), branch_computations={%region_7.7_spmd, %region_8.8_spmd, %region_9.9_spmd, %region_10.1... | conditional | bytes 1572912 | solution.py:103
  269.9 6.7 %collective-permute-done.1 = bf16[2,256,384]{2,1,0:T(8,128)(2,1)} collective-permute-done((bf16[2,256,384]{2,1,0:T(8,128)(2,1)S(1)}, bf16[2,256,384]{2,1,0:T(8,128)(2,1)}, u32[]{:S(2)}, u32[]{:S(2)}) %collective-permute-start.1) | collective-permute-done | bytes 393248 | tf_op jit(solution)/shard_map/while/body/eval_jaxpr/cond/branch_1_fun/ppermute | solution.py:22
  285.6 10.4 %conditional.3 = (bf16[2,256,384]{2,1,0:T(8,128)(2,1)}) conditional(s32[]{:T(128)} %clamp.13, bf16[2,256,384]{2,1,0:T(8,128)(2,1)S(1)} %get-tuple-element.462, bf16[2,256,384]{2,1,0:T(8,128)(2,1)S(1)} %get-tuple-element.462, bf16[2,256,384]{2,1,0:T(8,128)(2,1)S(1)} %get-tuple-element.462, ...), branch_computations={%region_7.7_spmd, %region_8.8_spmd, %region_9.9_spmd, %region_10.1... | conditional | bytes 1572912 | solution.py:103
  287.5 8.5 %collective-permute-done = bf16[2,256,384]{2,1,0:T(8,128)(2,1)} collective-permute-done((bf16[2,256,384]{2,1,0:T(8,128)(2,1)S(1)}, bf16[2,256,384]{2,1,0:T(8,128)(2,1)}, u32[]{:S(2)}, u32[]{:S(2)}) %collective-permute-start) | collective-permute-done | bytes 393248 | tf_op jit(solution)/shard_map/while/body/eval_jaxpr/cond/branch_0_fun/ppermute | solution.py:22
  311.8 49.1 %reduce-scatter.2.cloned.1.call-done = bf16[64,3072]{1,0:T(8,128)(2,1)} async-done(((bf16[256,3072]{1,0:T(8,128)(2,1)}), bf16[64,3072]{1,0:T(8,128)(2,1)}) %reduce-scatter.2.cloned.1.call-update) | async-done | bytes 393232 | tf_op jit(solution)/shard_map/reduce_scatter | solution.py:114
  (225 shorter events, 212.7 us)
Async XLA Ops:
  6.5 299.5 %copy-start = (bf16[384,3072]{1,0:T(8,128)(2,1)S(1)}, bf16[384,3072]{1,0:T(8,128)(2,1)}, u32[]{:S(2)}) copy-start(bf16[384,3072]{1,0:T(8,128)(2,1)} %param.18) | copy-start | bytes 7077892
  6.5 8.4 %copy-start.1 = (bf16[256,384]{1,0:T(8,128)(2,1)S(1)}, bf16[256,384]{1,0:T(8,128)(2,1)}, u32[]{:S(2)}) copy-start(bf16[256,384]{1,0:T(8,128)(2,1)} %param.17) | copy-start | bytes 589828
  6.5 354.4 %reduce-scatter.2.cloned.1.call-start = ((), (), s32[]{:S(2)}) async-start(), calls=%async_computation.1 | async-start | bytes 1966080 | tf_op jit(solution)/shard_map/reduce_scatter | solution.py:114
  19.2 9.3 %collective-permute-start = (bf16[2,256,384]{2,1,0:T(8,128)(2,1)S(1)}, bf16[2,256,384]{2,1,0:T(8,128)(2,1)}, u32[]{:S(2)}, u32[]{:S(2)}) collective-permute-start(bf16[2,256,384]{2,1,0:T(8,128)(2,1)S(1)} %param), channel_id=1, source_target_pairs={{0,4},{4,0},{8,12},{12,8},{16,20},{20,16},{24,28},{28,24},{32,36},... | collective-permute-start | bytes 1179656 | tf_op jit(solution)/shard_map/while/body/eval_jaxpr/cond/branch_0_fun/ppermute | solution.py:22
  37.5 15.2 %collective-permute-start.1 = (bf16[2,256,384]{2,1,0:T(8,128)(2,1)S(1)}, bf16[2,256,384]{2,1,0:T(8,128)(2,1)}, u32[]{:S(2)}, u32[]{:S(2)}) collective-permute-start(bf16[2,256,384]{2,1,0:T(8,128)(2,1)S(1)} %param.1), channel_id=1, source_target_pairs={{0,8},{8,0},{4,12},{12,4},{16,24},{24,16},{20,28},{28,20},{32,40},... | collective-permute-start | bytes 1179656 | tf_op jit(solution)/shard_map/while/body/eval_jaxpr/cond/branch_1_fun/ppermute | solution.py:22
  61.7 9.1 %collective-permute-start = (bf16[2,256,384]{2,1,0:T(8,128)(2,1)S(1)}, bf16[2,256,384]{2,1,0:T(8,128)(2,1)}, u32[]{:S(2)}, u32[]{:S(2)}) collective-permute-start(bf16[2,256,384]{2,1,0:T(8,128)(2,1)S(1)} %param), channel_id=1, source_target_pairs={{0,4},{4,0},{8,12},{12,8},{16,20},{20,16},{24,28},{28,24},{32,36},... | collective-permute-start | bytes 1179656 | tf_op jit(solution)/shard_map/while/body/eval_jaxpr/cond/branch_0_fun/ppermute | solution.py:22
  79.9 12.7 %collective-permute-start.2 = (bf16[2,256,384]{2,1,0:T(8,128)(2,1)S(1)}, bf16[2,256,384]{2,1,0:T(8,128)(2,1)}, u32[]{:S(2)}, u32[]{:S(2)}) collective-permute-start(bf16[2,256,384]{2,1,0:T(8,128)(2,1)S(1)} %param.2), channel_id=1, source_target_pairs={{0,16},{16,0},{4,20},{20,4},{8,24},{24,8},{12,28},{28,12},{32,48},... | collective-permute-start | bytes 1179656 | tf_op jit(solution)/shard_map/while/body/eval_jaxpr/cond/branch_2_fun/ppermute | solution.py:22
  101.6 8.6 %collective-permute-start = (bf16[2,256,384]{2,1,0:T(8,128)(2,1)S(1)}, bf16[2,256,384]{2,1,0:T(8,128)(2,1)}, u32[]{:S(2)}, u32[]{:S(2)}) collective-permute-start(bf16[2,256,384]{2,1,0:T(8,128)(2,1)S(1)} %param), channel_id=1, source_target_pairs={{0,4},{4,0},{8,12},{12,8},{16,20},{20,16},{24,28},{28,24},{32,36},... | collective-permute-start | bytes 1179656 | tf_op jit(solution)/shard_map/while/body/eval_jaxpr/cond/branch_0_fun/ppermute | solution.py:22
  119.3 10.1 %collective-permute-start.1 = (bf16[2,256,384]{2,1,0:T(8,128)(2,1)S(1)}, bf16[2,256,384]{2,1,0:T(8,128)(2,1)}, u32[]{:S(2)}, u32[]{:S(2)}) collective-permute-start(bf16[2,256,384]{2,1,0:T(8,128)(2,1)S(1)} %param.1), channel_id=1, source_target_pairs={{0,8},{8,0},{4,12},{12,4},{16,24},{24,16},{20,28},{28,20},{32,40},... | collective-permute-start | bytes 1179656 | tf_op jit(solution)/shard_map/while/body/eval_jaxpr/cond/branch_1_fun/ppermute | solution.py:22
  138.4 8.6 %collective-permute-start = (bf16[2,256,384]{2,1,0:T(8,128)(2,1)S(1)}, bf16[2,256,384]{2,1,0:T(8,128)(2,1)}, u32[]{:S(2)}, u32[]{:S(2)}) collective-permute-start(bf16[2,256,384]{2,1,0:T(8,128)(2,1)S(1)} %param), channel_id=1, source_target_pairs={{0,4},{4,0},{8,12},{12,8},{16,20},{20,16},{24,28},{28,24},{32,36},... | collective-permute-start | bytes 1179656 | tf_op jit(solution)/shard_map/while/body/eval_jaxpr/cond/branch_0_fun/ppermute | solution.py:22
  156.1 8.7 %collective-permute-start.3 = (bf16[2,256,384]{2,1,0:T(8,128)(2,1)S(1)}, bf16[2,256,384]{2,1,0:T(8,128)(2,1)}, u32[]{:S(2)}, u32[]{:S(2)}) collective-permute-start(bf16[2,256,384]{2,1,0:T(8,128)(2,1)S(1)} %param.3), channel_id=1, source_target_pairs={{0,32},{32,0},{4,36},{36,4},{8,40},{40,8},{12,44},{44,12},{16,48},... | collective-permute-start | bytes 1179656 | tf_op jit(solution)/shard_map/while/body/eval_jaxpr/cond/branch_3_fun/ppermute | solution.py:22
  173.9 8.6 %collective-permute-start = (bf16[2,256,384]{2,1,0:T(8,128)(2,1)S(1)}, bf16[2,256,384]{2,1,0:T(8,128)(2,1)}, u32[]{:S(2)}, u32[]{:S(2)}) collective-permute-start(bf16[2,256,384]{2,1,0:T(8,128)(2,1)S(1)} %param), channel_id=1, source_target_pairs={{0,4},{4,0},{8,12},{12,8},{16,20},{20,16},{24,28},{28,24},{32,36},... | collective-permute-start | bytes 1179656 | tf_op jit(solution)/shard_map/while/body/eval_jaxpr/cond/branch_0_fun/ppermute | solution.py:22
  191.5 10.1 %collective-permute-start.1 = (bf16[2,256,384]{2,1,0:T(8,128)(2,1)S(1)}, bf16[2,256,384]{2,1,0:T(8,128)(2,1)}, u32[]{:S(2)}, u32[]{:S(2)}) collective-permute-start(bf16[2,256,384]{2,1,0:T(8,128)(2,1)S(1)} %param.1), channel_id=1, source_target_pairs={{0,8},{8,0},{4,12},{12,4},{16,24},{24,16},{20,28},{28,20},{32,40},... | collective-permute-start | bytes 1179656 | tf_op jit(solution)/shard_map/while/body/eval_jaxpr/cond/branch_1_fun/ppermute | solution.py:22
  210.7 8.6 %collective-permute-start = (bf16[2,256,384]{2,1,0:T(8,128)(2,1)S(1)}, bf16[2,256,384]{2,1,0:T(8,128)(2,1)}, u32[]{:S(2)}, u32[]{:S(2)}) collective-permute-start(bf16[2,256,384]{2,1,0:T(8,128)(2,1)S(1)} %param), channel_id=1, source_target_pairs={{0,4},{4,0},{8,12},{12,8},{16,20},{20,16},{24,28},{28,24},{32,36},... | collective-permute-start | bytes 1179656 | tf_op jit(solution)/shard_map/while/body/eval_jaxpr/cond/branch_0_fun/ppermute | solution.py:22
  228.3 10.1 %collective-permute-start.2 = (bf16[2,256,384]{2,1,0:T(8,128)(2,1)S(1)}, bf16[2,256,384]{2,1,0:T(8,128)(2,1)}, u32[]{:S(2)}, u32[]{:S(2)}) collective-permute-start(bf16[2,256,384]{2,1,0:T(8,128)(2,1)S(1)} %param.2), channel_id=1, source_target_pairs={{0,16},{16,0},{4,20},{20,4},{8,24},{24,8},{12,28},{28,12},{32,48},... | collective-permute-start | bytes 1179656 | tf_op jit(solution)/shard_map/while/body/eval_jaxpr/cond/branch_2_fun/ppermute | solution.py:22
  247.5 8.6 %collective-permute-start = (bf16[2,256,384]{2,1,0:T(8,128)(2,1)S(1)}, bf16[2,256,384]{2,1,0:T(8,128)(2,1)}, u32[]{:S(2)}, u32[]{:S(2)}) collective-permute-start(bf16[2,256,384]{2,1,0:T(8,128)(2,1)S(1)} %param), channel_id=1, source_target_pairs={{0,4},{4,0},{8,12},{12,8},{16,20},{20,16},{24,28},{28,24},{32,36},... | collective-permute-start | bytes 1179656 | tf_op jit(solution)/shard_map/while/body/eval_jaxpr/cond/branch_0_fun/ppermute | solution.py:22
  265.1 11.4 %collective-permute-start.1 = (bf16[2,256,384]{2,1,0:T(8,128)(2,1)S(1)}, bf16[2,256,384]{2,1,0:T(8,128)(2,1)}, u32[]{:S(2)}, u32[]{:S(2)}) collective-permute-start(bf16[2,256,384]{2,1,0:T(8,128)(2,1)S(1)} %param.1), channel_id=1, source_target_pairs={{0,8},{8,0},{4,12},{12,4},{16,24},{24,16},{20,28},{28,20},{32,40},... | collective-permute-start | bytes 1179656 | tf_op jit(solution)/shard_map/while/body/eval_jaxpr/cond/branch_1_fun/ppermute | solution.py:22
  285.6 10.4 %collective-permute-start = (bf16[2,256,384]{2,1,0:T(8,128)(2,1)S(1)}, bf16[2,256,384]{2,1,0:T(8,128)(2,1)}, u32[]{:S(2)}, u32[]{:S(2)}) collective-permute-start(bf16[2,256,384]{2,1,0:T(8,128)(2,1)S(1)} %param), channel_id=1, source_target_pairs={{0,4},{4,0},{8,12},{12,8},{16,20},{20,16},{24,28},{28,24},{32,36},... | collective-permute-start | bytes 1179656 | tf_op jit(solution)/shard_map/while/body/eval_jaxpr/cond/branch_0_fun/ppermute | solution.py:22
  306.1 2.2 copy-start.3
  306.1 54.9 %copy-start.2 = (bf16[64,3072]{1,0:T(8,128)(2,1)S(1)}, bf16[64,3072]{1,0:T(8,128)(2,1)}, u32[]{:S(2)}) copy-start(bf16[64,3072]{1,0:T(8,128)(2,1)} %param.14) | copy-start | bytes 1179652
Sparse Core Ops, SparseCore 0:
  308.4 52.5 reduce-scatter.1
where the time goes:
time: 373 us; the launch traced here: 370 us
  waiting for transfers between devices  138 us (37%)
  starting transfers between devices  61.3 us (16%)
  other arithmetic  60 us (16%)
  matrix products  54.1 us (15%)
  local copies, waits for them, and re-layouts  41.6 us (11%)
  between operations  13.5 us (4%)
    ppermute x15, waiting for transfers between devices, from_partner(): return lax.ppermute(block, axis, route)  88.9 us
    ppermute x15, starting transfers between devices, from_partner(): return lax.ppermute(block, axis, route)  61.3 us
    reduce_scatter x1, waiting for transfers between devices, on_device(): lax.psum_scatter(jnp.dot(attended, proj_weight, preferred_element_type=jn...  49.1 us
    dot_general x16, matrix products, absorb(): jnp.einsum('qhk,khd->qhd', weights.astype(jnp.bfloat16), value_heads, pre...  31.8 us
    dot_general x16, matrix products, absorb(): jnp.einsum('qhd,khd->qhk', query_heads, key_heads, preferred_element_type...  20.1 us
    add x15, other arithmetic, absorb(): running_sum = running_sum * shrink + jnp.sum(weights, axis=2)  19.4 us
    reduce_sum x15, other arithmetic, cycle_step(): anchor_count = jnp.sum(jnp.where(members == anchor, counts, 0))  19.4 us
    slice x30, local copies, waits for them, and re-layouts, absorb(): value_heads = stacked[1].reshape(length, head_count, HEAD_DIM)  18.1 us
  transfers between devices with their start and end apart: 16, of which 16 were waited for; matrix products, arithmetic and copies ran while one was open for 1% of the time, Pallas kernels for 0%

commit v1 on v0

v1 whole, which is shorter than its diff:
```python
import math

import jax
import jax.numpy as jnp
from jax import lax
from jax.experimental import pallas as pl
from jax.experimental.pallas import tpu as pltpu
from jax.sharding import Mesh, PartitionSpec as P

HEAD_DIM = 128
GROUP = 16
LANES = 128
QMODE = "perm"
WMODE = "perm"
SCALE = math.log2(math.e) / math.sqrt(HEAD_DIM)


def place():
    z, h, y = lax.axis_index("z"), lax.axis_index("h"), lax.axis_index("y")
    return lax.axis_index("r"), z * 2 + h, y


def attend_kernel(split_ref, q0, q1, q2, q3, kv_ref, out_ref):
    request, mine, y = place()
    blocks, _, tokens, width = kv_ref.shape
    heads = width // HEAD_DIM
    keys = blocks * tokens
    quarter = tokens // 4
    slot = lax.broadcasted_iota(jnp.int32, (1, tokens), 1)
    bias = jnp.concatenate(
        [jnp.where(slot < split_ref[request, mine * 4 + b], 0.0, -1e30) for b in range(blocks)], axis=1
    )
    lane = lax.broadcasted_iota(jnp.int32, (tokens, LANES), 1)
    for d, q_ref in enumerate((q0, q1, q2, q3)):
        target = jnp.bitwise_xor(mine, d)
        stats = jnp.zeros((tokens, LANES), jnp.float32)
        for h in range(heads):
            cols = slice(h * HEAD_DIM, (h + 1) * HEAD_DIM)
            k = kv_ref[:, 0, :, cols].reshape(keys, HEAD_DIM)
            v = kv_ref[:, 1, :, cols].reshape(keys, HEAD_DIM)
            s = lax.dot_general(q_ref[:, cols], k, (((1,), (1,)), ((), ())), preferred_element_type=jnp.float32)
            s = s + bias
            top = jnp.max(s, axis=1, keepdims=True) * SCALE
            high = top.astype(jnp.bfloat16).astype(jnp.float32)
            low = (top - high + jnp.abs(top) * 2.0**-16).astype(jnp.bfloat16).astype(jnp.float32)
            p = jnp.exp2(s * SCALE - (high + low))
            total = jnp.sum(p, axis=1, keepdims=True)
            o = jnp.dot(p.astype(jnp.bfloat16), v, preferred_element_type=jnp.float32)
            ob = o.astype(jnp.bfloat16)
            for t in range(4):
                out_ref[target, t, :, cols] = ob[t * quarter:(t + 1) * quarter]
            thigh = total.astype(jnp.bfloat16).astype(jnp.float32)
            tlow = total - thigh
            for j, part in enumerate((high, low, thigh, tlow)):
                stats = jnp.where(lane == 4 * h + j, part, stats)
        sb = stats.astype(jnp.bfloat16)
        for t in range(4):
            out_ref[target, t, :, width:] = sb[t * quarter:(t + 1) * quarter]


def finish_kernel(split_ref, text_ref, part_ref, w0, w1, w2, w3, latent_ref, gate_ref, out_ref):
    request, mine, y = place()
    t_mine = lax.axis_index("l") * 2 + lax.axis_index("c")
    place_in = mine * 4 + y
    rows = latent_ref.shape[0]
    width = w0.shape[0]
    heads = width // HEAD_DIM
    acc = None
    for j, w_ref in enumerate((w0, w1, w2, w3)):
        t = jnp.bitwise_xor(t_mine, j)
        pieces = []
        stat = [part_ref[p * 4 + t, :, width:].astype(jnp.float32) for p in range(4)]
        for h in range(heads):
            cols = slice(h * HEAD_DIM, (h + 1) * HEAD_DIM)
            c = [[stat[p][:, 4 * h + i:4 * h + i + 1] for i in range(4)] for p in range(4)]
            tops = [c[p][0] + c[p][1] for p in range(4)]
            top = jnp.maximum(jnp.maximum(tops[0], tops[1]), jnp.maximum(tops[2], tops[3]))
            e = [jnp.exp2(tops[p] - top) for p in range(4)]
            total = sum(e[p] * (c[p][2] + c[p][3]) for p in range(4))
            a = sum(e[p] * part_ref[p * 4 + t, :, cols].astype(jnp.float32) for p in range(4))
            pieces.append((a / total).astype(jnp.bfloat16))
        att = jnp.concatenate(pieces, axis=1)
        d = jnp.dot(att, w_ref[...], preferred_element_type=jnp.float32)
        acc = d if acc is None else acc + d
    offset = jnp.int32(0)
    for g in range(GROUP):
        offset = offset + jnp.where(g < place_in, split_ref[request, g], 0)
    first = text_ref[request] - offset
    last = split_ref[request, place_in]
    slot = t_mine * rows + lax.broadcasted_iota(jnp.int32, (rows, 1), 0)
    image = (slot >= first) & (slot < last)
    base = latent_ref[...].astype(jnp.float32)
    gate = gate_ref[pl.ds(request, 1), :]
    out_ref[...] = jnp.where(image, base + gate * acc, base).astype(jnp.bfloat16)


def on_device(latent, queries, key_vectors, value_vectors, proj_weight, gate_scale, text_length, split_table):
    tokens, width = queries.shape
    smem = pl.BlockSpec(memory_space=pltpu.SMEM)
    vmem = pl.BlockSpec(memory_space=pltpu.VMEM)

    def swap(x, d):
        return lax.ppermute(x, ("z", "h"), [(i, i ^ d) for i in range(4)])

    if QMODE == "perm":
        qs = [queries] + [swap(queries, d) for d in (1, 2, 3)]
    stacked = jnp.stack([key_vectors, value_vectors])
    kv = lax.all_gather(stacked, "y")
    if WMODE == "perm":
        w0 = proj_weight
        route = []
        for h in range(2):
            for l in range(2):
                x = h * 2 + l
                for c in range(2):
                    sx = (x + 1) % 4 if c == 0 else (x + 3) % 4
                    route.append((sx * 2 + c, x * 2 + c))
        hop = [((sx // 4) * 4 + sx % 4, dx) for sx, dx in route]
        w2 = lax.ppermute(proj_weight, ("h", "l", "c"), hop)
        w1 = lax.ppermute(proj_weight, "c", [(0, 1), (1, 0)])
        w3 = lax.ppermute(w2, "c", [(0, 1), (1, 0)])
        ws = [w0, w1, w2, w3]
    parts = pl.pallas_call(
        attend_kernel,
        out_shape=jax.ShapeDtypeStruct((4, 4, tokens // 4, width + LANES), jnp.bfloat16),
        in_specs=[smem] + [vmem] * 5,
        out_specs=vmem,
        compiler_params=pltpu.CompilerParams(vmem_limit_bytes=40 << 20),
        name="attend",
    )(split_table, *qs, kv)
    parts = parts.reshape(16, tokens // 4, width + LANES)
    got = lax.all_to_all(parts, ("z", "h", "l", "c"), 0, 0, tiled=True)
    return pl.pallas_call(
        finish_kernel,
        out_shape=jax.ShapeDtypeStruct(latent.shape, jnp.bfloat16),
        in_specs=[smem, smem] + [vmem] * 7,
        out_specs=vmem,
        compiler_params=pltpu.CompilerParams(vmem_limit_bytes=40 << 20),
        name="finish",
    )(split_table, text_length, got, *ws, latent, gate_scale)


def solution(mesh):
    parts = Mesh(mesh.devices.reshape(-1, 2, 2, 4, 2, 2), ("r", "z", "h", "y", "l", "c"))
    seq, tp = ("r", "z", "h", "y"), ("l", "c")
    return jax.shard_map(
        on_device,
        mesh=parts,
        in_specs=(
            P(seq + tp, None), P(seq, tp), P(seq, tp), P(seq, tp), P(tp, None), P(), P(), P(),
        ),
        out_specs=P(seq + tp, None),
        check_vma=False,
    )
```

time: 373 us -> 102 us (0.27)
  waiting for transfers between devices: 138 us -> 35.8 us
  other arithmetic: 60 us -> 1.81 us
  matrix products: 54.1 us -> 0 us
  starting transfers between devices: 61.3 us -> 27.3 us
  local copies, waits for them, and re-layouts: 41.6 us -> 10.2 us
  Pallas kernels: 0 us -> 12.7 us
    ppermute x15 -> x6, waiting for transfers between devices: 88.9 us -> 31.4 us  [the longest x3 27.2 us: swap(): return lax.ppermute(x, ('z', 'h'), [(i, i ^ d) for i in range(4)])]
    dot_general x33 -> x0, matrix products: 54.1 us -> none  [the longest x16 31.8 us: absorb(): jnp.einsum('qhk,khd->qhd', weights.astype(jnp.bfloat16), value_heads, pre...]
    reduce_scatter x1 -> x0, waiting for transfers between devices: 49.1 us -> none  [on_device(): lax.psum_scatter(jnp.dot(attended, proj_weight, preferred_element_type=jn...]
    ppermute x15 -> x6, starting transfers between devices: 61.3 us -> 18.3 us  [the longest x3 10.1 us: swap(): return lax.ppermute(x, ('z', 'h'), [(i, i ^ d) for i in range(4)])]
    reduce_sum x33 -> x0, other arithmetic: 24.9 us -> none  [the longest x15 19.4 us: cycle_step(): anchor_count = jnp.sum(jnp.where(members == anchor, counts, 0))]
    add x15 -> x0, other arithmetic: 19.4 us -> none  [absorb(): running_sum = running_sum * shrink + jnp.sum(weights, axis=2)]
    slice x30 -> x0, local copies, waits for them, and re-layouts: 18.1 us -> none  [absorb(): value_heads = stacked[1].reshape(length, head_count, HEAD_DIM)]
    while x45 -> x0, local copies, waits for them, and re-layouts: 17.2 us -> none
  transfers between devices with their start and end apart: 16 -> 8, of which waited for: 16 -> 4; matrix products, arithmetic and copies ran while one was open for 1% -> 0% of each run, Pallas kernels for 0% -> 8%
where the time goes in v1:
time: 102 us; the launch traced here: 101 us
  waiting for transfers between devices  35.8 us (35%)
  starting transfers between devices  27.3 us (27%)
  between operations  13.5 us (13%)
  Pallas kernels  12.7 us (12%)
  local copies, waits for them, and re-layouts  10.2 us (10%)
  other arithmetic  1.81 us (2%)
    ppermute x3, waiting for transfers between devices, swap(): return lax.ppermute(x, ('z', 'h'), [(i, i ^ d) for i in range(4)])  27.2 us
    unnamed x24, local copies, waits for them, and re-layouts  10.2 us
    ppermute x3, starting transfers between devices, swap(): return lax.ppermute(x, ('z', 'h'), [(i, i ^ d) for i in range(4)])  10.1 us
    all_to_all x1, starting transfers between devices, on_device(): got = lax.all_to_all(parts, ('z', 'h', 'l', 'c'), 0, 0, tiled=True)  8.97 us
    pallas_call x1, Pallas kernels, on_device(): pl.pallas_call(attend_kernel, out_shape=jax.ShapeDtypeStruct((4, 4, token...  8.16 us
    pallas_call x1, Pallas kernels, on_device(): pl.pallas_call(finish_kernel, out_shape=jax.ShapeDtypeStruct(latent.shape...  4.54 us
    all_to_all x1, waiting for transfers between devices, on_device(): got = lax.all_to_all(parts, ('z', 'h', 'l', 'c'), 0, 0, tiled=True)  4.36 us
    ppermute x1, starting transfers between devices, on_device(): w2 = lax.ppermute(proj_weight, ('h', 'l', 'c'), hop)  3.95 us
  transfers between devices with their start and end apart: 8, of which 4 were waited for; matrix products, arithmetic and copies ran while one was open for 0% of the time, Pallas kernels for 8%

profile of v1, /device:TPU:1, one launch (start us, length us, event | category | flops | bytes accessed | tf_op | source)
XLA Modules:
  0.0 101.3 jit_solution(4001399658890304852)
XLA Ops:
  6.5 0.0 all-gather.3.cloned.1.call-start
  6.5 1.8 %pad_maximum_fusion = bf16[2,256,384]{2,1,0:T(8,128)(2,1)} fusion(bf16[1,256,384]{2,1,0:T(8,128)(2,1)} %bitcast.5, bf16[1,256,384]{2,1,0:T(8,128)(2,1)} %bitcast.6), kind=kLoop, calls=%fused_computation | loop fusion | flops 196608 | bytes 786432 | tf_op jit(solution)/shard_map/stack | solution.py:107
  8.3 0.0 all-gather.3.cloned.1.call-update
  8.4 4.0 %collective-permute-start.4 = (bf16[384,3072]{1,0:T(8,128)(2,1)}, bf16[384,3072]{1,0:T(8,128)(2,1)}, u32[]{:S(2)}, u32[]{:S(2)}) collective-permute-start(bf16[384,3072]{1,0:T(8,128)(2,1)} %w0.1), channel_id=1, source_target_pairs={{2,0},{19,1},{16,2},{1,3},{18,16},{3,17},{0,18},{17,19},{6,4},{23,... | collective-permute-start | bytes 7077896 | tf_op jit(solution)/shard_map/ppermute | solution.py:119
  12.3 3.5 %collective-permute-start.1 = (bf16[256,384]{1,0:T(8,128)(2,1)}, bf16[256,384]{1,0:T(8,128)(2,1)S(1)}, u32[]{:S(2)}, u32[]{:S(2)}) collective-permute-start(bf16[256,384]{1,0:T(8,128)(2,1)} %q0.1), channel_id=1, source_target_pairs={{0,32},{16,48},{32,0},{48,16},{1,33},{17,49},{33,1},{49,17},{2,34}... | collective-permute-start | bytes 589832 | tf_op jit(solution)/shard_map/ppermute | solution.py:103
  15.9 4.4 %collective-permute-start = (bf16[256,384]{1,0:T(8,128)(2,1)}, bf16[256,384]{1,0:T(8,128)(2,1)S(1)}, u32[]{:S(2)}, u32[]{:S(2)}) collective-permute-start(bf16[256,384]{1,0:T(8,128)(2,1)} %q0.1), channel_id=1, source_target_pairs={{0,16},{16,0},{32,48},{48,32},{1,17},{17,1},{33,49},{49,33},{2,18}... | collective-permute-start | bytes 589832 | tf_op jit(solution)/shard_map/ppermute | solution.py:103
  20.3 2.2 %collective-permute-start.2 = (bf16[256,384]{1,0:T(8,128)(2,1)}, bf16[256,384]{1,0:T(8,128)(2,1)S(1)}, u32[]{:S(2)}, u32[]{:S(2)}) collective-permute-start(bf16[256,384]{1,0:T(8,128)(2,1)} %q0.1), channel_id=1, source_target_pairs={{0,48},{16,32},{32,16},{48,0},{1,49},{17,33},{33,17},{49,1},{2,50}... | collective-permute-start | bytes 589832 | tf_op jit(solution)/shard_map/ppermute | solution.py:103
  22.4 0.0 collective-permute-done.1.q2
  22.4 27.2 %collective-permute-done.q1 = bf16[256,384]{1,0:T(8,128)(2,1)S(1)} collective-permute-done((bf16[256,384]{1,0:T(8,128)(2,1)}, bf16[256,384]{1,0:T(8,128)(2,1)S(1)}, u32[]{:S(2)}, u32[]{:S(2)}) %collective-permute-start) | collective-permute-done | bytes 196640 | tf_op jit(solution)/shard_map/ppermute | solution.py:103
  49.6 0.0 collective-permute-done.2.q3
  49.6 1.4 %copy-done.5 = bf16[8,256,384]{2,1,0:T(8,128)(2,1)S(1)} copy-done((bf16[8,256,384]{2,1,0:T(8,128)(2,1)S(1)}, bf16[8,256,384]{2,1,0:T(8,128)(2,1)}, u32[]{:S(2)}) %copy-start.5) | copy-done | bytes 1572888
  51.0 0.9 copy-done.7
  52.0 0.7 copy-done.9
  52.7 8.2 %attend.1 = bf16[4,4,64,512]{3,2,1,0:T(8,128)(2,1)} custom-call(s32[8,16]{1,0:T(8,128)S(1)} %copy-done.9, bf16[256,384]{1,0:T(8,128)(2,1)S(1)} %copy-done.7, bf16[256,384]{1,0:T(8,128)(2,1)S(1)} %collective-permute-done.q1, bf16[256,384]{1,0:T(8,128)(2,1)S(1)} %collective-permute-done.1.q2, bf16[256,384]{1,0:T(8,128)(2,1)S(1)} %collective-permute-done.2.q3, ...), custom_call_target="tpu_custom_call" | custom-call | tf_op jit(solution)/shard_map/attend/pallas_call | solution.py:123
  60.8 9.0 %all-to-all-start = ((bf16[16,64,512]{2,1,0:T(8,128)(2,1)}), bf16[16,64,512]{2,1,0:T(8,128)(2,1)S(1)}, u32[]{:S(2)}, u32[]{:S(2)}) async-start(bf16[16,64,512]{2,1,0:T(8,128)(2,1)} %bitcast.3), calls=%async_computation | async-start | bytes 2097152 | tf_op jit(solution)/shard_map/all_to_all | solution.py:132
  69.8 0.0 copy-done
  69.8 2.0 %collective-permute-start.3 = (bf16[384,3072]{1,0:T(8,128)(2,1)S(1)}, bf16[384,3072]{1,0:T(8,128)(2,1)S(1)}, u32[]{:S(2)}, u32[]{:S(2)}) collective-permute-start(bf16[384,3072]{1,0:T(8,128)(2,1)S(1)} %copy-done), channel_id=1, source_target_pairs={{0,1},{1,0},{2,3},{3,2},{4,5},{5,4},{6,7},{7,6},{8,9},{9,8},{10,11... | collective-permute-start | bytes 7077896 | tf_op jit(solution)/shard_map/ppermute | solution.py:120
  71.8 0.0 collective-permute-done.4.w2
  71.8 2.3 %collective-permute-start.5 = (bf16[384,3072]{1,0:T(8,128)(2,1)}, bf16[384,3072]{1,0:T(8,128)(2,1)S(1)}, u32[]{:S(2)}, u32[]{:S(2)}) collective-permute-start(bf16[384,3072]{1,0:T(8,128)(2,1)} %collective-permute-done.4.w2), channel_id=1, source_target_pairs={{0,1},{1,0},{2,3},{3,2},{4,5},{5,4},{6,7},{7,6},{8,9},{9,8},{10,11... | collective-permute-start | bytes 7077896 | tf_op jit(solution)/shard_map/ppermute | solution.py:121
  74.1 2.1 %collective-permute-done.3.w1 = bf16[384,3072]{1,0:T(8,128)(2,1)S(1)} collective-permute-done((bf16[384,3072]{1,0:T(8,128)(2,1)S(1)}, bf16[384,3072]{1,0:T(8,128)(2,1)S(1)}, u32[]{:S(2)}, u32[]{:S(2)}) %collective-permute-start.3) | collective-permute-done | bytes 2359328 | tf_op jit(solution)/shard_map/ppermute | solution.py:120
  76.2 1.4 %copy-done.1 = bf16[384,3072]{1,0:T(8,128)(2,1)} copy-done((bf16[384,3072]{1,0:T(8,128)(2,1)}, bf16[384,3072]{1,0:T(8,128)(2,1)S(1)}, u32[]{:S(2)}) %copy-start.1) | copy-done | bytes 2359320
  77.7 2.1 %collective-permute-done.5.w3 = bf16[384,3072]{1,0:T(8,128)(2,1)S(1)} collective-permute-done((bf16[384,3072]{1,0:T(8,128)(2,1)}, bf16[384,3072]{1,0:T(8,128)(2,1)S(1)}, u32[]{:S(2)}, u32[]{:S(2)}) %collective-permute-start.5) | collective-permute-done | bytes 2359328 | tf_op jit(solution)/shard_map/ppermute | solution.py:121
  79.8 1.4 %copy-done.3 = bf16[384,3072]{1,0:T(8,128)(2,1)} copy-done((bf16[384,3072]{1,0:T(8,128)(2,1)}, bf16[384,3072]{1,0:T(8,128)(2,1)S(1)}, u32[]{:S(2)}) %copy-start.3) | copy-done | bytes 2359320
  81.3 4.4 %all-to-all-done.part_ref = bf16[16,64,512]{2,1,0:T(8,128)(2,1)S(1)} async-done(((bf16[16,64,512]{2,1,0:T(8,128)(2,1)}), bf16[16,64,512]{2,1,0:T(8,128)(2,1)S(1)}, u32[]{:S(2)}, u32[]{:S(2)}) %all-to-all-start) | async-done | bytes 1048608 | tf_op jit(solution)/shard_map/all_to_all | solution.py:132
  85.6 0.0 copy-done.8
  85.6 0.0 copy-done.10
  85.6 0.0 copy-done.11
  85.6 0.0 copy-start.2
  85.6 1.7 %copy-done.2 = bf16[384,3072]{1,0:T(8,128)(2,1)S(1)} copy-done((bf16[384,3072]{1,0:T(8,128)(2,1)S(1)}, bf16[384,3072]{1,0:T(8,128)(2,1)}, u32[]{:S(2)}) %copy-start.2) | copy-done | bytes 2359320
  87.3 1.7 %copy-done.4 = bf16[384,3072]{1,0:T(8,128)(2,1)S(1)} copy-done((bf16[384,3072]{1,0:T(8,128)(2,1)S(1)}, bf16[384,3072]{1,0:T(8,128)(2,1)}, u32[]{:S(2)}) %copy-start.4) | copy-done | bytes 2359320
  89.0 1.0 copy-done.6
  90.0 4.5 %finish.1 = bf16[64,3072]{1,0:T(8,128)(2,1)} custom-call(s32[8,16]{1,0:T(8,128)S(1)} %copy-done.10, s32[8]{0:T(128)S(1)} %copy-done.11, bf16[16,64,512]{2,1,0:T(8,128)(2,1)S(1)} %all-to-all-done.part_ref, bf16[384,3072]{1,0:T(8,128)(2,1)S(1)} %copy-done, bf16[384,3072]{1,0:T(8,128)(2,1)S(1)} %copy-done.2, bf16[384,3072]{1,0:T(8,128)(2,1)} %collective-permute-done.4.w2, ...), custom_call_target="tpu_custom_call" | custom-call | tf_op jit(solution)/shard_map/finish/pallas_call | solution.py:133
  (12 shorter events, 0.0 us)
Async XLA Ops:
  6.5 43.1 %all-gather.3.cloned.1.call-start = ((), (), s32[]{:S(2)}) async-start(), calls=%async_computation.1 | async-start | bytes 1966080 | tf_op jit(solution)/shard_map/all_gather | solution.py:108
  8.4 63.4 %collective-permute-start.4 = (bf16[384,3072]{1,0:T(8,128)(2,1)}, bf16[384,3072]{1,0:T(8,128)(2,1)}, u32[]{:S(2)}, u32[]{:S(2)}) collective-permute-start(bf16[384,3072]{1,0:T(8,128)(2,1)} %w0.1), channel_id=1, source_target_pairs={{2,0},{19,1},{16,2},{1,3},{18,16},{3,17},{0,18},{17,19},{6,4},{23,... | collective-permute-start | bytes 7077896 | tf_op jit(solution)/shard_map/ppermute | solution.py:119
  12.3 10.1 %collective-permute-start.1 = (bf16[256,384]{1,0:T(8,128)(2,1)}, bf16[256,384]{1,0:T(8,128)(2,1)S(1)}, u32[]{:S(2)}, u32[]{:S(2)}) collective-permute-start(bf16[256,384]{1,0:T(8,128)(2,1)} %q0.1), channel_id=1, source_target_pairs={{0,32},{16,48},{32,0},{48,16},{1,33},{17,49},{33,1},{49,17},{2,34}... | collective-permute-start | bytes 589832 | tf_op jit(solution)/shard_map/ppermute | solution.py:103
  15.9 33.7 %collective-permute-start = (bf16[256,384]{1,0:T(8,128)(2,1)}, bf16[256,384]{1,0:T(8,128)(2,1)S(1)}, u32[]{:S(2)}, u32[]{:S(2)}) collective-permute-start(bf16[256,384]{1,0:T(8,128)(2,1)} %q0.1), channel_id=1, source_target_pairs={{0,16},{16,0},{32,48},{48,32},{1,17},{17,1},{33,49},{49,33},{2,18}... | collective-permute-start | bytes 589832 | tf_op jit(solution)/shard_map/ppermute | solution.py:103
  20.3 29.4 %collective-permute-start.2 = (bf16[256,384]{1,0:T(8,128)(2,1)}, bf16[256,384]{1,0:T(8,128)(2,1)S(1)}, u32[]{:S(2)}, u32[]{:S(2)}) collective-permute-start(bf16[256,384]{1,0:T(8,128)(2,1)} %q0.1), channel_id=1, source_target_pairs={{0,48},{16,32},{32,16},{48,0},{1,49},{17,33},{33,17},{49,1},{2,50}... | collective-permute-start | bytes 589832 | tf_op jit(solution)/shard_map/ppermute | solution.py:103
  49.6 1.4 %copy-start.5 = (bf16[8,256,384]{2,1,0:T(8,128)(2,1)S(1)}, bf16[8,256,384]{2,1,0:T(8,128)(2,1)}, u32[]{:S(2)}) copy-start(bf16[8,256,384]{2,1,0:T(8,128)(2,1)} %all-gather.3.cloned.1.call-done) | copy-start | bytes 4718596
  51.0 0.9 copy-start.7
  52.0 0.7 copy-start.9
  52.7 17.1 %copy-start = (bf16[384,3072]{1,0:T(8,128)(2,1)S(1)}, bf16[384,3072]{1,0:T(8,128)(2,1)}, u32[]{:S(2)}) copy-start(bf16[384,3072]{1,0:T(8,128)(2,1)} %w0.1) | copy-start | bytes 7077892
  52.7 33.0 %copy-start.8 = (f32[8,3072]{1,0:T(8,128)S(1)}, f32[8,3072]{1,0:T(8,128)}, u32[]{:S(2)}) copy-start(f32[8,3072]{1,0:T(8,128)} %gate_ref.1) | copy-start | bytes 294916
  52.7 33.0 %copy-start.10 = (s32[8,16]{1,0:T(8,128)S(1)}, s32[8,16]{1,0:T(8,128)}, u32[]{:S(2)}) copy-start(s32[8,16]{1,0:T(8,128)} %split_ref.3) | copy-start | bytes 1540
  52.7 33.0 %copy-start.11 = (s32[8]{0:T(128)S(1)}, s32[8]{0:T(128)}, u32[]{:S(2)}) copy-start(s32[8]{0:T(128)} %text_ref.1) | copy-start | bytes 100
  60.8 24.8 %all-to-all-start = ((bf16[16,64,512]{2,1,0:T(8,128)(2,1)}), bf16[16,64,512]{2,1,0:T(8,128)(2,1)S(1)}, u32[]{:S(2)}, u32[]{:S(2)}) async-start(bf16[16,64,512]{2,1,0:T(8,128)(2,1)} %bitcast.3), calls=%async_computation | async-start | bytes 2097152 | tf_op jit(solution)/shard_map/all_to_all | solution.py:132
  69.8 6.4 %collective-permute-start.3 = (bf16[384,3072]{1,0:T(8,128)(2,1)S(1)}, bf16[384,3072]{1,0:T(8,128)(2,1)S(1)}, u32[]{:S(2)}, u32[]{:S(2)}) collective-permute-start(bf16[384,3072]{1,0:T(8,128)(2,1)S(1)} %copy-done), channel_id=1, source_target_pairs={{0,1},{1,0},{2,3},{3,2},{4,5},{5,4},{6,7},{7,6},{8,9},{9,8},{10,11... | collective-permute-start | bytes 7077896 | tf_op jit(solution)/shard_map/ppermute | solution.py:120
  71.8 8.0 %collective-permute-start.5 = (bf16[384,3072]{1,0:T(8,128)(2,1)}, bf16[384,3072]{1,0:T(8,128)(2,1)S(1)}, u32[]{:S(2)}, u32[]{:S(2)}) collective-permute-start(bf16[384,3072]{1,0:T(8,128)(2,1)} %collective-permute-done.4.w2), channel_id=1, source_target_pairs={{0,1},{1,0},{2,3},{3,2},{4,5},{5,4},{6,7},{7,6},{8,9},{9,8},{10,11... | collective-permute-start | bytes 7077896 | tf_op jit(solution)/shard_map/ppermute | solution.py:121
  76.2 1.4 %copy-start.1 = (bf16[384,3072]{1,0:T(8,128)(2,1)}, bf16[384,3072]{1,0:T(8,128)(2,1)S(1)}, u32[]{:S(2)}) copy-start(bf16[384,3072]{1,0:T(8,128)(2,1)S(1)} %collective-permute-done.3.w1) | copy-start | bytes 7077892
  79.8 1.4 %copy-start.3 = (bf16[384,3072]{1,0:T(8,128)(2,1)}, bf16[384,3072]{1,0:T(8,128)(2,1)S(1)}, u32[]{:S(2)}) copy-start(bf16[384,3072]{1,0:T(8,128)(2,1)S(1)} %collective-permute-done.5.w3) | copy-start | bytes 7077892
  85.6 1.7 %copy-start.2 = (bf16[384,3072]{1,0:T(8,128)(2,1)S(1)}, bf16[384,3072]{1,0:T(8,128)(2,1)}, u32[]{:S(2)}) copy-start(bf16[384,3072]{1,0:T(8,128)(2,1)} %copy-done.1) | copy-start | bytes 7077892
  87.3 1.7 %copy-start.4 = (bf16[384,3072]{1,0:T(8,128)(2,1)S(1)}, bf16[384,3072]{1,0:T(8,128)(2,1)}, u32[]{:S(2)}) copy-start(bf16[384,3072]{1,0:T(8,128)(2,1)} %copy-done.3) | copy-start | bytes 7077892
  89.0 1.0 copy-start.6
Sparse Core Ops, SparseCore 0:
  9.5 39.5 all-gather.2

commit v2 on v1

v2 whole, which is shorter than its diff:
```python
import functools
import math

import jax
import jax.numpy as jnp
from jax import lax
from jax.experimental import pallas as pl
from jax.experimental.pallas import tpu as pltpu
from jax.sharding import Mesh, PartitionSpec as P

HEAD_DIM = 128
GROUP = 16
LANES = 128
SCALE = math.log2(math.e) / math.sqrt(HEAD_DIM)
SMEM = pl.BlockSpec(memory_space=pltpu.SMEM)
VMEM = pl.BlockSpec(memory_space=pltpu.VMEM)
PARAMS = pltpu.CompilerParams(vmem_limit_bytes=40 << 20)


def attend_kernel(split_ref, q0, q1, q2, q3, kv_ref, out_ref):
    request = lax.axis_index("r")
    mine_z, mine_h, side = lax.axis_index("z"), lax.axis_index("h"), lax.axis_index("l")
    mine = mine_z * 2 + mine_h
    blocks, _, tokens, width = kv_ref.shape
    heads = width // HEAD_DIM
    keys = blocks * tokens
    part = tokens // 4
    slot = lax.broadcasted_iota(jnp.int32, (1, tokens), 1)
    bias = jnp.concatenate(
        [jnp.where(slot < split_ref[request, mine * 4 + b], 0.0, -1e30) for b in range(blocks)], axis=1
    )
    lane = lax.broadcasted_iota(jnp.int32, (tokens, LANES), 1)
    for d, q_ref in enumerate((q0, q1, q2, q3)):
        z, h_block = jnp.bitwise_xor(mine_z, d // 2), jnp.bitwise_xor(mine_h, d % 2)
        places = []
        for quarter in range(4):
            core, own = quarter % 2, side == quarter // 2
            h_to = jnp.where(own | (side == core), h_block, 1 - h_block)
            start = pl.multiple_of(jnp.where(own, 0, part), part)
            places.append((z * 4 + h_to * 2 + core, pl.ds(start, part), slice(quarter * part, (quarter + 1) * part)))
        stats = jnp.zeros((tokens, LANES), jnp.float32)
        for h in range(heads):
            cols = slice(h * HEAD_DIM, (h + 1) * HEAD_DIM)
            k = kv_ref[:, 0, :, cols].reshape(keys, HEAD_DIM)
            v = kv_ref[:, 1, :, cols].reshape(keys, HEAD_DIM)
            s = lax.dot_general(q_ref[:, cols], k, (((1,), (1,)), ((), ())), preferred_element_type=jnp.float32)
            s = s + bias
            top = jnp.max(s, axis=1, keepdims=True) * SCALE
            high = top.astype(jnp.bfloat16).astype(jnp.float32)
            low = (top - high + jnp.abs(top) * 2.0**-16).astype(jnp.bfloat16).astype(jnp.float32)
            p = jnp.exp2(s * SCALE - (high + low))
            total = jnp.sum(p, axis=1, keepdims=True)
            o = jnp.dot(p.astype(jnp.bfloat16), v, preferred_element_type=jnp.float32).astype(jnp.bfloat16)
            for to, row, source in places:
                out_ref[to, row, cols] = o[source]
            total_high = total.astype(jnp.bfloat16).astype(jnp.float32)
            for j, piece in enumerate((high, low, total_high, total - total_high)):
                stats = jnp.where(lane == 4 * h + j, piece, stats)
        stats = stats.astype(jnp.bfloat16)
        for to, row, source in places:
            out_ref[to, row, width:] = stats[source]


def project_kernel(part_ref, w_mine, w_other, own_ref, give_ref):
    rows = own_ref.shape[0]
    width = w_mine.shape[0]
    heads = width // HEAD_DIM
    core = lax.axis_index("c")
    both = None
    for w_ref, head_side in ((w_mine, core), (w_other, 1 - core)):
        stat = [part_ref[2 * p + head_side, :, width:].astype(jnp.float32) for p in range(4)]
        pieces = []
        for h in range(heads):
            cols = slice(h * HEAD_DIM, (h + 1) * HEAD_DIM)
            c = [[s[:, 4 * h + i:4 * h + i + 1] for i in range(4)] for s in stat]
            tops = [x[0] + x[1] for x in c]
            top = functools.reduce(jnp.maximum, tops)
            e = [jnp.exp2(x - top) for x in tops]
            total = sum(a * (x[2] + x[3]) for a, x in zip(e, c))
            mixed = sum(a * part_ref[2 * p + head_side, :, cols].astype(jnp.float32) for p, a in enumerate(e))
            pieces.append((mixed / total).astype(jnp.bfloat16))
        product = jnp.dot(jnp.concatenate(pieces, axis=1), w_ref[...], preferred_element_type=jnp.float32)
        both = product if both is None else both + product
    own_ref[...] = both[:rows]
    give_ref[...] = both[rows:].astype(jnp.bfloat16)


def finish_kernel(split_ref, text_ref, own_ref, got_ref, latent_ref, gate_ref, out_ref):
    request = lax.axis_index("r")
    index = (lax.axis_index("z") * 2 + lax.axis_index("h")) * 4 + lax.axis_index("y")
    rows = latent_ref.shape[0]
    offset = jnp.int32(0)
    for g in range(GROUP):
        offset = offset + jnp.where(g < index, split_ref[request, g], 0)
    first = text_ref[request] - offset
    last = split_ref[request, index]
    slot = (lax.axis_index("l") * 2 + lax.axis_index("c")) * rows
    slot = slot + lax.broadcasted_iota(jnp.int32, (rows, 1), 0)
    image = (slot >= first) & (slot < last)
    base = latent_ref[...].astype(jnp.float32)
    projected = own_ref[...] + got_ref[...].astype(jnp.float32)
    gate = gate_ref[pl.ds(request, 1), :]
    out_ref[...] = jnp.where(image, base + gate * projected, base).astype(jnp.bfloat16)


def call(kernel, name, outs, specs, args):
    return pl.pallas_call(
        kernel,
        out_shape=[jax.ShapeDtypeStruct(*o) for o in outs],
        in_specs=specs,
        out_specs=[VMEM] * len(outs),
        compiler_params=PARAMS,
        name=name,
    )(*args)


def on_device(latent, queries, key_vectors, value_vectors, proj_weight, gate_scale, text_length, split_table):
    tokens, width = queries.shape
    rows, depth = latent.shape
    bf16 = jnp.bfloat16

    def swap(x, d):
        return lax.ppermute(x, ("z", "h"), [(i, i ^ d) for i in range(4)])

    stacked = jnp.broadcast_to(jnp.stack([key_vectors, value_vectors])[None], (4, 2) + key_vectors.shape)
    kv = lax.all_to_all(stacked, "y", 0, 0, tiled=True)
    q = [queries] + [swap(queries, d) for d in (1, 2, 3)]
    late_weight, _ = lax.optimization_barrier((proj_weight, q[2]))
    w_other = lax.ppermute(late_weight, "c", [(0, 1), (1, 0)])
    parts = call(
        attend_kernel, "attend", [((8, 2 * rows, width + LANES), bf16)], [SMEM] + [VMEM] * 5, (split_table, *q, kv)
    )[0]
    parts = lax.all_to_all(parts, ("z", "h", "c"), 0, 0, tiled=True)
    own, give = call(
        project_kernel, "project", [((rows, depth), jnp.float32), ((rows, depth), bf16)], [VMEM] * 3,
        (parts, proj_weight, w_other),
    )
    along = [(x * 2 + c, (x + (1 if c == 0 else 3)) % 4 * 2 + c) for x in range(4) for c in range(2)]
    got = lax.ppermute(give, ("h", "l", "c"), along)
    return call(
        finish_kernel, "finish", [((rows, depth), bf16)], [SMEM] * 2 + [VMEM] * 4,
        (split_table, text_length, own, got, latent, gate_scale),
    )[0]


def solution(mesh):
    parts = Mesh(mesh.devices.reshape(-1, 2, 2, 4, 2, 2), ("r", "z", "h", "y", "l", "c"))
    seq, tp = ("r", "z", "h", "y"), ("l", "c")
    return jax.shard_map(
        on_device,
        mesh=parts,
        in_specs=(
            P(seq + tp, None), P(seq, tp), P(seq, tp), P(seq, tp), P(tp, None), P(), P(), P(),
        ),
        out_specs=P(seq + tp, None),
        check_vma=False,
    )
```

time: 102 us -> 73.5 us (0.72)
  the two profiles are of different devices: /device:TPU:1 before, /device:TPU:64 now
where the time goes in v2:
time: 73.5 us; the launch traced here: 73.1 us
  waiting for transfers between devices  31.9 us (43%)
  starting transfers between devices  25.9 us (35%)
  Pallas kernels  11.2 us (15%)
  local copies, waits for them, and re-layouts  2.99 us (4%)
  other arithmetic  1.07 us (1%)
    pallas_call x3, Pallas kernels, call(): pl.pallas_call(kernel, out_shape=[jax.ShapeDtypeStruct(*o) for o in outs]...  11.2 us
    ppermute x3, starting transfers between devices, swap(): return lax.ppermute(x, ('z', 'h'), [(i, i ^ d) for i in range(4)])  10.7 us
    all_to_all x1, waiting for transfers between devices, on_device(): parts = lax.all_to_all(parts, ('z', 'h', 'c'), 0, 0, tiled=True)  9.2 us
    ppermute x1, waiting for transfers between devices, on_device(): got = lax.ppermute(give, ('h', 'l', 'c'), along)  8.37 us
    ppermute x3, waiting for transfers between devices, swap(): return lax.ppermute(x, ('z', 'h'), [(i, i ^ d) for i in range(4)])  8.12 us
    all_to_all x1, starting transfers between devices, on_device(): parts = lax.all_to_all(parts, ('z', 'h', 'c'), 0, 0, tiled=True)  5.79 us
    all_to_all x1, starting transfers between devices, on_device(): kv = lax.all_to_all(stacked, 'y', 0, 0, tiled=True)  4.46 us
    ppermute x1, waiting for transfers between devices, on_device(): w_other = lax.ppermute(late_weight, 'c', [(0, 1), (1, 0)])  4.35 us
  transfers between devices with their start and end apart: 7, of which 6 were waited for; matrix products, arithmetic and copies ran while one was open for 0% of the time, Pallas kernels for 0%

profile of v2, /device:TPU:64, one launch (start us, length us, event | category | flops | bytes accessed | tf_op | source)
XLA Modules:
  0.0 73.1 jit_solution(14736042530684379351)
XLA Ops:
  0.0 1.1 %pad_maximum_fusion = bf16[2,256,384]{2,1,0:T(8,128)(2,1)S(1)} fusion(bf16[1,256,384]{2,1,0:T(8,128)(2,1)} %bitcast.2, bf16[1,256,384]{2,1,0:T(8,128)(2,1)} %bitcast.3), kind=kLoop, calls=%fused_computation | loop fusion | flops 196608 | bytes 786432 | tf_op jit(solution)/shard_map/stack | solution.py:125
  1.1 0.0 copy-start.2
  1.1 0.0 copy-start.4
  1.1 1.3 %broadcast_in_dim.2 = bf16[4,2,256,384]{3,2,1,0:T(8,128)(2,1)} broadcast(bf16[2,256,384]{2,1,0:T(8,128)(2,1)S(1)} %pad_maximum_fusion), dimensions={1,2,3} | broadcast | bytes 1966080 | tf_op jit(solution)/shard_map/broadcast_in_dim | solution.py:125
  2.4 4.5 %all-to-all-start = ((bf16[4,2,256,384]{3,2,1,0:T(8,128)(2,1)}), bf16[4,2,256,384]{3,2,1,0:T(8,128)(2,1)S(1)}, u32[]{:S(2)}, u32[]{:S(2)}) async-start(bf16[4,2,256,384]{3,2,1,0:T(8,128)(2,1)} %broadcast_in_dim.2), calls=%async_computation | async-start | bytes 3145728 | tf_op jit(solution)/shard_map/all_to_all | solution.py:126
  6.9 0.0 copy-done.2
  6.9 3.8 %collective-permute-start.1 = (bf16[256,384]{1,0:T(8,128)(2,1)S(1)}, bf16[256,384]{1,0:T(8,128)(2,1)S(1)}, u32[]{:S(2)}, u32[]{:S(2)}) collective-permute-start(bf16[256,384]{1,0:T(8,128)(2,1)S(1)} %copy-done.2), channel_id=1, source_target_pairs={{0,32},{16,48},{32,0},{48,16},{1,33},{17,49},{33,1},{49,17},{2,34}... | collective-permute-start | bytes 589832 | tf_op jit(solution)/shard_map/ppermute | solution.py:123
  10.7 4.9 %collective-permute-start = (bf16[256,384]{1,0:T(8,128)(2,1)S(1)}, bf16[256,384]{1,0:T(8,128)(2,1)S(1)}, u32[]{:S(2)}, u32[]{:S(2)}) collective-permute-start(bf16[256,384]{1,0:T(8,128)(2,1)S(1)} %copy-done.2), channel_id=1, source_target_pairs={{0,16},{16,0},{32,48},{48,32},{1,17},{17,1},{33,49},{49,33},{2,18}... | collective-permute-start | bytes 589832 | tf_op jit(solution)/shard_map/ppermute | solution.py:123
  15.6 2.0 %collective-permute-start.2 = (bf16[256,384]{1,0:T(8,128)(2,1)S(1)}, bf16[256,384]{1,0:T(8,128)(2,1)S(1)}, u32[]{:S(2)}, u32[]{:S(2)}) collective-permute-start(bf16[256,384]{1,0:T(8,128)(2,1)S(1)} %copy-done.2), channel_id=1, source_target_pairs={{0,48},{16,32},{32,16},{48,0},{1,49},{17,33},{33,17},{49,1},{2,50}... | collective-permute-start | bytes 589832 | tf_op jit(solution)/shard_map/ppermute | solution.py:123
  17.6 0.0 collective-permute-done.1.q2
  17.6 5.8 %collective-permute-done.q1 = bf16[256,384]{1,0:T(8,128)(2,1)S(1)} collective-permute-done((bf16[256,384]{1,0:T(8,128)(2,1)S(1)}, bf16[256,384]{1,0:T(8,128)(2,1)S(1)}, u32[]{:S(2)}, u32[]{:S(2)}) %collective-permute-start) | collective-permute-done | bytes 196640 | tf_op jit(solution)/shard_map/ppermute | solution.py:123
  23.4 2.3 %collective-permute-done.2.q3 = bf16[256,384]{1,0:T(8,128)(2,1)S(1)} collective-permute-done((bf16[256,384]{1,0:T(8,128)(2,1)S(1)}, bf16[256,384]{1,0:T(8,128)(2,1)S(1)}, u32[]{:S(2)}, u32[]{:S(2)}) %collective-permute-start.2) | collective-permute-done | bytes 196640 | tf_op jit(solution)/shard_map/ppermute | solution.py:123
  25.7 1.8 %all-to-all-done.kv_ref = bf16[4,2,256,384]{3,2,1,0:T(8,128)(2,1)S(1)} async-done(((bf16[4,2,256,384]{3,2,1,0:T(8,128)(2,1)}), bf16[4,2,256,384]{3,2,1,0:T(8,128)(2,1)S(1)}, u32[]{:S(2)}, u32[]{:S(2)}) %all-to-all-start) | async-done | bytes 1572896 | tf_op jit(solution)/shard_map/all_to_all | solution.py:126
  27.6 0.0 copy-done.4
  27.6 8.0 %attend.1 = bf16[8,128,512]{2,1,0:T(8,128)(2,1)} custom-call(s32[8,16]{1,0:T(8,128)S(1)} %copy-done.4, bf16[256,384]{1,0:T(8,128)(2,1)S(1)} %copy-done.2, bf16[256,384]{1,0:T(8,128)(2,1)S(1)} %collective-permute-done.q1, bf16[256,384]{1,0:T(8,128)(2,1)S(1)} %collective-permute-done.1.q2, bf16[256,384]{1,0:T(8,128)(2,1)S(1)} %collective-permute-done.2.q3, ...), custom_call_target="tpu_custom_call" | custom-call | tf_op jit(solution)/shard_map/attend/pallas_call | solution.py:107
  35.6 0.0 copy-start.3
  35.6 0.0 copy-start.5
  35.6 5.8 %all-to-all-start.1 = ((bf16[8,128,512]{2,1,0:T(8,128)(2,1)}), bf16[8,128,512]{2,1,0:T(8,128)(2,1)S(1)}, u32[]{:S(2)}, u32[]{:S(2)}) async-start(bf16[8,128,512]{2,1,0:T(8,128)(2,1)} %attend.1), calls=%async_computation.1 | async-start | bytes 2097152 | tf_op jit(solution)/shard_map/all_to_all | solution.py:133
  41.3 2.4 %collective-permute-start.3 = (bf16[384,3072]{1,0:T(8,128)(2,1)}, bf16[384,3072]{1,0:T(8,128)(2,1)S(1)}, u32[]{:S(2)}, u32[]{:S(2)}) collective-permute-start(bf16[384,3072]{1,0:T(8,128)(2,1)} %w_mine.1), channel_id=1, source_target_pairs={{0,1},{1,0},{2,3},{3,2},{4,5},{5,4},{6,7},{7,6},{8,9},{9,8},{10,11... | collective-permute-start | bytes 7077896 | tf_op jit(solution)/shard_map/ppermute | solution.py:129
  43.8 4.3 %collective-permute-done.3.w_other = bf16[384,3072]{1,0:T(8,128)(2,1)S(1)} collective-permute-done((bf16[384,3072]{1,0:T(8,128)(2,1)}, bf16[384,3072]{1,0:T(8,128)(2,1)S(1)}, u32[]{:S(2)}, u32[]{:S(2)}) %collective-permute-start.3) | collective-permute-done | bytes 2359328 | tf_op jit(solution)/shard_map/ppermute | solution.py:129
  48.1 9.2 %all-to-all-done.1.part_ref = bf16[8,128,512]{2,1,0:T(8,128)(2,1)S(1)} async-done(((bf16[8,128,512]{2,1,0:T(8,128)(2,1)}), bf16[8,128,512]{2,1,0:T(8,128)(2,1)S(1)}, u32[]{:S(2)}, u32[]{:S(2)}) %all-to-all-start.1) | async-done | bytes 1048608 | tf_op jit(solution)/shard_map/all_to_all | solution.py:133
  57.3 0.0 copy-start
  57.3 1.7 %copy-done = bf16[384,3072]{1,0:T(8,128)(2,1)S(1)} copy-done((bf16[384,3072]{1,0:T(8,128)(2,1)S(1)}, bf16[384,3072]{1,0:T(8,128)(2,1)}, u32[]{:S(2)}) %copy-start) | copy-done | bytes 2359320
  59.0 0.0 copy-start.1
  59.0 1.6 %project.1 = (f32[64,3072]{1,0:T(8,128)S(1)}, bf16[64,3072]{1,0:T(8,128)(2,1)S(1)}) custom-call(bf16[8,128,512]{2,1,0:T(8,128)(2,1)S(1)} %all-to-all-done.1.part_ref, bf16[384,3072]{1,0:T(8,128)(2,1)S(1)} %copy-done, bf16[384,3072]{1,0:T(8,128)(2,1)S(1)} %collective-permute-done.3.w_other), custom_call_target="tpu_custom_call" | custom-call | tf_op jit(solution)/shard_map/project/pallas_call | solution.py:107
  60.6 2.5 %collective-permute-start.4 = (bf16[64,3072]{1,0:T(8,128)(2,1)S(1)}, bf16[64,3072]{1,0:T(8,128)(2,1)S(1)}, u32[]{:S(2)}, u32[]{:S(2)}) collective-permute-start(bf16[64,3072]{1,0:T(8,128)(2,1)S(1)} %get-tuple-element.10), channel_id=1, source_target_pairs={{0,2},{1,19},{2,16},{3,1},{16,18},{17,3},{18,0},{19,17},{4,6},{5,2... | collective-permute-start | bytes 1179656 | tf_op jit(solution)/shard_map/ppermute | solution.py:139
  63.1 8.4 %collective-permute-done.4.got_ref = bf16[64,3072]{1,0:T(8,128)(2,1)S(1)} collective-permute-done((bf16[64,3072]{1,0:T(8,128)(2,1)S(1)}, bf16[64,3072]{1,0:T(8,128)(2,1)S(1)}, u32[]{:S(2)}, u32[]{:S(2)}) %collective-permute-start.4) | collective-permute-done | bytes 393248 | tf_op jit(solution)/shard_map/ppermute | solution.py:139
  71.5 0.0 copy-done.3
  71.5 0.0 copy-done.5
  71.5 0.0 copy-done.1
  71.5 1.6 %finish.1 = bf16[64,3072]{1,0:T(8,128)(2,1)} custom-call(s32[8,16]{1,0:T(8,128)S(1)} %copy-done.4, s32[8]{0:T(128)S(1)} %copy-done.5, f32[64,3072]{1,0:T(8,128)S(1)} %get-tuple-element.9.own_ref, bf16[64,3072]{1,0:T(8,128)(2,1)S(1)} %collective-permute-done.4.got_ref, bf16[64,3072]{1,0:T(8,128)(2,1)S(1)} %copy-done.1, f32[8,3072]{1,0:T(8,128)S(1)} %copy-done.3), custom_call_target="tpu_custom_call" | custom-call | tf_op jit(solution)/shard_map/finish/pallas_call | solution.py:107
Async XLA Ops:
  1.1 5.8 %copy-start.2 = (bf16[256,384]{1,0:T(8,128)(2,1)S(1)}, bf16[256,384]{1,0:T(8,128)(2,1)}, u32[]{:S(2)}) copy-start(bf16[256,384]{1,0:T(8,128)(2,1)} %q0.1) | copy-start | bytes 589828
  1.1 26.5 %copy-start.4 = (s32[8,16]{1,0:T(8,128)S(1)}, s32[8,16]{1,0:T(8,128)}, u32[]{:S(2)}) copy-start(s32[8,16]{1,0:T(8,128)} %split_ref.3) | copy-start | bytes 1540
  2.4 25.2 %all-to-all-start = ((bf16[4,2,256,384]{3,2,1,0:T(8,128)(2,1)}), bf16[4,2,256,384]{3,2,1,0:T(8,128)(2,1)S(1)}, u32[]{:S(2)}, u32[]{:S(2)}) async-start(bf16[4,2,256,384]{3,2,1,0:T(8,128)(2,1)} %broadcast_in_dim.2), calls=%async_computation | async-start | bytes 3145728 | tf_op jit(solution)/shard_map/all_to_all | solution.py:126
  6.9 10.7 %collective-permute-start.1 = (bf16[256,384]{1,0:T(8,128)(2,1)S(1)}, bf16[256,384]{1,0:T(8,128)(2,1)S(1)}, u32[]{:S(2)}, u32[]{:S(2)}) collective-permute-start(bf16[256,384]{1,0:T(8,128)(2,1)S(1)} %copy-done.2), channel_id=1, source_target_pairs={{0,32},{16,48},{32,0},{48,16},{1,33},{17,49},{33,1},{49,17},{2,34}... | collective-permute-start | bytes 589832 | tf_op jit(solution)/shard_map/ppermute | solution.py:123
  10.7 12.7 %collective-permute-start = (bf16[256,384]{1,0:T(8,128)(2,1)S(1)}, bf16[256,384]{1,0:T(8,128)(2,1)S(1)}, u32[]{:S(2)}, u32[]{:S(2)}) collective-permute-start(bf16[256,384]{1,0:T(8,128)(2,1)S(1)} %copy-done.2), channel_id=1, source_target_pairs={{0,16},{16,0},{32,48},{48,32},{1,17},{17,1},{33,49},{49,33},{2,18}... | collective-permute-start | bytes 589832 | tf_op jit(solution)/shard_map/ppermute | solution.py:123
  15.6 10.1 %collective-permute-start.2 = (bf16[256,384]{1,0:T(8,128)(2,1)S(1)}, bf16[256,384]{1,0:T(8,128)(2,1)S(1)}, u32[]{:S(2)}, u32[]{:S(2)}) collective-permute-start(bf16[256,384]{1,0:T(8,128)(2,1)S(1)} %copy-done.2), channel_id=1, source_target_pairs={{0,48},{16,32},{32,16},{48,0},{1,49},{17,33},{33,17},{49,1},{2,50}... | collective-permute-start | bytes 589832 | tf_op jit(solution)/shard_map/ppermute | solution.py:123
  35.6 35.9 %copy-start.3 = (f32[8,3072]{1,0:T(8,128)S(1)}, f32[8,3072]{1,0:T(8,128)}, u32[]{:S(2)}) copy-start(f32[8,3072]{1,0:T(8,128)} %gate_ref.1) | copy-start | bytes 294916
  35.6 35.9 %copy-start.5 = (s32[8]{0:T(128)S(1)}, s32[8]{0:T(128)}, u32[]{:S(2)}) copy-start(s32[8]{0:T(128)} %text_ref.1) | copy-start | bytes 100
  35.6 21.8 %all-to-all-start.1 = ((bf16[8,128,512]{2,1,0:T(8,128)(2,1)}), bf16[8,128,512]{2,1,0:T(8,128)(2,1)S(1)}, u32[]{:S(2)}, u32[]{:S(2)}) async-start(bf16[8,128,512]{2,1,0:T(8,128)(2,1)} %attend.1), calls=%async_computation.1 | async-start | bytes 2097152 | tf_op jit(solution)/shard_map/all_to_all | solution.py:133
  41.3 6.8 %collective-permute-start.3 = (bf16[384,3072]{1,0:T(8,128)(2,1)}, bf16[384,3072]{1,0:T(8,128)(2,1)S(1)}, u32[]{:S(2)}, u32[]{:S(2)}) collective-permute-start(bf16[384,3072]{1,0:T(8,128)(2,1)} %w_mine.1), channel_id=1, source_target_pairs={{0,1},{1,0},{2,3},{3,2},{4,5},{5,4},{6,7},{7,6},{8,9},{9,8},{10,11... | collective-permute-start | bytes 7077896 | tf_op jit(solution)/shard_map/ppermute | solution.py:129
  57.3 1.7 %copy-start = (bf16[384,3072]{1,0:T(8,128)(2,1)S(1)}, bf16[384,3072]{1,0:T(8,128)(2,1)}, u32[]{:S(2)}) copy-start(bf16[384,3072]{1,0:T(8,128)(2,1)} %w_mine.1) | copy-start | bytes 7077892
  59.0 12.5 %copy-start.1 = (bf16[64,3072]{1,0:T(8,128)(2,1)S(1)}, bf16[64,3072]{1,0:T(8,128)(2,1)}, u32[]{:S(2)}) copy-start(bf16[64,3072]{1,0:T(8,128)(2,1)} %latent_ref.1) | copy-start | bytes 1179652
  60.6 10.9 %collective-permute-start.4 = (bf16[64,3072]{1,0:T(8,128)(2,1)S(1)}, bf16[64,3072]{1,0:T(8,128)(2,1)S(1)}, u32[]{:S(2)}, u32[]{:S(2)}) collective-permute-start(bf16[64,3072]{1,0:T(8,128)(2,1)S(1)} %get-tuple-element.10), channel_id=1, source_target_pairs={{0,2},{1,19},{2,16},{3,1},{16,18},{17,3},{18,0},{19,17},{4,6},{5,2... | collective-permute-start | bytes 1179656 | tf_op jit(solution)/shard_map/ppermute | solution.py:139

commit v3 on v2

v3 whole, which is shorter than its diff:
```python
import functools
import math

import jax
import jax.numpy as jnp
from jax import lax
from jax.experimental import pallas as pl
from jax.experimental.pallas import tpu as pltpu
from jax.sharding import Mesh, PartitionSpec as P

HEAD_DIM = 128
GROUP = 16
LANES = 128
STATS = 8
SCALE = math.log2(math.e) / math.sqrt(HEAD_DIM)
SMEM = pl.BlockSpec(memory_space=pltpu.SMEM)
VMEM = pl.BlockSpec(memory_space=pltpu.VMEM)
HBM = pl.BlockSpec(memory_space=pltpu.HBM)


def attend_kernel(split_ref, q0, q1, q2, q3, kv_ref, out_ref, v_ones):
    request = lax.axis_index("r")
    mine_z, mine_h, side = lax.axis_index("z"), lax.axis_index("h"), lax.axis_index("l")
    mine = mine_z * 2 + mine_h
    blocks, _, tokens, width = kv_ref.shape
    heads = width // HEAD_DIM
    keys = blocks * tokens
    part = tokens // 4
    slot = lax.broadcasted_iota(jnp.int32, (1, tokens), 1)
    bias = jnp.concatenate(
        [jnp.where(slot < split_ref[request, mine * 4 + b], 0.0, -1e30) for b in range(blocks)], axis=1
    )
    lane = lax.broadcasted_iota(jnp.int32, (tokens, LANES), 1)
    for h in range(heads):
        v_ones[h, :, :HEAD_DIM] = kv_ref[:, 1, :, h * HEAD_DIM:(h + 1) * HEAD_DIM].reshape(keys, HEAD_DIM)
        v_ones[h, :, HEAD_DIM:] = jnp.ones((keys, LANES), jnp.bfloat16)
    for d, q_ref in enumerate((q0, q1, q2, q3)):
        z, h_block = jnp.bitwise_xor(mine_z, d // 2), jnp.bitwise_xor(mine_h, d % 2)
        places = []
        for quarter in range(4):
            core, own = quarter % 2, side == quarter // 2
            h_to = jnp.where(own | (side == core), h_block, 1 - h_block)
            start = jnp.where(own, 0, part + STATS)
            places.append((z * 4 + h_to * 2 + core, pl.multiple_of(start, 8), quarter))
        stats = jnp.zeros((tokens, LANES), jnp.float32)
        for h in range(heads):
            cols = slice(h * HEAD_DIM, (h + 1) * HEAD_DIM)
            k = kv_ref[:, 0, :, cols].reshape(keys, HEAD_DIM)
            s = lax.dot_general(q_ref[:, cols], k, (((1,), (1,)), ((), ())), preferred_element_type=jnp.float32)
            s = s + bias
            top = jnp.max(s, axis=1, keepdims=True) * SCALE
            high = top.astype(jnp.bfloat16).astype(jnp.float32)
            low = (top - high + jnp.abs(top) * 2.0**-16).astype(jnp.bfloat16).astype(jnp.float32)
            p = jnp.exp2(s * SCALE - (high + low))
            both = jnp.dot(p.astype(jnp.bfloat16), v_ones[h], preferred_element_type=jnp.float32)
            o, total = both[:, :HEAD_DIM].astype(jnp.bfloat16), both[:, HEAD_DIM:]
            for to, start, quarter in places:
                out_ref[to, pl.ds(start, part), cols] = o[quarter * part:(quarter + 1) * part]
            total_high = total.astype(jnp.bfloat16).astype(jnp.float32)
            for j, piece in enumerate((high, low, total_high, total - total_high)):
                stats = jnp.where(lane == STATS * h + j, piece, stats)
        stats = stats.T.astype(jnp.bfloat16)
        for to, start, quarter in places:
            here = slice(quarter // 2 * LANES, (quarter // 2 + 1) * LANES)
            tile = [stats[STATS * h:STATS * (h + 1), here] for h in range(heads)]
            out_ref[to, pl.ds(start + part, STATS)] = jnp.concatenate(tile, axis=1)


def project_kernel(first, part_ref, w_any, w_other, out_ref, w_mine, sems):
    count = out_ref.shape[0]
    rows = pl.ds(first, count)
    share = w_any.shape[0] // sems.shape[0]
    fetches = []
    for i in range(sems.shape[0]):
        piece = pl.ds(i * share, share)
        fetches.append(pltpu.make_async_copy(w_any.at[piece], w_mine.at[piece], sems.at[i]))
        fetches[i].start()
    width = w_other.shape[0]
    heads = width // HEAD_DIM
    core = lax.axis_index("c")
    attended = []
    for head_side in (1 - core, core):
        stat = [part_ref[2 * p + head_side, pl.ds(first + count, STATS)].astype(jnp.float32) for p in range(4)]
        stat = [s[:, h * HEAD_DIM:(h + 1) * HEAD_DIM] for s in stat for h in range(heads)]
        stat.append(jnp.zeros((LANES - STATS * len(stat), LANES), jnp.float32))
        stat = jnp.concatenate(stat, axis=0).T
        stat = jnp.where(core == 0, stat[:count], stat[LANES - count:])
        pieces = []
        for h in range(heads):
            cols = slice(h * HEAD_DIM, (h + 1) * HEAD_DIM)
            at = [STATS * (heads * p + h) for p in range(4)]
            c = [[stat[:, a + i:a + i + 1] for i in range(4)] for a in at]
            tops = [x[0] + x[1] for x in c]
            top = functools.reduce(jnp.maximum, tops)
            e = [jnp.exp2(x - top) for x in tops]
            total = sum(a * (x[2] + x[3]) for a, x in zip(e, c))
            mixed = sum(a * part_ref[2 * p + head_side, rows, cols].astype(jnp.float32) for p, a in enumerate(e))
            pieces.append((mixed / total).astype(jnp.bfloat16))
        attended.append(jnp.concatenate(pieces, axis=1))
    both = jnp.dot(attended[0], w_other[...], preferred_element_type=jnp.float32)
    for fetch in fetches:
        fetch.wait()
    both = both + jnp.dot(attended[1], w_mine[...], preferred_element_type=jnp.float32)
    out_ref[...] = both.astype(out_ref.dtype)


def finish_kernel(split_ref, text_ref, own_ref, got_ref, latent_ref, gate_ref, out_ref):
    request = lax.axis_index("r")
    index = (lax.axis_index("z") * 2 + lax.axis_index("h")) * 4 + lax.axis_index("y")
    rows = latent_ref.shape[0]
    offset = jnp.int32(0)
    for g in range(GROUP):
        offset = offset + jnp.where(g < index, split_ref[request, g], 0)
    first = text_ref[request] - offset
    last = split_ref[request, index]
    slot = (lax.axis_index("l") * 2 + lax.axis_index("c")) * rows
    slot = slot + lax.broadcasted_iota(jnp.int32, (rows, 1), 0)
    image = (slot >= first) & (slot < last)
    base = latent_ref[...].astype(jnp.float32)
    projected = own_ref[...] + got_ref[...].astype(jnp.float32)
    gate = gate_ref[pl.ds(request, 1), :]
    out_ref[...] = jnp.where(image, base + gate * projected, base).astype(jnp.bfloat16)


def call(kernel, name, outs, specs, args, scratch=(), out_spec=VMEM, room=8):
    return pl.pallas_call(
        kernel,
        out_shape=[jax.ShapeDtypeStruct(*o) for o in outs],
        in_specs=specs,
        out_specs=[out_spec] * len(outs),
        scratch_shapes=scratch,
        compiler_params=pltpu.CompilerParams(vmem_limit_bytes=room << 20),
        name=name,
    )(*args)


def in_hbm(x):
    return pltpu.with_memory_space_constraint(x, pltpu.HBM)


def on_device(latent, queries, key_vectors, value_vectors, proj_weight, gate_scale, text_length, split_table):
    tokens, width = queries.shape
    rows, depth = latent.shape
    bf16 = jnp.bfloat16

    def swap(x, d):
        return lax.ppermute(x, ("z", "h"), [(i, i ^ d) for i in range(4)])

    stacked = jnp.broadcast_to(jnp.stack([key_vectors, value_vectors])[None], (4, 2) + key_vectors.shape)
    kv = lax.all_to_all(stacked, "y", 0, 0, tiled=True)
    q = [queries] + [swap(queries, d) for d in (1, 2, 3)]
    late_weight, _ = lax.optimization_barrier((proj_weight, q[2]))
    w_other = lax.ppermute(late_weight, "c", [(0, 1), (1, 0)])
    parts = call(
        attend_kernel, "attend", [((8, 2 * (rows + STATS), width), bf16)], [SMEM] + [VMEM] * 5, (split_table, *q, kv),
        [pltpu.VMEM((width // HEAD_DIM, 4 * tokens, HEAD_DIM + LANES), bf16)], room=20,
    )[0]
    parts = lax.all_to_all(parts, ("z", "h", "c"), 0, 0, tiled=True)
    weights = (in_hbm(proj_weight), w_other)
    room = [pltpu.VMEM(proj_weight.shape, bf16), pltpu.SemaphoreType.DMA((4,))]
    give = call(
        functools.partial(project_kernel, rows + STATS), "project_given", [((rows, depth), bf16)], [VMEM, HBM, VMEM],
        (parts, *weights), room, room=12,
    )[0]
    own = call(
        functools.partial(project_kernel, 0), "project_own", [((rows, depth), jnp.float32)], [VMEM, HBM, VMEM],
        (parts, *weights), room, room=12,
    )[0]
    along = [(x * 2 + c, (x + (1 if c == 0 else 3)) % 4 * 2 + c) for x in range(4) for c in range(2)]
    got = lax.ppermute(give, ("h", "l", "c"), along)
    return call(
        finish_kernel, "finish", [((rows, depth), bf16)], [SMEM] * 2 + [VMEM] * 4,
        (split_table, text_length, own, got, latent, gate_scale),
    )[0]


def solution(mesh):
    parts = Mesh(mesh.devices.reshape(-1, 2, 2, 4, 2, 2), ("r", "z", "h", "y", "l", "c"))
    seq, tp = ("r", "z", "h", "y"), ("l", "c")
    return jax.shard_map(
        on_device,
        mesh=parts,
        in_specs=(
            P(seq + tp, None), P(seq, tp), P(seq, tp), P(seq, tp), P(tp, None), P(), P(), P(),
        ),
        out_specs=P(seq + tp, None),
        check_vma=False,
    )
```

time: 73.5 us -> 70 us (0.952)
  waiting for transfers between devices: 31.9 us -> 27.3 us
  Pallas kernels: 11.2 us -> 13.9 us
  local copies, waits for them, and re-layouts: 2.99 us -> 1.33 us
    ppermute x1, waiting for transfers between devices: 8.37 us -> 5.54 us  [on_device(): got = lax.ppermute(give, ('h', 'l', 'c'), along)]
    pallas_call x3 -> x4, Pallas kernels: 11.2 us -> 13.9 us  [call(): pl.pallas_call(kernel, out_shape=[jax.ShapeDtypeStruct(*o) for o in outs]...]
    all_to_all x1, waiting for transfers between devices: 9.2 us -> 7.45 us  [on_device(): parts = lax.all_to_all(parts, ('z', 'h', 'c'), 0, 0, tiled=True)]
    unnamed x12 -> x10, local copies, waits for them, and re-layouts: 1.69 us -> 0.03 us
  transfers between devices with their start and end apart: 7 -> 7, of which waited for: 6 -> 6; matrix products, arithmetic and copies ran while one was open for 0% -> 0% of each run, Pallas kernels for 0% -> 4%
where the time goes in v3:
time: 70 us; the launch traced here: 69.6 us
  waiting for transfers between devices  27.3 us (39%)
  starting transfers between devices  25.8 us (37%)
  Pallas kernels  13.9 us (20%)
  local copies, waits for them, and re-layouts  1.33 us (2%)
  other arithmetic  1.07 us (2%)
    pallas_call x4, Pallas kernels, call(): pl.pallas_call(kernel, out_shape=[jax.ShapeDtypeStruct(*o) for o in outs]...  13.9 us
    ppermute x3, starting transfers between devices, swap(): return lax.ppermute(x, ('z', 'h'), [(i, i ^ d) for i in range(4)])  10.7 us
    ppermute x3, waiting for transfers between devices, swap(): return lax.ppermute(x, ('z', 'h'), [(i, i ^ d) for i in range(4)])  8.12 us
    all_to_all x1, waiting for transfers between devices, on_device(): parts = lax.all_to_all(parts, ('z', 'h', 'c'), 0, 0, tiled=True)  7.45 us
    all_to_all x1, starting transfers between devices, on_device(): parts = lax.all_to_all(parts, ('z', 'h', 'c'), 0, 0, tiled=True)  5.65 us
    ppermute x1, waiting for transfers between devices, on_device(): got = lax.ppermute(give, ('h', 'l', 'c'), along)  5.54 us
    all_to_all x1, starting transfers between devices, on_device(): kv = lax.all_to_all(stacked, 'y', 0, 0, tiled=True)  4.46 us
    ppermute x1, waiting for transfers between devices, on_device(): w_other = lax.ppermute(late_weight, 'c', [(0, 1), (1, 0)])  4.35 us
  transfers between devices with their start and end apart: 7, of which 6 were waited for; matrix products, arithmetic and copies ran while one was open for 0% of the time, Pallas kernels for 4%

profile of v3, /device:TPU:64, one launch (start us, length us, event | category | flops | bytes accessed | tf_op | source)
XLA Modules:
  0.0 69.6 jit_solution(17129602384942178966)
XLA Ops:
  0.0 1.1 %pad_maximum_fusion = bf16[2,256,384]{2,1,0:T(8,128)(2,1)S(1)} fusion(bf16[1,256,384]{2,1,0:T(8,128)(2,1)} %bitcast.2, bf16[1,256,384]{2,1,0:T(8,128)(2,1)} %bitcast.3), kind=kLoop, calls=%fused_computation | loop fusion | flops 196608 | bytes 786432 | tf_op jit(solution)/shard_map/stack | solution.py:149
  1.1 0.0 copy-start.1
  1.1 0.0 copy-start.3
  1.1 1.3 %broadcast_in_dim.2 = bf16[4,2,256,384]{3,2,1,0:T(8,128)(2,1)} broadcast(bf16[2,256,384]{2,1,0:T(8,128)(2,1)S(1)} %pad_maximum_fusion), dimensions={1,2,3} | broadcast | bytes 1966080 | tf_op jit(solution)/shard_map/broadcast_in_dim | solution.py:149
  2.4 4.5 %all-to-all-start = ((bf16[4,2,256,384]{3,2,1,0:T(8,128)(2,1)}), bf16[4,2,256,384]{3,2,1,0:T(8,128)(2,1)S(1)}, u32[]{:S(2)}, u32[]{:S(2)}) async-start(bf16[4,2,256,384]{3,2,1,0:T(8,128)(2,1)} %broadcast_in_dim.2), calls=%async_computation | async-start | bytes 3145728 | tf_op jit(solution)/shard_map/all_to_all | solution.py:150
  6.9 0.0 copy-done.1
  6.9 3.8 %collective-permute-start.1 = (bf16[256,384]{1,0:T(8,128)(2,1)S(1)}, bf16[256,384]{1,0:T(8,128)(2,1)S(1)}, u32[]{:S(2)}, u32[]{:S(2)}) collective-permute-start(bf16[256,384]{1,0:T(8,128)(2,1)S(1)} %copy-done.1), channel_id=1, source_target_pairs={{0,32},{16,48},{32,0},{48,16},{1,33},{17,49},{33,1},{49,17},{2,34}... | collective-permute-start | bytes 589832 | tf_op jit(solution)/shard_map/ppermute | solution.py:147
  10.7 4.9 %collective-permute-start = (bf16[256,384]{1,0:T(8,128)(2,1)S(1)}, bf16[256,384]{1,0:T(8,128)(2,1)S(1)}, u32[]{:S(2)}, u32[]{:S(2)}) collective-permute-start(bf16[256,384]{1,0:T(8,128)(2,1)S(1)} %copy-done.1), channel_id=1, source_target_pairs={{0,16},{16,0},{32,48},{48,32},{1,17},{17,1},{33,49},{49,33},{2,18}... | collective-permute-start | bytes 589832 | tf_op jit(solution)/shard_map/ppermute | solution.py:147
  15.6 2.0 %collective-permute-start.2 = (bf16[256,384]{1,0:T(8,128)(2,1)S(1)}, bf16[256,384]{1,0:T(8,128)(2,1)S(1)}, u32[]{:S(2)}, u32[]{:S(2)}) collective-permute-start(bf16[256,384]{1,0:T(8,128)(2,1)S(1)} %copy-done.1), channel_id=1, source_target_pairs={{0,48},{16,32},{32,16},{48,0},{1,49},{17,33},{33,17},{49,1},{2,50}... | collective-permute-start | bytes 589832 | tf_op jit(solution)/shard_map/ppermute | solution.py:147
  17.6 0.0 collective-permute-done.1.q2
  17.6 5.8 %collective-permute-done.q1 = bf16[256,384]{1,0:T(8,128)(2,1)S(1)} collective-permute-done((bf16[256,384]{1,0:T(8,128)(2,1)S(1)}, bf16[256,384]{1,0:T(8,128)(2,1)S(1)}, u32[]{:S(2)}, u32[]{:S(2)}) %collective-permute-start) | collective-permute-done | bytes 196640 | tf_op jit(solution)/shard_map/ppermute | solution.py:147
  23.4 2.3 %collective-permute-done.2.q3 = bf16[256,384]{1,0:T(8,128)(2,1)S(1)} collective-permute-done((bf16[256,384]{1,0:T(8,128)(2,1)S(1)}, bf16[256,384]{1,0:T(8,128)(2,1)S(1)}, u32[]{:S(2)}, u32[]{:S(2)}) %collective-permute-start.2) | collective-permute-done | bytes 196640 | tf_op jit(solution)/shard_map/ppermute | solution.py:147
  25.7 1.8 %all-to-all-done.kv_ref = bf16[4,2,256,384]{3,2,1,0:T(8,128)(2,1)S(1)} async-done(((bf16[4,2,256,384]{3,2,1,0:T(8,128)(2,1)}), bf16[4,2,256,384]{3,2,1,0:T(8,128)(2,1)S(1)}, u32[]{:S(2)}, u32[]{:S(2)}) %all-to-all-start) | async-done | bytes 1572896 | tf_op jit(solution)/shard_map/all_to_all | solution.py:150
  27.6 0.0 copy-done.3
  27.6 6.6 %attend.1 = bf16[8,144,384]{2,1,0:T(8,128)(2,1)} custom-call(s32[8,16]{1,0:T(8,128)S(1)} %copy-done.3, bf16[256,384]{1,0:T(8,128)(2,1)S(1)} %copy-done.1, bf16[256,384]{1,0:T(8,128)(2,1)S(1)} %collective-permute-done.q1, bf16[256,384]{1,0:T(8,128)(2,1)S(1)} %collective-permute-done.1.q2, bf16[256,384]{1,0:T(8,128)(2,1)S(1)} %collective-permute-done.2.q3, ...), custom_call_target="tpu_custom_call" | custom-call | tf_op jit(solution)/shard_map/attend/pallas_call | solution.py:126
  34.2 5.7 %all-to-all-start.1 = ((bf16[8,144,384]{2,1,0:T(8,128)(2,1)}), bf16[8,144,384]{2,1,0:T(8,128)(2,1)S(1)}, u32[]{:S(2)}, u32[]{:S(2)}) async-start(bf16[8,144,384]{2,1,0:T(8,128)(2,1)} %attend.1), calls=%async_computation.1 | async-start | bytes 1769472 | tf_op jit(solution)/shard_map/all_to_all | solution.py:158
  39.9 2.4 %collective-permute-start.3 = (bf16[384,3072]{1,0:T(8,128)(2,1)}, bf16[384,3072]{1,0:T(8,128)(2,1)S(1)}, u32[]{:S(2)}, u32[]{:S(2)}) collective-permute-start(bf16[384,3072]{1,0:T(8,128)(2,1)} %w_any.3), channel_id=1, source_target_pairs={{0,1},{1,0},{2,3},{3,2},{4,5},{5,4},{6,7},{7,6},{8,9},{9,8},{10,11... | collective-permute-start | bytes 7077896 | tf_op jit(solution)/shard_map/ppermute | solution.py:153
  42.3 4.3 %collective-permute-done.3.w_other = bf16[384,3072]{1,0:T(8,128)(2,1)S(1)} collective-permute-done((bf16[384,3072]{1,0:T(8,128)(2,1)}, bf16[384,3072]{1,0:T(8,128)(2,1)S(1)}, u32[]{:S(2)}, u32[]{:S(2)}) %collective-permute-start.3) | collective-permute-done | bytes 2359328 | tf_op jit(solution)/shard_map/ppermute | solution.py:153
  46.6 7.4 %all-to-all-done.1.part_ref = bf16[8,144,384]{2,1,0:T(8,128)(2,1)S(1)} async-done(((bf16[8,144,384]{2,1,0:T(8,128)(2,1)}), bf16[8,144,384]{2,1,0:T(8,128)(2,1)S(1)}, u32[]{:S(2)}, u32[]{:S(2)}) %all-to-all-start.1) | async-done | bytes 884768 | tf_op jit(solution)/shard_map/all_to_all | solution.py:158
  54.1 2.8 %project_given.1 = bf16[64,3072]{1,0:T(8,128)(2,1)S(1)} custom-call(bf16[8,144,384]{2,1,0:T(8,128)(2,1)S(1)} %all-to-all-done.1.part_ref, bf16[384,3072]{1,0:T(8,128)(2,1)} %w_any.3, bf16[384,3072]{1,0:T(8,128)(2,1)S(1)} %collective-permute-done.3.w_other), custom_call_target="tpu_custom_call" | custom-call | tf_op jit(solution)/shard_map/project_given/pallas_call | solution.py:126
  56.9 0.0 copy-start
  56.9 0.0 copy-start.2
  56.9 0.0 copy-start.4
  56.9 2.6 %collective-permute-start.4 = (bf16[64,3072]{1,0:T(8,128)(2,1)S(1)}, bf16[64,3072]{1,0:T(8,128)(2,1)S(1)}, u32[]{:S(2)}, u32[]{:S(2)}) collective-permute-start(bf16[64,3072]{1,0:T(8,128)(2,1)S(1)} %project_given.1), channel_id=1, source_target_pairs={{0,2},{1,19},{2,16},{3,1},{16,18},{17,3},{18,0},{19,17},{4,6},{5,2... | collective-permute-start | bytes 1179656 | tf_op jit(solution)/shard_map/ppermute | solution.py:170
  59.6 2.8 %project_own.1.own_ref = f32[64,3072]{1,0:T(8,128)S(1)} custom-call(bf16[8,144,384]{2,1,0:T(8,128)(2,1)S(1)} %all-to-all-done.1.part_ref, bf16[384,3072]{1,0:T(8,128)(2,1)} %w_any.3, bf16[384,3072]{1,0:T(8,128)(2,1)S(1)} %collective-permute-done.3.w_other), custom_call_target="tpu_custom_call" | custom-call | tf_op jit(solution)/shard_map/project_own/pallas_call | solution.py:126
  62.4 5.5 %collective-permute-done.4.got_ref = bf16[64,3072]{1,0:T(8,128)(2,1)S(1)} collective-permute-done((bf16[64,3072]{1,0:T(8,128)(2,1)S(1)}, bf16[64,3072]{1,0:T(8,128)(2,1)S(1)}, u32[]{:S(2)}, u32[]{:S(2)}) %collective-permute-start.4) | collective-permute-done | bytes 393248 | tf_op jit(solution)/shard_map/ppermute | solution.py:170
  68.0 0.0 copy-done
  68.0 0.0 copy-done.2
  68.0 0.0 copy-done.4
  68.0 1.6 %finish.1 = bf16[64,3072]{1,0:T(8,128)(2,1)} custom-call(s32[8,16]{1,0:T(8,128)S(1)} %copy-done.3, s32[8]{0:T(128)S(1)} %copy-done.4, f32[64,3072]{1,0:T(8,128)S(1)} %project_own.1.own_ref, bf16[64,3072]{1,0:T(8,128)(2,1)S(1)} %collective-permute-done.4.got_ref, bf16[64,3072]{1,0:T(8,128)(2,1)S(1)} %copy-done, f32[8,3072]{1,0:T(8,128)S(1)} %copy-done.2), custom_call_target="tpu_custom_call" | custom-call | tf_op jit(solution)/shard_map/finish/pallas_call | solution.py:126
Async XLA Ops:
  1.1 5.8 %copy-start.1 = (bf16[256,384]{1,0:T(8,128)(2,1)S(1)}, bf16[256,384]{1,0:T(8,128)(2,1)}, u32[]{:S(2)}) copy-start(bf16[256,384]{1,0:T(8,128)(2,1)} %q0.1) | copy-start | bytes 589828
  1.1 26.5 %copy-start.3 = (s32[8,16]{1,0:T(8,128)S(1)}, s32[8,16]{1,0:T(8,128)}, u32[]{:S(2)}) copy-start(s32[8,16]{1,0:T(8,128)} %split_ref.3) | copy-start | bytes 1540
  2.4 25.2 %all-to-all-start = ((bf16[4,2,256,384]{3,2,1,0:T(8,128)(2,1)}), bf16[4,2,256,384]{3,2,1,0:T(8,128)(2,1)S(1)}, u32[]{:S(2)}, u32[]{:S(2)}) async-start(bf16[4,2,256,384]{3,2,1,0:T(8,128)(2,1)} %broadcast_in_dim.2), calls=%async_computation | async-start | bytes 3145728 | tf_op jit(solution)/shard_map/all_to_all | solution.py:150
  6.9 10.7 %collective-permute-start.1 = (bf16[256,384]{1,0:T(8,128)(2,1)S(1)}, bf16[256,384]{1,0:T(8,128)(2,1)S(1)}, u32[]{:S(2)}, u32[]{:S(2)}) collective-permute-start(bf16[256,384]{1,0:T(8,128)(2,1)S(1)} %copy-done.1), channel_id=1, source_target_pairs={{0,32},{16,48},{32,0},{48,16},{1,33},{17,49},{33,1},{49,17},{2,34}... | collective-permute-start | bytes 589832 | tf_op jit(solution)/shard_map/ppermute | solution.py:147
  10.7 12.7 %collective-permute-start = (bf16[256,384]{1,0:T(8,128)(2,1)S(1)}, bf16[256,384]{1,0:T(8,128)(2,1)S(1)}, u32[]{:S(2)}, u32[]{:S(2)}) collective-permute-start(bf16[256,384]{1,0:T(8,128)(2,1)S(1)} %copy-done.1), channel_id=1, source_target_pairs={{0,16},{16,0},{32,48},{48,32},{1,17},{17,1},{33,49},{49,33},{2,18}... | collective-permute-start | bytes 589832 | tf_op jit(solution)/shard_map/ppermute | solution.py:147
  15.6 10.1 %collective-permute-start.2 = (bf16[256,384]{1,0:T(8,128)(2,1)S(1)}, bf16[256,384]{1,0:T(8,128)(2,1)S(1)}, u32[]{:S(2)}, u32[]{:S(2)}) collective-permute-start(bf16[256,384]{1,0:T(8,128)(2,1)S(1)} %copy-done.1), channel_id=1, source_target_pairs={{0,48},{16,32},{32,16},{48,0},{1,49},{17,33},{33,17},{49,1},{2,50}... | collective-permute-start | bytes 589832 | tf_op jit(solution)/shard_map/ppermute | solution.py:147
  34.2 19.9 %all-to-all-start.1 = ((bf16[8,144,384]{2,1,0:T(8,128)(2,1)}), bf16[8,144,384]{2,1,0:T(8,128)(2,1)S(1)}, u32[]{:S(2)}, u32[]{:S(2)}) async-start(bf16[8,144,384]{2,1,0:T(8,128)(2,1)} %attend.1), calls=%async_computation.1 | async-start | bytes 1769472 | tf_op jit(solution)/shard_map/all_to_all | solution.py:158
  39.9 6.8 %collective-permute-start.3 = (bf16[384,3072]{1,0:T(8,128)(2,1)}, bf16[384,3072]{1,0:T(8,128)(2,1)S(1)}, u32[]{:S(2)}, u32[]{:S(2)}) collective-permute-start(bf16[384,3072]{1,0:T(8,128)(2,1)} %w_any.3), channel_id=1, source_target_pairs={{0,1},{1,0},{2,3},{3,2},{4,5},{5,4},{6,7},{7,6},{8,9},{9,8},{10,11... | collective-permute-start | bytes 7077896 | tf_op jit(solution)/shard_map/ppermute | solution.py:153
  56.9 11.1 %copy-start = (bf16[64,3072]{1,0:T(8,128)(2,1)S(1)}, bf16[64,3072]{1,0:T(8,128)(2,1)}, u32[]{:S(2)}) copy-start(bf16[64,3072]{1,0:T(8,128)(2,1)} %latent_ref.1) | copy-start | bytes 1179652
  56.9 11.0 %copy-start.2 = (f32[8,3072]{1,0:T(8,128)S(1)}, f32[8,3072]{1,0:T(8,128)}, u32[]{:S(2)}) copy-start(f32[8,3072]{1,0:T(8,128)} %gate_ref.1) | copy-start | bytes 294916
  56.9 11.0 %copy-start.4 = (s32[8]{0:T(128)S(1)}, s32[8]{0:T(128)}, u32[]{:S(2)}) copy-start(s32[8]{0:T(128)} %text_ref.1) | copy-start | bytes 100
  56.9 11.0 %collective-permute-start.4 = (bf16[64,3072]{1,0:T(8,128)(2,1)S(1)}, bf16[64,3072]{1,0:T(8,128)(2,1)S(1)}, u32[]{:S(2)}, u32[]{:S(2)}) collective-permute-start(bf16[64,3072]{1,0:T(8,128)(2,1)S(1)} %project_given.1), channel_id=1, source_target_pairs={{0,2},{1,19},{2,16},{3,1},{16,18},{17,3},{18,0},{19,17},{4,6},{5,2... | collective-permute-start | bytes 1179656 | tf_op jit(solution)/shard_map/ppermute | solution.py:170

commit v4 on v3

v4 whole, which is shorter than its diff:
```python
import functools
import math

import jax
import jax.numpy as jnp
from jax import lax
from jax.experimental import pallas as pl
from jax.experimental.pallas import tpu as pltpu
from jax.sharding import Mesh, PartitionSpec as P

HEAD_DIM = 128
GROUP = 16
LANES = 128
STATS = 8
SCALE = math.log2(math.e) / math.sqrt(HEAD_DIM)
SMEM = pl.BlockSpec(memory_space=pltpu.SMEM)
VMEM = pl.BlockSpec(memory_space=pltpu.VMEM)
HBM = pl.BlockSpec(memory_space=pltpu.HBM)


def attend_kernel(split_ref, q0, q1, q2, q3, kv_ref, out_ref, v_ones):
    request = lax.axis_index("r")
    column, y, first_core = lax.axis_index("z") * 2 + lax.axis_index("h"), lax.axis_index("y"), lax.axis_index("c") == 0
    mine = jnp.where(first_core, column, y)
    blocks, _, tokens, width = kv_ref.shape
    heads = width // HEAD_DIM
    keys = blocks * tokens
    part = tokens // 4
    slot = lax.broadcasted_iota(jnp.int32, (1, tokens), 1)
    bias = jnp.concatenate(
        [jnp.where(slot < split_ref[request, jnp.where(first_core, column * 4 + b, b * 4 + y)], 0.0, -1e30) for b in range(blocks)], axis=1
    )
    lane = lax.broadcasted_iota(jnp.int32, (tokens, LANES), 1)
    for h in range(heads):
        v_ones[h, :, :HEAD_DIM] = kv_ref[:, 1, :, h * HEAD_DIM:(h + 1) * HEAD_DIM].reshape(keys, HEAD_DIM)
        v_ones[h, :, HEAD_DIM:] = jnp.ones((keys, LANES), jnp.bfloat16)
    for d, q_ref in enumerate((q0, q1, q2, q3)):
        target = jnp.bitwise_xor(mine, d)
        stats = jnp.zeros((tokens, LANES), jnp.float32)
        for h in range(heads):
            cols = slice(h * HEAD_DIM, (h + 1) * HEAD_DIM)
            k = kv_ref[:, 0, :, cols].reshape(keys, HEAD_DIM)
            s = lax.dot_general(q_ref[:, cols], k, (((1,), (1,)), ((), ())), preferred_element_type=jnp.float32)
            s = s + bias
            top = jnp.max(s, axis=1, keepdims=True) * SCALE
            high = top.astype(jnp.bfloat16).astype(jnp.float32)
            low = (top - high + jnp.abs(top) * 2.0**-16).astype(jnp.bfloat16).astype(jnp.float32)
            p = jnp.exp2(s * SCALE - (high + low))
            both = jnp.dot(p.astype(jnp.bfloat16), v_ones[h], preferred_element_type=jnp.float32)
            o, total = both[:, :HEAD_DIM].astype(jnp.bfloat16), both[:, HEAD_DIM:]
            for quarter in range(4):
                start = quarter * (part + STATS)
                out_ref[target, start:start + part, cols] = o[quarter * part:(quarter + 1) * part]
            total_high = total.astype(jnp.bfloat16).astype(jnp.float32)
            for j, piece in enumerate((high, low, total_high, total - total_high)):
                stats = jnp.where(lane == STATS * h + j, piece, stats)
        stats = stats.T.astype(jnp.bfloat16)
        for quarter in range(4):
            start = quarter * (part + STATS) + part
            here = slice(quarter // 2 * LANES, (quarter // 2 + 1) * LANES)
            tile = [stats[STATS * h:STATS * (h + 1), here] for h in range(heads)]
            out_ref[target, start:start + STATS] = jnp.concatenate(tile, axis=1)


def combine_kernel(part_ref, w_any, keep_ref, give_ref, w_ref, sem):
    fetch = pltpu.make_async_copy(w_any, w_ref, sem)
    fetch.start()
    count, width = keep_ref.shape[0] // 2, keep_ref.shape[1]
    heads = width // HEAD_DIM
    side, core = lax.axis_index("l"), lax.axis_index("c")
    for ref, parity in ((keep_ref, core), (give_ref, 1 - core)):
        for chunk, pair in enumerate((side, 1 - side)):
            first = pl.multiple_of((2 * pair + parity) * (count + STATS), 8)
            stat = [part_ref[p, pl.ds(first + count, STATS)].astype(jnp.float32) for p in range(4)]
            stat = [s[:, h * HEAD_DIM:(h + 1) * HEAD_DIM] for s in stat for h in range(heads)]
            stat.append(jnp.zeros((LANES - STATS * len(stat), LANES), jnp.float32))
            stat = jnp.concatenate(stat, axis=0).T
            stat = jnp.where(parity == 0, stat[:count], stat[LANES - count:])
            for h in range(heads):
                cols = slice(h * HEAD_DIM, (h + 1) * HEAD_DIM)
                at = [STATS * (heads * p + h) for p in range(4)]
                c = [[stat[:, a + i:a + i + 1] for i in range(4)] for a in at]
                tops = [x[0] + x[1] for x in c]
                top = functools.reduce(jnp.maximum, tops)
                e = [jnp.exp2(x - top) for x in tops]
                total = sum(a * (x[2] + x[3]) for a, x in zip(e, c))
                mixed = sum(a * part_ref[p, pl.ds(first, count), cols].astype(jnp.float32) for p, a in enumerate(e))
                ref[chunk * count:(chunk + 1) * count, cols] = (mixed / total).astype(jnp.bfloat16)
    fetch.wait()


def project_kernel(first, keep_ref, got_ref, w_mine, w_other, out_ref):
    rows = slice(first, first + out_ref.shape[0])
    both = jnp.dot(keep_ref[rows], w_mine[...], preferred_element_type=jnp.float32)
    both = both + jnp.dot(got_ref[rows], w_other[...], preferred_element_type=jnp.float32)
    out_ref[...] = both.astype(out_ref.dtype)


def finish_kernel(split_ref, text_ref, own_ref, got_ref, latent_ref, gate_ref, out_ref):
    request = lax.axis_index("r")
    index = (lax.axis_index("z") * 2 + lax.axis_index("h")) * 4 + lax.axis_index("y")
    rows = latent_ref.shape[0]
    offset = jnp.int32(0)
    for g in range(GROUP):
        offset = offset + jnp.where(g < index, split_ref[request, g], 0)
    first = text_ref[request] - offset
    last = split_ref[request, index]
    slot = (lax.axis_index("l") * 2 + lax.axis_index("c")) * rows
    slot = slot + lax.broadcasted_iota(jnp.int32, (rows, 1), 0)
    image = (slot >= first) & (slot < last)
    base = latent_ref[...].astype(jnp.float32)
    projected = own_ref[...] + got_ref[...].astype(jnp.float32)
    gate = gate_ref[pl.ds(request, 1), :]
    out_ref[...] = jnp.where(image, base + gate * projected, base).astype(jnp.bfloat16)


def call(kernel, name, outs, specs, args, scratch=(), room=8):
    return pl.pallas_call(
        kernel,
        out_shape=[jax.ShapeDtypeStruct(*o) for o in outs],
        in_specs=specs,
        out_specs=[VMEM] * len(outs),
        scratch_shapes=scratch,
        compiler_params=pltpu.CompilerParams(vmem_limit_bytes=room << 20),
        name=name,
    )(*args)


def in_hbm(x):
    return pltpu.with_memory_space_constraint(x, pltpu.HBM)


def on_device(latent, queries, key_vectors, value_vectors, proj_weight, gate_scale, text_length, split_table):
    tokens, width = queries.shape
    rows, depth = latent.shape
    bf16 = jnp.bfloat16
    group = ("z", "h", "y", "c")

    def spot(column, y, core):
        return (column * 4 + y) * 2 + core

    four = range(4)
    along_y = [[[spot(i, j, core) for j in four] for i in four] for core in (0, 1)]
    across = [[[spot(j, i, core) for j in four] for i in four] for core in (0, 1)]

    def swap(x, d):
        pairs = [(spot(i, j, 0), spot(i ^ d, j, 0)) for i in four for j in four]
        pairs += [(spot(i, j, 1), spot(i, j ^ d, 1)) for i in four for j in four]
        return lax.ppermute(x, group, pairs)

    def exchange(x, groups):
        return lax.all_to_all(x, group, 0, 0, tiled=True, axis_index_groups=groups)

    is_key = lax.broadcasted_iota(jnp.int32, (4, 2) + key_vectors.shape, 1) == 0
    stacked = jnp.where(is_key, key_vectors[None, None], value_vectors[None, None])
    kv = exchange(stacked, along_y[0] + across[1])
    q = [queries] + [swap(queries, d) for d in (1, 2, 3)]
    other_core = [(0, 1), (1, 0)]
    late_weight, _ = lax.optimization_barrier((proj_weight, q[2]))
    w_other = lax.ppermute(late_weight, "c", other_core)
    parts = call(
        attend_kernel, "attend", [((4, 4 * (rows + STATS), width), bf16)], [SMEM] + [VMEM] * 5, (split_table, *q, kv),
        [pltpu.VMEM((width // HEAD_DIM, 4 * tokens, HEAD_DIM + LANES), bf16)], room=20,
    )[0]
    parts = exchange(parts, across[0] + along_y[1])
    keep, give, w_mine = call(
        combine_kernel, "combine", [((2 * rows, width), bf16)] * 2 + [(proj_weight.shape, bf16)], [VMEM, HBM],
        (parts, in_hbm(proj_weight)), [pltpu.SemaphoreType.DMA], room=12,
    )
    got = lax.ppermute(give, "c", other_core)
    operands = (keep, got, w_mine, w_other)
    give = call(
        functools.partial(project_kernel, rows), "project_given", [((rows, depth), bf16)], [VMEM] * 4, operands, room=12
    )[0]
    own = call(
        functools.partial(project_kernel, 0), "project_own", [((rows, depth), jnp.float32)], [VMEM] * 4, operands, room=12
    )[0]
    got = lax.ppermute(give, "l", [(0, 1), (1, 0)])
    return call(
        finish_kernel, "finish", [((rows, depth), bf16)], [SMEM] * 2 + [VMEM] * 4,
        (split_table, text_length, own, got, latent, gate_scale),
    )[0]


def solution(mesh):
    parts = Mesh(mesh.devices.reshape(-1, 2, 2, 4, 2, 2), ("r", "z", "h", "y", "l", "c"))
    seq, tp = ("r", "z", "h", "y"), ("l", "c")
    return jax.shard_map(
        on_device,
        mesh=parts,
        in_specs=(
            P(seq + tp, None), P(seq, tp), P(seq, tp), P(seq, tp), P(tp, None), P(), P(), P(),
        ),
        out_specs=P(seq + tp, None),
        check_vma=False,
    )
```

time: 70 us -> 70 us (level)
  the two profiles are of different devices: /device:TPU:64 before, /device:TPU:1 now
where the time goes in v4:
time: 70 us; the launch traced here: 69.5 us
  starting transfers between devices  33.1 us (47%)
  waiting for transfers between devices  21.8 us (31%)
  Pallas kernels  11.2 us (16%)
  other arithmetic  2.42 us (3%)
  local copies, waits for them, and re-layouts  0.95 us (1%)
    all_to_all x2, starting transfers between devices, exchange(): return lax.all_to_all(x, group, 0, 0, tiled=True, axis_index_groups=groups)  14.4 us
    pallas_call x5, Pallas kernels, call(): pl.pallas_call(kernel, out_shape=[jax.ShapeDtypeStruct(*o) for o in outs]...  11.2 us
    ppermute x3, starting transfers between devices, swap(): return lax.ppermute(x, group, pairs)  9.41 us
    ppermute x1, waiting for transfers between devices, on_device(): got = lax.ppermute(give, 'l', [(0, 1), (1, 0)])  9.35 us
    all_to_all x2, waiting for transfers between devices, exchange(): return lax.all_to_all(x, group, 0, 0, tiled=True, axis_index_groups=groups)  5.99 us
    ppermute x3, waiting for transfers between devices, swap(): return lax.ppermute(x, group, pairs)  5.51 us
    ppermute x1, starting transfers between devices, on_device(): got = lax.ppermute(give, 'c', other_core)  4.03 us
    ppermute x1, starting transfers between devices, on_device(): w_other = lax.ppermute(late_weight, 'c', other_core)  3.16 us
  transfers between devices with their start and end apart: 8, of which 6 were waited for; matrix products, arithmetic and copies ran while one was open for 0% of the time, Pallas kernels for 4%

profile of v4, /device:TPU:1, one launch (start us, length us, event | category | flops | bytes accessed | tf_op | source)
XLA Modules:
  0.0 69.5 jit_solution(15442501988373698550)
XLA Ops:
  0.0 2.4 %broadcast_select_fusion = bf16[4,2,256,384]{3,2,1,0:T(8,128)(2,1)} fusion(pred[2]{0:T(512)(128)(4,1)S(1)} %iota_compare_fusion, bf16[256,384]{1,0:T(8,128)(2,1)} %param.11, bf16[256,384]{1,0:T(8,128)(2,1)} %param.10), kind=kLoop, calls=%fused_computation | loop fusion | flops 786432 | bytes 1966082 | tf_op jit(solution)/shard_map/jit(_where)/select_n | solution.py:155
  2.4 0.0 copy-start.2
  2.4 6.3 %all-to-all-start = ((bf16[4,2,256,384]{3,2,1,0:T(8,128)(2,1)}), bf16[4,2,256,384]{3,2,1,0:T(8,128)(2,1)S(1)}, u32[]{:S(2)}, u32[]{:S(2)}) async-start(bf16[4,2,256,384]{3,2,1,0:T(8,128)(2,1)} %broadcast_select_fusion), calls=%async_computation | async-start | bytes 3145728 | tf_op jit(solution)/shard_map/all_to_all | solution.py:152
  8.8 0.0 copy-done.2
  8.8 4.8 %collective-permute-start.1 = (bf16[256,384]{1,0:T(8,128)(2,1)S(1)}, bf16[256,384]{1,0:T(8,128)(2,1)S(1)}, u32[]{:S(2)}, u32[]{:S(2)}) collective-permute-start(bf16[256,384]{1,0:T(8,128)(2,1)S(1)} %copy-done.2), channel_id=1, source_target_pairs={{0,32},{4,36},{8,40},{12,44},{16,48},{20,52},{24,56},{28,60},{32,0... | collective-permute-start | bytes 589832 | tf_op jit(solution)/shard_map/ppermute | solution.py:149
  13.6 2.3 %collective-permute-start = (bf16[256,384]{1,0:T(8,128)(2,1)S(1)}, bf16[256,384]{1,0:T(8,128)(2,1)S(1)}, u32[]{:S(2)}, u32[]{:S(2)}) collective-permute-start(bf16[256,384]{1,0:T(8,128)(2,1)S(1)} %copy-done.2), channel_id=1, source_target_pairs={{0,16},{4,20},{8,24},{12,28},{16,0},{20,4},{24,8},{28,12},{32,48},... | collective-permute-start | bytes 589832 | tf_op jit(solution)/shard_map/ppermute | solution.py:149
  15.9 2.3 %collective-permute-start.2 = (bf16[256,384]{1,0:T(8,128)(2,1)S(1)}, bf16[256,384]{1,0:T(8,128)(2,1)S(1)}, u32[]{:S(2)}, u32[]{:S(2)}) collective-permute-start(bf16[256,384]{1,0:T(8,128)(2,1)S(1)} %copy-done.2), channel_id=1, source_target_pairs={{0,48},{4,52},{8,56},{12,60},{16,32},{20,36},{24,40},{28,44},{32,1... | collective-permute-start | bytes 589832 | tf_op jit(solution)/shard_map/ppermute | solution.py:149
  18.2 0.1 collective-permute-done.1.q2
  18.3 4.3 %collective-permute-done.q1 = bf16[256,384]{1,0:T(8,128)(2,1)S(1)} collective-permute-done((bf16[256,384]{1,0:T(8,128)(2,1)S(1)}, bf16[256,384]{1,0:T(8,128)(2,1)S(1)}, u32[]{:S(2)}, u32[]{:S(2)}) %collective-permute-start) | collective-permute-done | bytes 196640 | tf_op jit(solution)/shard_map/ppermute | solution.py:149
  22.6 1.2 %collective-permute-done.2.q3 = bf16[256,384]{1,0:T(8,128)(2,1)S(1)} collective-permute-done((bf16[256,384]{1,0:T(8,128)(2,1)S(1)}, bf16[256,384]{1,0:T(8,128)(2,1)S(1)}, u32[]{:S(2)}, u32[]{:S(2)}) %collective-permute-start.2) | collective-permute-done | bytes 196640 | tf_op jit(solution)/shard_map/ppermute | solution.py:149
  23.7 0.0 all-to-all-done.kv_ref
  23.7 0.0 copy-done.4
  23.7 5.8 %attend.1 = bf16[4,288,384]{2,1,0:T(8,128)(2,1)S(1)} custom-call(s32[8,16]{1,0:T(8,128)S(1)} %copy-done.4, bf16[256,384]{1,0:T(8,128)(2,1)S(1)} %copy-done.2, bf16[256,384]{1,0:T(8,128)(2,1)S(1)} %collective-permute-done.q1, bf16[256,384]{1,0:T(8,128)(2,1)S(1)} %collective-permute-done.1.q2, bf16[256,384]{1,0:T(8,128)(2,1)S(1)} %collective-permute-done.2.q3, ...), custom_call_target="tpu_custom_call" | custom-call | tf_op jit(solution)/shard_map/attend/pallas_call | solution.py:118
  29.5 0.9 %copy-done = bf16[4,288,384]{2,1,0:T(8,128)(2,1)} copy-done((bf16[4,288,384]{2,1,0:T(8,128)(2,1)}, bf16[4,288,384]{2,1,0:T(8,128)(2,1)S(1)}, u32[]{:S(2)}) %copy-start) | copy-done | bytes 884760
  30.4 8.1 %all-to-all-start.1 = ((bf16[4,288,384]{2,1,0:T(8,128)(2,1)}), bf16[4,288,384]{2,1,0:T(8,128)(2,1)S(1)}, u32[]{:S(2)}, u32[]{:S(2)}) async-start(bf16[4,288,384]{2,1,0:T(8,128)(2,1)} %copy-done), calls=%async_computation.1 | async-start | bytes 1769472 | tf_op jit(solution)/shard_map/all_to_all | solution.py:152
  38.5 3.2 %collective-permute-start.4 = (bf16[384,3072]{1,0:T(8,128)(2,1)}, bf16[384,3072]{1,0:T(8,128)(2,1)S(1)}, u32[]{:S(2)}, u32[]{:S(2)}) collective-permute-start(bf16[384,3072]{1,0:T(8,128)(2,1)} %w_any.1), channel_id=1, source_target_pairs={{0,1},{1,0},{2,3},{3,2},{4,5},{5,4},{6,7},{7,6},{8,9},{9,8},{10,11... | collective-permute-start | bytes 7077896 | tf_op jit(solution)/shard_map/ppermute | solution.py:160
  41.7 6.0 %all-to-all-done.1.part_ref = bf16[4,288,384]{2,1,0:T(8,128)(2,1)S(1)} async-done(((bf16[4,288,384]{2,1,0:T(8,128)(2,1)}), bf16[4,288,384]{2,1,0:T(8,128)(2,1)S(1)}, u32[]{:S(2)}, u32[]{:S(2)}) %all-to-all-start.1) | async-done | bytes 884768 | tf_op jit(solution)/shard_map/all_to_all | solution.py:152
  47.7 2.0 %combine.1 = (bf16[128,384]{1,0:T(8,128)(2,1)S(1)}, bf16[128,384]{1,0:T(8,128)(2,1)S(1)}, bf16[384,3072]{1,0:T(8,128)(2,1)S(1)}) custom-call(bf16[4,288,384]{2,1,0:T(8,128)(2,1)S(1)} %all-to-all-done.1.part_ref, bf16[384,3072]{1,0:T(8,128)(2,1)} %w_any.1), custom_call_target="tpu_custom_call" | custom-call | tf_op jit(solution)/shard_map/combine/pallas_call | solution.py:118
  49.6 4.0 %collective-permute-start.3 = (bf16[128,384]{1,0:T(8,128)(2,1)S(1)}, bf16[128,384]{1,0:T(8,128)(2,1)S(1)}, u32[]{:S(2)}, u32[]{:S(2)}) collective-permute-start(bf16[128,384]{1,0:T(8,128)(2,1)S(1)} %get-tuple-element.10), channel_id=1, source_target_pairs={{0,1},{1,0},{2,3},{3,2},{4,5},{5,4},{6,7},{7,6},{8,9},{9,8},{10,11... | collective-permute-start | bytes 294920 | tf_op jit(solution)/shard_map/ppermute | solution.py:170
  53.7 0.0 collective-permute-done.4.w_other
  53.7 0.9 %collective-permute-done.3.got_ref = bf16[128,384]{1,0:T(8,128)(2,1)S(1)} collective-permute-done((bf16[128,384]{1,0:T(8,128)(2,1)S(1)}, bf16[128,384]{1,0:T(8,128)(2,1)S(1)}, u32[]{:S(2)}, u32[]{:S(2)}) %collective-permute-start.3) | collective-permute-done | bytes 98336 | tf_op jit(solution)/shard_map/ppermute | solution.py:170
  54.6 1.0 %project_given.1 = bf16[64,3072]{1,0:T(8,128)(2,1)S(1)} custom-call(bf16[128,384]{1,0:T(8,128)(2,1)S(1)} %get-tuple-element.9.keep_ref, bf16[128,384]{1,0:T(8,128)(2,1)S(1)} %collective-permute-done.3.got_ref, bf16[384,3072]{1,0:T(8,128)(2,1)S(1)} %get-tuple-element.11.w_mine, bf16[384,3072]{1,0:T(8,128)(2,1)S(1)} %collective-permute-done.4.w_other), custom_call_target="tpu_custom_call" | custom-call | tf_op jit(solution)/shard_map/project_given/pallas_call | solution.py:118
  55.5 0.0 copy-start.1
  55.6 0.0 copy-start.3
  55.6 0.0 copy-start.5
  55.6 2.1 %collective-permute-start.5 = (bf16[64,3072]{1,0:T(8,128)(2,1)S(1)}, bf16[64,3072]{1,0:T(8,128)(2,1)S(1)}, u32[]{:S(2)}, u32[]{:S(2)}) collective-permute-start(bf16[64,3072]{1,0:T(8,128)(2,1)S(1)} %project_given.1), channel_id=1, source_target_pairs={{0,2},{2,0},{1,3},{3,1},{4,6},{6,4},{5,7},{7,5},{8,10},{10,8},{9,1... | collective-permute-start | bytes 1179656 | tf_op jit(solution)/shard_map/ppermute | solution.py:178
  57.6 1.0 %project_own.1.own_ref = f32[64,3072]{1,0:T(8,128)S(1)} custom-call(bf16[128,384]{1,0:T(8,128)(2,1)S(1)} %get-tuple-element.9.keep_ref, bf16[128,384]{1,0:T(8,128)(2,1)S(1)} %collective-permute-done.3.got_ref, bf16[384,3072]{1,0:T(8,128)(2,1)S(1)} %get-tuple-element.11.w_mine, bf16[384,3072]{1,0:T(8,128)(2,1)S(1)} %collective-permute-done.4.w_other), custom_call_target="tpu_custom_call" | custom-call | tf_op jit(solution)/shard_map/project_own/pallas_call | solution.py:118
  58.6 9.3 %collective-permute-done.5.got_ref = bf16[64,3072]{1,0:T(8,128)(2,1)S(1)} collective-permute-done((bf16[64,3072]{1,0:T(8,128)(2,1)S(1)}, bf16[64,3072]{1,0:T(8,128)(2,1)S(1)}, u32[]{:S(2)}, u32[]{:S(2)}) %collective-permute-start.5) | collective-permute-done | bytes 393248 | tf_op jit(solution)/shard_map/ppermute | solution.py:178
  68.0 0.0 copy-done.1
  68.0 0.0 copy-done.3
  68.0 0.0 copy-done.5
  68.0 1.6 %finish.1 = bf16[64,3072]{1,0:T(8,128)(2,1)} custom-call(s32[8,16]{1,0:T(8,128)S(1)} %copy-done.4, s32[8]{0:T(128)S(1)} %copy-done.5, f32[64,3072]{1,0:T(8,128)S(1)} %project_own.1.own_ref, bf16[64,3072]{1,0:T(8,128)(2,1)S(1)} %collective-permute-done.5.got_ref, bf16[64,3072]{1,0:T(8,128)(2,1)S(1)} %copy-done.1, f32[8,3072]{1,0:T(8,128)S(1)} %copy-done.3), custom_call_target="tpu_custom_call" | custom-call | tf_op jit(solution)/shard_map/finish/pallas_call | solution.py:118
  (3 shorter events, 0.0 us)
Async XLA Ops:
  2.4 6.3 %copy-start.2 = (bf16[256,384]{1,0:T(8,128)(2,1)S(1)}, bf16[256,384]{1,0:T(8,128)(2,1)}, u32[]{:S(2)}) copy-start(bf16[256,384]{1,0:T(8,128)(2,1)} %q0.1) | copy-start | bytes 589828
  2.4 21.3 %copy-start.4 = (s32[8,16]{1,0:T(8,128)S(1)}, s32[8,16]{1,0:T(8,128)}, u32[]{:S(2)}) copy-start(s32[8,16]{1,0:T(8,128)} %split_ref.3) | copy-start | bytes 1540
  2.4 21.3 %all-to-all-start = ((bf16[4,2,256,384]{3,2,1,0:T(8,128)(2,1)}), bf16[4,2,256,384]{3,2,1,0:T(8,128)(2,1)S(1)}, u32[]{:S(2)}, u32[]{:S(2)}) async-start(bf16[4,2,256,384]{3,2,1,0:T(8,128)(2,1)} %broadcast_select_fusion), calls=%async_computation | async-start | bytes 3145728 | tf_op jit(solution)/shard_map/all_to_all | solution.py:152
  8.8 9.5 %collective-permute-start.1 = (bf16[256,384]{1,0:T(8,128)(2,1)S(1)}, bf16[256,384]{1,0:T(8,128)(2,1)S(1)}, u32[]{:S(2)}, u32[]{:S(2)}) collective-permute-start(bf16[256,384]{1,0:T(8,128)(2,1)S(1)} %copy-done.2), channel_id=1, source_target_pairs={{0,32},{4,36},{8,40},{12,44},{16,48},{20,52},{24,56},{28,60},{32,0... | collective-permute-start | bytes 589832 | tf_op jit(solution)/shard_map/ppermute | solution.py:149
  13.6 9.0 %collective-permute-start = (bf16[256,384]{1,0:T(8,128)(2,1)S(1)}, bf16[256,384]{1,0:T(8,128)(2,1)S(1)}, u32[]{:S(2)}, u32[]{:S(2)}) collective-permute-start(bf16[256,384]{1,0:T(8,128)(2,1)S(1)} %copy-done.2), channel_id=1, source_target_pairs={{0,16},{4,20},{8,24},{12,28},{16,0},{20,4},{24,8},{28,12},{32,48},... | collective-permute-start | bytes 589832 | tf_op jit(solution)/shard_map/ppermute | solution.py:149
  15.9 7.8 %collective-permute-start.2 = (bf16[256,384]{1,0:T(8,128)(2,1)S(1)}, bf16[256,384]{1,0:T(8,128)(2,1)S(1)}, u32[]{:S(2)}, u32[]{:S(2)}) collective-permute-start(bf16[256,384]{1,0:T(8,128)(2,1)S(1)} %copy-done.2), channel_id=1, source_target_pairs={{0,48},{4,52},{8,56},{12,60},{16,32},{20,36},{24,40},{28,44},{32,1... | collective-permute-start | bytes 589832 | tf_op jit(solution)/shard_map/ppermute | solution.py:149
  29.5 0.9 %copy-start = (bf16[4,288,384]{2,1,0:T(8,128)(2,1)}, bf16[4,288,384]{2,1,0:T(8,128)(2,1)S(1)}, u32[]{:S(2)}) copy-start(bf16[4,288,384]{2,1,0:T(8,128)(2,1)S(1)} %attend.1) | copy-start | bytes 2654212
  30.4 17.3 %all-to-all-start.1 = ((bf16[4,288,384]{2,1,0:T(8,128)(2,1)}), bf16[4,288,384]{2,1,0:T(8,128)(2,1)S(1)}, u32[]{:S(2)}, u32[]{:S(2)}) async-start(bf16[4,288,384]{2,1,0:T(8,128)(2,1)} %copy-done), calls=%async_computation.1 | async-start | bytes 1769472 | tf_op jit(solution)/shard_map/all_to_all | solution.py:152
  38.5 15.2 %collective-permute-start.4 = (bf16[384,3072]{1,0:T(8,128)(2,1)}, bf16[384,3072]{1,0:T(8,128)(2,1)S(1)}, u32[]{:S(2)}, u32[]{:S(2)}) collective-permute-start(bf16[384,3072]{1,0:T(8,128)(2,1)} %w_any.1), channel_id=1, source_target_pairs={{0,1},{1,0},{2,3},{3,2},{4,5},{5,4},{6,7},{7,6},{8,9},{9,8},{10,11... | collective-permute-start | bytes 7077896 | tf_op jit(solution)/shard_map/ppermute | solution.py:160
  49.6 5.0 %collective-permute-start.3 = (bf16[128,384]{1,0:T(8,128)(2,1)S(1)}, bf16[128,384]{1,0:T(8,128)(2,1)S(1)}, u32[]{:S(2)}, u32[]{:S(2)}) collective-permute-start(bf16[128,384]{1,0:T(8,128)(2,1)S(1)} %get-tuple-element.10), channel_id=1, source_target_pairs={{0,1},{1,0},{2,3},{3,2},{4,5},{5,4},{6,7},{7,6},{8,9},{9,8},{10,11... | collective-permute-start | bytes 294920 | tf_op jit(solution)/shard_map/ppermute | solution.py:170
  55.5 12.4 %copy-start.1 = (bf16[64,3072]{1,0:T(8,128)(2,1)S(1)}, bf16[64,3072]{1,0:T(8,128)(2,1)}, u32[]{:S(2)}) copy-start(bf16[64,3072]{1,0:T(8,128)(2,1)} %latent_ref.1) | copy-start | bytes 1179652
  55.6 12.4 %copy-start.3 = (f32[8,3072]{1,0:T(8,128)S(1)}, f32[8,3072]{1,0:T(8,128)}, u32[]{:S(2)}) copy-start(f32[8,3072]{1,0:T(8,128)} %gate_ref.1) | copy-start | bytes 294916
  55.6 12.4 %copy-start.5 = (s32[8]{0:T(128)S(1)}, s32[8]{0:T(128)}, u32[]{:S(2)}) copy-start(s32[8]{0:T(128)} %text_ref.1) | copy-start | bytes 100
  55.6 12.4 %collective-permute-start.5 = (bf16[64,3072]{1,0:T(8,128)(2,1)S(1)}, bf16[64,3072]{1,0:T(8,128)(2,1)S(1)}, u32[]{:S(2)}, u32[]{:S(2)}) collective-permute-start(bf16[64,3072]{1,0:T(8,128)(2,1)S(1)} %project_given.1), channel_id=1, source_target_pairs={{0,2},{2,0},{1,3},{3,1},{4,6},{6,4},{5,7},{7,5},{8,10},{10,8},{9,1... | collective-permute-start | bytes 1179656 | tf_op jit(solution)/shard_map/ppermute | solution.py:178

commit v5 on v4

--- a/solution.py
+++ b/solution.py
@@ -12,48 +12,65 @@
 GROUP = 16
 LANES = 128
 STATS = 8
+FIRST, LAST = 3, (1, 2)
 SCALE = math.log2(math.e) / math.sqrt(HEAD_DIM)
 SMEM = pl.BlockSpec(memory_space=pltpu.SMEM)
 VMEM = pl.BlockSpec(memory_space=pltpu.VMEM)
 HBM = pl.BlockSpec(memory_space=pltpu.HBM)
 
 
-def attend_kernel(split_ref, q0, q1, q2, q3, kv_ref, out_ref, v_ones):
+def attend_kernel(offsets, split_ref, q_ref, kv_a, kv_b, *refs):
     request = lax.axis_index("r")
     column, y, first_core = lax.axis_index("z") * 2 + lax.axis_index("h"), lax.axis_index("y"), lax.axis_index("c") == 0
-    mine = jnp.where(first_core, column, y)
-    blocks, _, tokens, width = kv_ref.shape
+    earlier = len(refs) == 5
+    if earlier:
+        sum_ref, top_ref, out_ref, k_all, v_ones = refs
+    else:
+        sum_ref, top_ref, k_all, v_ones = refs
+    blocks, tokens, width = q_ref.shape
     heads = width // HEAD_DIM
-    keys = blocks * tokens
     part = tokens // 4
     slot = lax.broadcasted_iota(jnp.int32, (1, tokens), 1)
-    bias = jnp.concatenate(
-        [jnp.where(slot < split_ref[request, jnp.where(first_core, column * 4 + b, b * 4 + y)], 0.0, -1e30) for b in range(blocks)], axis=1
-    )
+    owners = [jnp.where(first_core, column * 4 + (y ^ b), (column ^ b) * 4 + y) for b in offsets]
+    bias = jnp.concatenate([jnp.where(slot < split_ref[request, i], 0.0, -1e30) for i in owners], axis=1)
     lane = lax.broadcasted_iota(jnp.int32, (tokens, LANES), 1)
-    for h in range(heads):
-        v_ones[h, :, :HEAD_DIM] = kv_ref[:, 1, :, h * HEAD_DIM:(h + 1) * HEAD_DIM].reshape(keys, HEAD_DIM)
-        v_ones[h, :, HEAD_DIM:] = jnp.ones((keys, LANES), jnp.bfloat16)
-    for d, q_ref in enumerate((q0, q1, q2, q3)):
-        target = jnp.bitwise_xor(mine, d)
+    for b, kv_ref in enumerate((kv_a, kv_b)):
+        rows = slice(b * tokens, (b + 1) * tokens)
+        k_all[rows] = kv_ref[0]
+        for h in range(heads):
+            v_ones[h, rows, :HEAD_DIM] = kv_ref[1, :, h * HEAD_DIM:(h + 1) * HEAD_DIM]
+            v_ones[h, rows, HEAD_DIM:] = jnp.ones((tokens, LANES), jnp.bfloat16)
+    for target in range(blocks):
         stats = jnp.zeros((tokens, LANES), jnp.float32)
         for h in range(heads):
             cols = slice(h * HEAD_DIM, (h + 1) * HEAD_DIM)
-            k = kv_ref[:, 0, :, cols].reshape(keys, HEAD_DIM)
-            s = lax.dot_general(q_ref[:, cols], k, (((1,), (1,)), ((), ())), preferred_element_type=jnp.float32)
+            s = lax.dot_general(
+                q_ref[target, :, cols], k_all[:, cols], (((1,), (1,)), ((), ())), preferred_element_type=jnp.float32
+            )
             s = s + bias
-            top = jnp.max(s, axis=1, keepdims=True) * SCALE
+            top = jnp.broadcast_to(jnp.max(s, axis=1, keepdims=True) * SCALE, (tokens, LANES))
+            if earlier:
+                before = top_ref[target, h]
+                top = jnp.maximum(top, before)
             high = top.astype(jnp.bfloat16).astype(jnp.float32)
             low = (top - high + jnp.abs(top) * 2.0**-16).astype(jnp.bfloat16).astype(jnp.float32)
-            p = jnp.exp2(s * SCALE - (high + low))
+            p = jnp.exp2(s * SCALE - jnp.tile(high + low, (1, s.shape[1] // LANES)))
             both = jnp.dot(p.astype(jnp.bfloat16), v_ones[h], preferred_element_type=jnp.float32)
-            o, total = both[:, :HEAD_DIM].astype(jnp.bfloat16), both[:, HEAD_DIM:]
+            if not earlier:
+                sum_ref[target, h] = both
+                top_ref[target, h] = high + low
+                continue
+            shrink = jnp.exp2(before - (high + low))
+            o = (both[:, :HEAD_DIM] + shrink * sum_ref[target, h, :, :HEAD_DIM]).astype(jnp.bfloat16)
+            total = both[:, HEAD_DIM:] + shrink * sum_ref[target, h, :, HEAD_DIM:]
             for quarter in range(4):
                 start = quarter * (part + STATS)
                 out_ref[target, start:start + part, cols] = o[quarter * part:(quarter + 1) * part]
             total_high = total.astype(jnp.bfloat16).astype(jnp.float32)
             for j, piece in enumerate((high, low, total_high, total - total_high)):
                 stats = jnp.where(lane == STATS * h + j, piece, stats)
+        if not earlier:
+            continue
         stats = stats.T.astype(jnp.bfloat16)
         for quarter in range(4):
             start = quarter * (part + STATS) + part
@@ -144,23 +161,29 @@
     across = [[[spot(j, i, core) for j in four] for i in four] for core in (0, 1)]
 
     def swap(x, d):
-        pairs = [(spot(i, j, 0), spot(i ^ d, j, 0)) for i in four for j in four]
-        pairs += [(spot(i, j, 1), spot(i, j ^ d, 1)) for i in four for j in four]
+        pairs = [(spot(i, j, 0), spot(i, j ^ d, 0)) for i in four for j in four]
+        pairs += [(spot(i, j, 1), spot(i ^ d, j, 1)) for i in four for j in four]
         return lax.ppermute(x, group, pairs)
 
     def exchange(x, groups):
         return lax.all_to_all(x, group, 0, 0, tiled=True, axis_index_groups=groups)
 
-    is_key = lax.broadcasted_iota(jnp.int32, (4, 2) + key_vectors.shape, 1) == 0
-    stacked = jnp.where(is_key, key_vectors[None, None], value_vectors[None, None])
-    kv = exchange(stacked, along_y[0] + across[1])
-    q = [queries] + [swap(queries, d) for d in (1, 2, 3)]
+    stacked = jnp.stack([key_vectors, value_vectors])
+    kv = [stacked] + [swap(stacked, d) for d in (1, 2, 3)]
+    q = exchange(jnp.broadcast_to(queries[None], (4,) + queries.shape), across[0] + along_y[1])
     other_core = [(0, 1), (1, 0)]
-    late_weight, _ = lax.optimization_barrier((proj_weight, q[2]))
+    late_weight, _ = lax.optimization_barrier((proj_weight, kv[LAST[0]]))
     w_other = lax.ppermute(late_weight, "c", other_core)
+    held = [pltpu.VMEM((2 * tokens, width), bf16)]
+    held.append(pltpu.VMEM((width // HEAD_DIM, 2 * tokens, HEAD_DIM + LANES), bf16))
+    state = call(
+        functools.partial(attend_kernel, (0, FIRST)), "attend_early",
+        [((4, width // HEAD_DIM, tokens, n), jnp.float32) for n in (HEAD_DIM + LANES, LANES)], [SMEM] + [VMEM] * 3,
+        (split_table, q, kv[0], kv[FIRST]), held, room=20,
+    )
     parts = call(
-        attend_kernel, "attend", [((4, 4 * (rows + STATS), width), bf16)], [SMEM] + [VMEM] * 5, (split_table, *q, kv),
-        [pltpu.VMEM((width // HEAD_DIM, 4 * tokens, HEAD_DIM + LANES), bf16)], room=20,
+        functools.partial(attend_kernel, LAST), "attend_late", [((4, 4 * (rows + STATS), width), bf16)],
+        [SMEM] + [VMEM] * 5, (split_table, q, kv[LAST[0]], kv[LAST[1]], *state), held, room=20,
     )[0]
     parts = exchange(parts, across[0] + along_y[1])
     keep, give, w_mine = call(

time: 70 us -> 71.7 us (1.024)
  starting transfers between devices: 33.1 us -> 37.6 us
  waiting for transfers between devices: 21.8 us -> 17.8 us
  Pallas kernels: 11.2 us -> 13.7 us
  other arithmetic: 2.42 us -> 0.05 us
  local copies, waits for them, and re-layouts: 0.95 us -> 1.97 us
    all_to_all x2, starting transfers between devices: 14.4 us -> 8.73 us  [exchange(): return lax.all_to_all(x, group, 0, 0, tiled=True, axis_index_groups=groups)]
    ppermute x1, starting transfers between devices: 4.03 us -> 8.95 us  [on_device(): got = lax.ppermute(give, 'c', other_core)]
    all_to_all x2, waiting for transfers between devices: 5.99 us -> 1.07 us  [exchange(): return lax.all_to_all(x, group, 0, 0, tiled=True, axis_index_groups=groups)]
    ppermute x1, starting transfers between devices: 3.16 us -> 7.79 us  [on_device(): w_other = lax.ppermute(late_weight, 'c', other_core)]
    pallas_call x5 -> x6, Pallas kernels: 11.2 us -> 13.7 us  [call(): pl.pallas_call(kernel, out_shape=[jax.ShapeDtypeStruct(*o) for o in outs]...]
    select_n x1 -> x0, other arithmetic: 2.42 us -> none  [on_device(): jnp.where(is_key, key_vectors[None, None], value_vectors[None, None])]
    broadcast_in_dim x0 -> x1, local copies, waits for them, and re-layouts: none -> 1.94 us  [on_device(): jnp.broadcast_to(queries[None], (4,) + queries.shape)]
    ppermute x3, waiting for transfers between devices: 5.51 us -> 6.49 us  [swap(): return lax.ppermute(x, group, pairs)]
  transfers between devices with their start and end apart: 8 -> 8, of which waited for: 6 -> 5; matrix products, arithmetic and copies ran while one was open for 0% -> 0% of each run, Pallas kernels for 4% -> 9%
where the time goes in v5:
time: 71.7 us; the launch traced here: 71.3 us
  starting transfers between devices  37.6 us (52%)
  waiting for transfers between devices  17.8 us (25%)
  Pallas kernels  13.7 us (19%)
  local copies, waits for them, and re-layouts  1.97 us (3%)
    pallas_call x6, Pallas kernels, call(): pl.pallas_call(kernel, out_shape=[jax.ShapeDtypeStruct(*o) for o in outs]...  13.7 us
    ppermute x3, starting transfers between devices, swap(): return lax.ppermute(x, group, pairs)  10.1 us
    ppermute x1, waiting for transfers between devices, on_device(): got = lax.ppermute(give, 'l', [(0, 1), (1, 0)])  9.35 us
    ppermute x1, starting transfers between devices, on_device(): got = lax.ppermute(give, 'c', other_core)  8.95 us
    all_to_all x2, starting transfers between devices, exchange(): return lax.all_to_all(x, group, 0, 0, tiled=True, axis_index_groups=groups)  8.73 us
    ppermute x1, starting transfers between devices, on_device(): w_other = lax.ppermute(late_weight, 'c', other_core)  7.79 us
    ppermute x3, waiting for transfers between devices, swap(): return lax.ppermute(x, group, pairs)  6.49 us
    ppermute x1, starting transfers between devices, on_device(): got = lax.ppermute(give, 'l', [(0, 1), (1, 0)])  2.05 us
  transfers between devices with their start and end apart: 8, of which 5 were waited for; matrix products, arithmetic and copies ran while one was open for 0% of the time, Pallas kernels for 9%

profile of v5, /device:TPU:1, one launch (start us, length us, event | category | flops | bytes accessed | tf_op | source)
XLA Modules:
  0.0 71.3 jit_solution(2413490170235560354)
XLA Ops:
  0.0 1.9 %broadcast_in_dim.2 = bf16[4,256,384]{2,1,0:T(8,128)(2,1)} broadcast(bf16[256,384]{1,0:T(8,128)(2,1)} %param.9), dimensions={1,2} | broadcast | bytes 983040 | tf_op jit(solution)/shard_map/broadcast_in_dim | solution.py:173
  2.0 5.0 %all-to-all-start = ((bf16[4,256,384]{2,1,0:T(8,128)(2,1)}), bf16[4,256,384]{2,1,0:T(8,128)(2,1)S(1)}, u32[]{:S(2)}, u32[]{:S(2)}) async-start(bf16[4,256,384]{2,1,0:T(8,128)(2,1)} %broadcast_in_dim.2), calls=%async_computation | async-start | bytes 1572864 | tf_op jit(solution)/shard_map/all_to_all | solution.py:169
  7.0 0.0 copy-done.5
  7.0 0.0 copy-done.4
  7.0 6.0 %collective-permute-start.2 = (bf16[2,256,384]{2,1,0:T(8,128)(2,1)S(1)}, bf16[2,256,384]{2,1,0:T(8,128)(2,1)S(1)}, u32[]{:S(2)}, u32[]{:S(2)}) collective-permute-start(bf16[2,256,384]{2,1,0:T(8,128)(2,1)S(1)} %pad_maximum_fusion.kv_a), channel_id=1, source_target_pairs={{0,12},{4,8},{8,4},{12,0},{16,28},{20,24},{24,20},{28,16},{32,44},... | collective-permute-start | bytes 1179656 | tf_op jit(solution)/shard_map/ppermute | solution.py:166
  13.0 2.1 %collective-permute-start = (bf16[2,256,384]{2,1,0:T(8,128)(2,1)S(1)}, bf16[2,256,384]{2,1,0:T(8,128)(2,1)S(1)}, u32[]{:S(2)}, u32[]{:S(2)}) collective-permute-start(bf16[2,256,384]{2,1,0:T(8,128)(2,1)S(1)} %pad_maximum_fusion.kv_a), channel_id=1, source_target_pairs={{0,4},{4,0},{8,12},{12,8},{16,20},{20,16},{24,28},{28,24},{32,36},... | collective-permute-start | bytes 1179656 | tf_op jit(solution)/shard_map/ppermute | solution.py:166
  15.2 2.0 %collective-permute-start.1 = (bf16[2,256,384]{2,1,0:T(8,128)(2,1)S(1)}, bf16[2,256,384]{2,1,0:T(8,128)(2,1)S(1)}, u32[]{:S(2)}, u32[]{:S(2)}) collective-permute-start(bf16[2,256,384]{2,1,0:T(8,128)(2,1)S(1)} %pad_maximum_fusion.kv_a), channel_id=1, source_target_pairs={{0,8},{4,12},{8,0},{12,4},{16,24},{20,28},{24,16},{28,20},{32,40},... | collective-permute-start | bytes 1179656 | tf_op jit(solution)/shard_map/ppermute | solution.py:166
  17.2 4.5 %collective-permute-done.2.kv_b = bf16[2,256,384]{2,1,0:T(8,128)(2,1)S(1)} collective-permute-done((bf16[2,256,384]{2,1,0:T(8,128)(2,1)S(1)}, bf16[2,256,384]{2,1,0:T(8,128)(2,1)S(1)}, u32[]{:S(2)}, u32[]{:S(2)}) %collective-permute-start.2) | collective-permute-done | bytes 393248 | tf_op jit(solution)/shard_map/ppermute | solution.py:166
  21.7 0.0 all-to-all-done.q_ref
  21.7 0.0 copy-done.2
  21.7 3.2 %attend_early.1 = (f32[4,3,256,256]{3,2,1,0:T(8,128)S(1)}, f32[4,3,256,128]{3,2,1,0:T(8,128)S(1)}) custom-call(s32[8,16]{1,0:T(8,128)S(1)} %copy-done.2, bf16[4,256,384]{2,1,0:T(8,128)(2,1)S(1)} %all-to-all-done.q_ref, bf16[2,256,384]{2,1,0:T(8,128)(2,1)S(1)} %pad_maximum_fusion.kv_a, bf16[2,256,384]{2,1,0:T(8,128)(2,1)S(1)} %collective-permute-done.2.kv_b), custom_call_target="tpu_custom_call" | custom-call | tf_op jit(solution)/shard_map/attend_early/pallas_call | solution.py:135
  24.9 2.0 %collective-permute-done.kv_a = bf16[2,256,384]{2,1,0:T(8,128)(2,1)S(1)} collective-permute-done((bf16[2,256,384]{2,1,0:T(8,128)(2,1)S(1)}, bf16[2,256,384]{2,1,0:T(8,128)(2,1)S(1)}, u32[]{:S(2)}, u32[]{:S(2)}) %collective-permute-start) | collective-permute-done | bytes 393248 | tf_op jit(solution)/shard_map/ppermute | solution.py:166
  26.9 0.0 collective-permute-done.1.kv_b
  26.9 5.0 %attend_late.1 = bf16[4,288,384]{2,1,0:T(8,128)(2,1)} custom-call(s32[8,16]{1,0:T(8,128)S(1)} %copy-done.2, bf16[4,256,384]{2,1,0:T(8,128)(2,1)S(1)} %all-to-all-done.q_ref, bf16[2,256,384]{2,1,0:T(8,128)(2,1)S(1)} %collective-permute-done.kv_a, bf16[2,256,384]{2,1,0:T(8,128)(2,1)S(1)} %collective-permute-done.1.kv_b, ...), custom_call_target="tpu_custom_call" | custom-call | tf_op jit(solution)/shard_map/attend_late/pallas_call | solution.py:135
  31.9 3.7 %all-to-all-start.1 = ((bf16[4,288,384]{2,1,0:T(8,128)(2,1)}), bf16[4,288,384]{2,1,0:T(8,128)(2,1)S(1)}, u32[]{:S(2)}, u32[]{:S(2)}) async-start(bf16[4,288,384]{2,1,0:T(8,128)(2,1)} %attend_late.1), calls=%async_computation.1 | async-start | bytes 1769472 | tf_op jit(solution)/shard_map/all_to_all | solution.py:169
  35.6 7.8 %collective-permute-start.4 = (bf16[384,3072]{1,0:T(8,128)(2,1)}, bf16[384,3072]{1,0:T(8,128)(2,1)S(1)}, u32[]{:S(2)}, u32[]{:S(2)}) collective-permute-start(bf16[384,3072]{1,0:T(8,128)(2,1)} %w_any.1), channel_id=1, source_target_pairs={{0,1},{1,0},{2,3},{3,2},{4,5},{5,4},{6,7},{7,6},{8,9},{9,8},{10,11... | collective-permute-start | bytes 7077896 | tf_op jit(solution)/shard_map/ppermute | solution.py:176
  43.4 1.1 %all-to-all-done.1.part_ref = bf16[4,288,384]{2,1,0:T(8,128)(2,1)S(1)} async-done(((bf16[4,288,384]{2,1,0:T(8,128)(2,1)}), bf16[4,288,384]{2,1,0:T(8,128)(2,1)S(1)}, u32[]{:S(2)}, u32[]{:S(2)}) %all-to-all-start.1) | async-done | bytes 884768 | tf_op jit(solution)/shard_map/all_to_all | solution.py:169
  44.5 2.0 %combine.1 = (bf16[128,384]{1,0:T(8,128)(2,1)S(1)}, bf16[128,384]{1,0:T(8,128)(2,1)S(1)}, bf16[384,3072]{1,0:T(8,128)(2,1)S(1)}) custom-call(bf16[4,288,384]{2,1,0:T(8,128)(2,1)S(1)} %all-to-all-done.1.part_ref, bf16[384,3072]{1,0:T(8,128)(2,1)} %w_any.1), custom_call_target="tpu_custom_call" | custom-call | tf_op jit(solution)/shard_map/combine/pallas_call | solution.py:135
  46.4 9.0 %collective-permute-start.3 = (bf16[128,384]{1,0:T(8,128)(2,1)S(1)}, bf16[128,384]{1,0:T(8,128)(2,1)S(1)}, u32[]{:S(2)}, u32[]{:S(2)}) collective-permute-start(bf16[128,384]{1,0:T(8,128)(2,1)S(1)} %get-tuple-element.14), channel_id=1, source_target_pairs={{0,1},{1,0},{2,3},{3,2},{4,5},{5,4},{6,7},{7,6},{8,9},{9,8},{10,11... | collective-permute-start | bytes 294920 | tf_op jit(solution)/shard_map/ppermute | solution.py:193
  55.4 0.0 collective-permute-done.4.w_other
  55.4 0.9 %collective-permute-done.3.got_ref = bf16[128,384]{1,0:T(8,128)(2,1)S(1)} collective-permute-done((bf16[128,384]{1,0:T(8,128)(2,1)S(1)}, bf16[128,384]{1,0:T(8,128)(2,1)S(1)}, u32[]{:S(2)}, u32[]{:S(2)}) %collective-permute-start.3) | collective-permute-done | bytes 98336 | tf_op jit(solution)/shard_map/ppermute | solution.py:193
  56.3 1.0 %project_given.1 = bf16[64,3072]{1,0:T(8,128)(2,1)S(1)} custom-call(bf16[128,384]{1,0:T(8,128)(2,1)S(1)} %get-tuple-element.13.keep_ref, bf16[128,384]{1,0:T(8,128)(2,1)S(1)} %collective-permute-done.3.got_ref, bf16[384,3072]{1,0:T(8,128)(2,1)S(1)} %get-tuple-element.15.w_mine, bf16[384,3072]{1,0:T(8,128)(2,1)S(1)} %collective-permute-done.4.w_other), custom_call_target="tpu_custom_call" | custom-call | tf_op jit(solution)/shard_map/project_given/pallas_call | solution.py:135
  57.3 0.0 copy-start
  57.3 0.0 copy-start.1
  57.3 0.0 copy-start.3
  57.3 2.1 %collective-permute-start.5 = (bf16[64,3072]{1,0:T(8,128)(2,1)S(1)}, bf16[64,3072]{1,0:T(8,128)(2,1)S(1)}, u32[]{:S(2)}, u32[]{:S(2)}) collective-permute-start(bf16[64,3072]{1,0:T(8,128)(2,1)S(1)} %project_given.1), channel_id=1, source_target_pairs={{0,2},{2,0},{1,3},{3,1},{4,6},{6,4},{5,7},{7,5},{8,10},{10,8},{9,1... | collective-permute-start | bytes 1179656 | tf_op jit(solution)/shard_map/ppermute | solution.py:201
  59.4 1.0 %project_own.1.own_ref = f32[64,3072]{1,0:T(8,128)S(1)} custom-call(bf16[128,384]{1,0:T(8,128)(2,1)S(1)} %get-tuple-element.13.keep_ref, bf16[128,384]{1,0:T(8,128)(2,1)S(1)} %collective-permute-done.3.got_ref, bf16[384,3072]{1,0:T(8,128)(2,1)S(1)} %get-tuple-element.15.w_mine, bf16[384,3072]{1,0:T(8,128)(2,1)S(1)} %collective-permute-done.4.w_other), custom_call_target="tpu_custom_call" | custom-call | tf_op jit(solution)/shard_map/project_own/pallas_call | solution.py:135
  60.3 9.3 %collective-permute-done.5.got_ref = bf16[64,3072]{1,0:T(8,128)(2,1)S(1)} collective-permute-done((bf16[64,3072]{1,0:T(8,128)(2,1)S(1)}, bf16[64,3072]{1,0:T(8,128)(2,1)S(1)}, u32[]{:S(2)}, u32[]{:S(2)}) %collective-permute-start.5) | collective-permute-done | bytes 393248 | tf_op jit(solution)/shard_map/ppermute | solution.py:201
  69.7 0.0 copy-done
  69.7 0.0 copy-done.1
  69.7 0.0 copy-done.3
  69.7 1.6 %finish.1 = bf16[64,3072]{1,0:T(8,128)(2,1)} custom-call(s32[8,16]{1,0:T(8,128)S(1)} %copy-done.2, s32[8]{0:T(128)S(1)} %copy-done.3, f32[64,3072]{1,0:T(8,128)S(1)} %project_own.1.own_ref, bf16[64,3072]{1,0:T(8,128)(2,1)S(1)} %collective-permute-done.5.got_ref, bf16[64,3072]{1,0:T(8,128)(2,1)S(1)} %copy-done, f32[8,3072]{1,0:T(8,128)S(1)} %copy-done.1), custom_call_target="tpu_custom_call" | custom-call | tf_op jit(solution)/shard_map/finish/pallas_call | solution.py:135
  (4 shorter events, 0.1 us)
Async XLA Ops:
  0.0 7.0 %copy-start.5 = (bf16[256,384]{1,0:T(8,128)(2,1)S(1)}, bf16[256,384]{1,0:T(8,128)(2,1)}, u32[]{:S(2)}) copy-start(bf16[256,384]{1,0:T(8,128)(2,1)} %param.10) | copy-start | bytes 589828
  0.0 7.0 %copy-start.4 = (bf16[256,384]{1,0:T(8,128)(2,1)S(1)}, bf16[256,384]{1,0:T(8,128)(2,1)}, u32[]{:S(2)}) copy-start(bf16[256,384]{1,0:T(8,128)(2,1)} %param.11) | copy-start | bytes 589828
  0.0 21.7 %copy-start.2 = (s32[8,16]{1,0:T(8,128)S(1)}, s32[8,16]{1,0:T(8,128)}, u32[]{:S(2)}) copy-start(s32[8,16]{1,0:T(8,128)} %split_ref.5) | copy-start | bytes 1540
  2.0 19.7 %all-to-all-start = ((bf16[4,256,384]{2,1,0:T(8,128)(2,1)}), bf16[4,256,384]{2,1,0:T(8,128)(2,1)S(1)}, u32[]{:S(2)}, u32[]{:S(2)}) async-start(bf16[4,256,384]{2,1,0:T(8,128)(2,1)} %broadcast_in_dim.2), calls=%async_computation | async-start | bytes 1572864 | tf_op jit(solution)/shard_map/all_to_all | solution.py:169
  7.0 14.7 %collective-permute-start.2 = (bf16[2,256,384]{2,1,0:T(8,128)(2,1)S(1)}, bf16[2,256,384]{2,1,0:T(8,128)(2,1)S(1)}, u32[]{:S(2)}, u32[]{:S(2)}) collective-permute-start(bf16[2,256,384]{2,1,0:T(8,128)(2,1)S(1)} %pad_maximum_fusion.kv_a), channel_id=1, source_target_pairs={{0,12},{4,8},{8,4},{12,0},{16,28},{20,24},{24,20},{28,16},{32,44},... | collective-permute-start | bytes 1179656 | tf_op jit(solution)/shard_map/ppermute | solution.py:166
  13.0 13.9 %collective-permute-start = (bf16[2,256,384]{2,1,0:T(8,128)(2,1)S(1)}, bf16[2,256,384]{2,1,0:T(8,128)(2,1)S(1)}, u32[]{:S(2)}, u32[]{:S(2)}) collective-permute-start(bf16[2,256,384]{2,1,0:T(8,128)(2,1)S(1)} %pad_maximum_fusion.kv_a), channel_id=1, source_target_pairs={{0,4},{4,0},{8,12},{12,8},{16,20},{20,16},{24,28},{28,24},{32,36},... | collective-permute-start | bytes 1179656 | tf_op jit(solution)/shard_map/ppermute | solution.py:166
  15.2 11.7 %collective-permute-start.1 = (bf16[2,256,384]{2,1,0:T(8,128)(2,1)S(1)}, bf16[2,256,384]{2,1,0:T(8,128)(2,1)S(1)}, u32[]{:S(2)}, u32[]{:S(2)}) collective-permute-start(bf16[2,256,384]{2,1,0:T(8,128)(2,1)S(1)} %pad_maximum_fusion.kv_a), channel_id=1, source_target_pairs={{0,8},{4,12},{8,0},{12,4},{16,24},{20,28},{24,16},{28,20},{32,40},... | collective-permute-start | bytes 1179656 | tf_op jit(solution)/shard_map/ppermute | solution.py:166
  31.9 12.6 %all-to-all-start.1 = ((bf16[4,288,384]{2,1,0:T(8,128)(2,1)}), bf16[4,288,384]{2,1,0:T(8,128)(2,1)S(1)}, u32[]{:S(2)}, u32[]{:S(2)}) async-start(bf16[4,288,384]{2,1,0:T(8,128)(2,1)} %attend_late.1), calls=%async_computation.1 | async-start | bytes 1769472 | tf_op jit(solution)/shard_map/all_to_all | solution.py:169
  35.6 19.8 %collective-permute-start.4 = (bf16[384,3072]{1,0:T(8,128)(2,1)}, bf16[384,3072]{1,0:T(8,128)(2,1)S(1)}, u32[]{:S(2)}, u32[]{:S(2)}) collective-permute-start(bf16[384,3072]{1,0:T(8,128)(2,1)} %w_any.1), channel_id=1, source_target_pairs={{0,1},{1,0},{2,3},{3,2},{4,5},{5,4},{6,7},{7,6},{8,9},{9,8},{10,11... | collective-permute-start | bytes 7077896 | tf_op jit(solution)/shard_map/ppermute | solution.py:176
  46.4 9.9 %collective-permute-start.3 = (bf16[128,384]{1,0:T(8,128)(2,1)S(1)}, bf16[128,384]{1,0:T(8,128)(2,1)S(1)}, u32[]{:S(2)}, u32[]{:S(2)}) collective-permute-start(bf16[128,384]{1,0:T(8,128)(2,1)S(1)} %get-tuple-element.14), channel_id=1, source_target_pairs={{0,1},{1,0},{2,3},{3,2},{4,5},{5,4},{6,7},{7,6},{8,9},{9,8},{10,11... | collective-permute-start | bytes 294920 | tf_op jit(solution)/shard_map/ppermute | solution.py:193
  57.3 12.4 %copy-start = (bf16[64,3072]{1,0:T(8,128)(2,1)S(1)}, bf16[64,3072]{1,0:T(8,128)(2,1)}, u32[]{:S(2)}) copy-start(bf16[64,3072]{1,0:T(8,128)(2,1)} %latent_ref.1) | copy-start | bytes 1179652
  57.3 12.4 %copy-start.1 = (f32[8,3072]{1,0:T(8,128)S(1)}, f32[8,3072]{1,0:T(8,128)}, u32[]{:S(2)}) copy-start(f32[8,3072]{1,0:T(8,128)} %gate_ref.1) | copy-start | bytes 294916
  57.3 12.4 %copy-start.3 = (s32[8]{0:T(128)S(1)}, s32[8]{0:T(128)}, u32[]{:S(2)}) copy-start(s32[8]{0:T(128)} %text_ref.1) | copy-start | bytes 100
  57.3 12.4 %collective-permute-start.5 = (bf16[64,3072]{1,0:T(8,128)(2,1)S(1)}, bf16[64,3072]{1,0:T(8,128)(2,1)S(1)}, u32[]{:S(2)}, u32[]{:S(2)}) collective-permute-start(bf16[64,3072]{1,0:T(8,128)(2,1)S(1)} %project_given.1), channel_id=1, source_target_pairs={{0,2},{2,0},{1,3},{3,1},{4,6},{6,4},{5,7},{7,5},{8,10},{10,8},{9,1... | collective-permute-start | bytes 1179656 | tf_op jit(solution)/shard_map/ppermute | solution.py:201

commit v6 on v3

--- a/solution.py
+++ b/solution.py
@@ -48,10 +48,10 @@
             k = kv_ref[:, 0, :, cols].reshape(keys, HEAD_DIM)
             s = lax.dot_general(q_ref[:, cols], k, (((1,), (1,)), ((), ())), preferred_element_type=jnp.float32)
             s = s + bias
-            top = jnp.max(s, axis=1, keepdims=True) * SCALE
+            top = jnp.broadcast_to(jnp.max(s, axis=1, keepdims=True) * SCALE, (tokens, LANES))
             high = top.astype(jnp.bfloat16).astype(jnp.float32)
             low = (top - high + jnp.abs(top) * 2.0**-16).astype(jnp.bfloat16).astype(jnp.float32)
-            p = jnp.exp2(s * SCALE - (high + low))
+            p = jnp.exp2(s * SCALE - jnp.tile(high + low, (1, keys // LANES)))
             both = jnp.dot(p.astype(jnp.bfloat16), v_ones[h], preferred_element_type=jnp.float32)
             o, total = both[:, :HEAD_DIM].astype(jnp.bfloat16), both[:, HEAD_DIM:]
             for to, start, quarter in places:
@@ -69,10 +69,10 @@
 def project_kernel(first, part_ref, w_any, w_other, out_ref, w_mine, sems):
     count = out_ref.shape[0]
     rows = pl.ds(first, count)
-    share = w_any.shape[0] // sems.shape[0]
+    share = w_any.shape[1] // sems.shape[0]
     fetches = []
     for i in range(sems.shape[0]):
-        piece = pl.ds(i * share, share)
+        piece = (slice(None), pl.ds(i * share, share))
         fetches.append(pltpu.make_async_copy(w_any.at[piece], w_mine.at[piece], sems.at[i]))
         fetches[i].start()
     width = w_other.shape[0]
@@ -97,11 +97,12 @@
             mixed = sum(a * part_ref[2 * p + head_side, rows, cols].astype(jnp.float32) for p, a in enumerate(e))
             pieces.append((mixed / total).astype(jnp.bfloat16))
         attended.append(jnp.concatenate(pieces, axis=1))
-    both = jnp.dot(attended[0], w_other[...], preferred_element_type=jnp.float32)
-    for fetch in fetches:
+    for i, fetch in enumerate(fetches):
+        cols = slice(i * share, (i + 1) * share)
+        both = jnp.dot(attended[0], w_other[:, cols], preferred_element_type=jnp.float32)
         fetch.wait()
-    both = both + jnp.dot(attended[1], w_mine[...], preferred_element_type=jnp.float32)
-    out_ref[...] = both.astype(out_ref.dtype)
+        both = both + jnp.dot(attended[1], w_mine[:, cols], preferred_element_type=jnp.float32)
+        out_ref[:, cols] = both.astype(out_ref.dtype)
 
 
 def finish_kernel(split_ref, text_ref, own_ref, got_ref, latent_ref, gate_ref, out_ref):

time: 70 us -> 69.9 us (level)
  no operation moved by 1% of the time
where the time goes in v6:
time: 69.9 us; the launch traced here: 69.4 us
  waiting for transfers between devices  27.4 us (39%)
  starting transfers between devices  25.9 us (37%)
  Pallas kernels  13.6 us (19%)
  local copies, waits for them, and re-layouts  1.33 us (2%)
  other arithmetic  1.07 us (2%)
    pallas_call x4, Pallas kernels, call(): pl.pallas_call(kernel, out_shape=[jax.ShapeDtypeStruct(*o) for o in outs]...  13.6 us
    ppermute x3, starting transfers between devices, swap(): return lax.ppermute(x, ('z', 'h'), [(i, i ^ d) for i in range(4)])  10.7 us
    ppermute x3, waiting for transfers between devices, swap(): return lax.ppermute(x, ('z', 'h'), [(i, i ^ d) for i in range(4)])  8.12 us
    all_to_all x1, waiting for transfers between devices, on_device(): parts = lax.all_to_all(parts, ('z', 'h', 'c'), 0, 0, tiled=True)  7.45 us
    ppermute x1, waiting for transfers between devices, on_device(): got = lax.ppermute(give, ('h', 'l', 'c'), along)  5.66 us
    all_to_all x1, starting transfers between devices, on_device(): parts = lax.all_to_all(parts, ('z', 'h', 'c'), 0, 0, tiled=True)  5.65 us
    all_to_all x1, starting transfers between devices, on_device(): kv = lax.all_to_all(stacked, 'y', 0, 0, tiled=True)  4.46 us
    ppermute x1, waiting for transfers between devices, on_device(): w_other = lax.ppermute(late_weight, 'c', [(0, 1), (1, 0)])  4.35 us
  transfers between devices with their start and end apart: 7, of which 6 were waited for; matrix products, arithmetic and copies ran while one was open for 0% of the time, Pallas kernels for 4%

profile of v6, /device:TPU:64, one launch (start us, length us, event | category | flops | bytes accessed | tf_op | source)
XLA Modules:
  0.0 69.4 jit_solution(3880422419923833650)
XLA Ops:
  0.0 1.1 %pad_maximum_fusion = bf16[2,256,384]{2,1,0:T(8,128)(2,1)S(1)} fusion(bf16[1,256,384]{2,1,0:T(8,128)(2,1)} %bitcast.2, bf16[1,256,384]{2,1,0:T(8,128)(2,1)} %bitcast.3), kind=kLoop, calls=%fused_computation | loop fusion | flops 196608 | bytes 786432 | tf_op jit(solution)/shard_map/stack | solution.py:150
  1.1 0.0 copy-start.1
  1.1 0.0 copy-start.3
  1.1 1.3 %broadcast_in_dim.2 = bf16[4,2,256,384]{3,2,1,0:T(8,128)(2,1)} broadcast(bf16[2,256,384]{2,1,0:T(8,128)(2,1)S(1)} %pad_maximum_fusion), dimensions={1,2,3} | broadcast | bytes 1966080 | tf_op jit(solution)/shard_map/broadcast_in_dim | solution.py:150
  2.4 4.5 %all-to-all-start = ((bf16[4,2,256,384]{3,2,1,0:T(8,128)(2,1)}), bf16[4,2,256,384]{3,2,1,0:T(8,128)(2,1)S(1)}, u32[]{:S(2)}, u32[]{:S(2)}) async-start(bf16[4,2,256,384]{3,2,1,0:T(8,128)(2,1)} %broadcast_in_dim.2), calls=%async_computation | async-start | bytes 3145728 | tf_op jit(solution)/shard_map/all_to_all | solution.py:151
  6.9 0.0 copy-done.1
  6.9 3.8 %collective-permute-start.1 = (bf16[256,384]{1,0:T(8,128)(2,1)S(1)}, bf16[256,384]{1,0:T(8,128)(2,1)S(1)}, u32[]{:S(2)}, u32[]{:S(2)}) collective-permute-start(bf16[256,384]{1,0:T(8,128)(2,1)S(1)} %copy-done.1), channel_id=1, source_target_pairs={{0,32},{16,48},{32,0},{48,16},{1,33},{17,49},{33,1},{49,17},{2,34}... | collective-permute-start | bytes 589832 | tf_op jit(solution)/shard_map/ppermute | solution.py:148
  10.7 4.9 %collective-permute-start = (bf16[256,384]{1,0:T(8,128)(2,1)S(1)}, bf16[256,384]{1,0:T(8,128)(2,1)S(1)}, u32[]{:S(2)}, u32[]{:S(2)}) collective-permute-start(bf16[256,384]{1,0:T(8,128)(2,1)S(1)} %copy-done.1), channel_id=1, source_target_pairs={{0,16},{16,0},{32,48},{48,32},{1,17},{17,1},{33,49},{49,33},{2,18}... | collective-permute-start | bytes 589832 | tf_op jit(solution)/shard_map/ppermute | solution.py:148
  15.6 2.0 %collective-permute-start.2 = (bf16[256,384]{1,0:T(8,128)(2,1)S(1)}, bf16[256,384]{1,0:T(8,128)(2,1)S(1)}, u32[]{:S(2)}, u32[]{:S(2)}) collective-permute-start(bf16[256,384]{1,0:T(8,128)(2,1)S(1)} %copy-done.1), channel_id=1, source_target_pairs={{0,48},{16,32},{32,16},{48,0},{1,49},{17,33},{33,17},{49,1},{2,50}... | collective-permute-start | bytes 589832 | tf_op jit(solution)/shard_map/ppermute | solution.py:148
  17.6 0.0 collective-permute-done.1.q2
  17.6 5.8 %collective-permute-done.q1 = bf16[256,384]{1,0:T(8,128)(2,1)S(1)} collective-permute-done((bf16[256,384]{1,0:T(8,128)(2,1)S(1)}, bf16[256,384]{1,0:T(8,128)(2,1)S(1)}, u32[]{:S(2)}, u32[]{:S(2)}) %collective-permute-start) | collective-permute-done | bytes 196640 | tf_op jit(solution)/shard_map/ppermute | solution.py:148
  23.4 2.3 %collective-permute-done.2.q3 = bf16[256,384]{1,0:T(8,128)(2,1)S(1)} collective-permute-done((bf16[256,384]{1,0:T(8,128)(2,1)S(1)}, bf16[256,384]{1,0:T(8,128)(2,1)S(1)}, u32[]{:S(2)}, u32[]{:S(2)}) %collective-permute-start.2) | collective-permute-done | bytes 196640 | tf_op jit(solution)/shard_map/ppermute | solution.py:148
  25.7 1.8 %all-to-all-done.kv_ref = bf16[4,2,256,384]{3,2,1,0:T(8,128)(2,1)S(1)} async-done(((bf16[4,2,256,384]{3,2,1,0:T(8,128)(2,1)}), bf16[4,2,256,384]{3,2,1,0:T(8,128)(2,1)S(1)}, u32[]{:S(2)}, u32[]{:S(2)}) %all-to-all-start) | async-done | bytes 1572896 | tf_op jit(solution)/shard_map/all_to_all | solution.py:151
  27.6 0.0 copy-done.3
  27.6 6.6 %attend.1 = bf16[8,144,384]{2,1,0:T(8,128)(2,1)} custom-call(s32[8,16]{1,0:T(8,128)S(1)} %copy-done.3, bf16[256,384]{1,0:T(8,128)(2,1)S(1)} %copy-done.1, bf16[256,384]{1,0:T(8,128)(2,1)S(1)} %collective-permute-done.q1, bf16[256,384]{1,0:T(8,128)(2,1)S(1)} %collective-permute-done.1.q2, bf16[256,384]{1,0:T(8,128)(2,1)S(1)} %collective-permute-done.2.q3, ...), custom_call_target="tpu_custom_call" | custom-call | tf_op jit(solution)/shard_map/attend/pallas_call | solution.py:127
  34.2 5.7 %all-to-all-start.1 = ((bf16[8,144,384]{2,1,0:T(8,128)(2,1)}), bf16[8,144,384]{2,1,0:T(8,128)(2,1)S(1)}, u32[]{:S(2)}, u32[]{:S(2)}) async-start(bf16[8,144,384]{2,1,0:T(8,128)(2,1)} %attend.1), calls=%async_computation.1 | async-start | bytes 1769472 | tf_op jit(solution)/shard_map/all_to_all | solution.py:159
  39.9 2.4 %collective-permute-start.3 = (bf16[384,3072]{1,0:T(8,128)(2,1)}, bf16[384,3072]{1,0:T(8,128)(2,1)S(1)}, u32[]{:S(2)}, u32[]{:S(2)}) collective-permute-start(bf16[384,3072]{1,0:T(8,128)(2,1)} %w_any.3), channel_id=1, source_target_pairs={{0,1},{1,0},{2,3},{3,2},{4,5},{5,4},{6,7},{7,6},{8,9},{9,8},{10,11... | collective-permute-start | bytes 7077896 | tf_op jit(solution)/shard_map/ppermute | solution.py:154
  42.3 4.3 %collective-permute-done.3.w_other = bf16[384,3072]{1,0:T(8,128)(2,1)S(1)} collective-permute-done((bf16[384,3072]{1,0:T(8,128)(2,1)}, bf16[384,3072]{1,0:T(8,128)(2,1)S(1)}, u32[]{:S(2)}, u32[]{:S(2)}) %collective-permute-start.3) | collective-permute-done | bytes 2359328 | tf_op jit(solution)/shard_map/ppermute | solution.py:154
  46.6 7.4 %all-to-all-done.1.part_ref = bf16[8,144,384]{2,1,0:T(8,128)(2,1)S(1)} async-done(((bf16[8,144,384]{2,1,0:T(8,128)(2,1)}), bf16[8,144,384]{2,1,0:T(8,128)(2,1)S(1)}, u32[]{:S(2)}, u32[]{:S(2)}) %all-to-all-start.1) | async-done | bytes 884768 | tf_op jit(solution)/shard_map/all_to_all | solution.py:159
  54.1 2.7 %project_given.1 = bf16[64,3072]{1,0:T(8,128)(2,1)S(1)} custom-call(bf16[8,144,384]{2,1,0:T(8,128)(2,1)S(1)} %all-to-all-done.1.part_ref, bf16[384,3072]{1,0:T(8,128)(2,1)} %w_any.3, bf16[384,3072]{1,0:T(8,128)(2,1)S(1)} %collective-permute-done.3.w_other), custom_call_target="tpu_custom_call" | custom-call | tf_op jit(solution)/shard_map/project_given/pallas_call | solution.py:127
  56.8 0.0 copy-start
  56.8 0.0 copy-start.2
  56.8 0.0 copy-start.4
  56.8 2.6 %collective-permute-start.4 = (bf16[64,3072]{1,0:T(8,128)(2,1)S(1)}, bf16[64,3072]{1,0:T(8,128)(2,1)S(1)}, u32[]{:S(2)}, u32[]{:S(2)}) collective-permute-start(bf16[64,3072]{1,0:T(8,128)(2,1)S(1)} %project_given.1), channel_id=1, source_target_pairs={{0,2},{1,19},{2,16},{3,1},{16,18},{17,3},{18,0},{19,17},{4,6},{5,2... | collective-permute-start | bytes 1179656 | tf_op jit(solution)/shard_map/ppermute | solution.py:171
  59.5 2.7 %project_own.1.own_ref = f32[64,3072]{1,0:T(8,128)S(1)} custom-call(bf16[8,144,384]{2,1,0:T(8,128)(2,1)S(1)} %all-to-all-done.1.part_ref, bf16[384,3072]{1,0:T(8,128)(2,1)} %w_any.3, bf16[384,3072]{1,0:T(8,128)(2,1)S(1)} %collective-permute-done.3.w_other), custom_call_target="tpu_custom_call" | custom-call | tf_op jit(solution)/shard_map/project_own/pallas_call | solution.py:127
  62.2 5.7 %collective-permute-done.4.got_ref = bf16[64,3072]{1,0:T(8,128)(2,1)S(1)} collective-permute-done((bf16[64,3072]{1,0:T(8,128)(2,1)S(1)}, bf16[64,3072]{1,0:T(8,128)(2,1)S(1)}, u32[]{:S(2)}, u32[]{:S(2)}) %collective-permute-start.4) | collective-permute-done | bytes 393248 | tf_op jit(solution)/shard_map/ppermute | solution.py:171
  67.8 0.0 copy-done
  67.8 0.0 copy-done.2
  67.8 0.0 copy-done.4
  67.9 1.6 %finish.1 = bf16[64,3072]{1,0:T(8,128)(2,1)} custom-call(s32[8,16]{1,0:T(8,128)S(1)} %copy-done.3, s32[8]{0:T(128)S(1)} %copy-done.4, f32[64,3072]{1,0:T(8,128)S(1)} %project_own.1.own_ref, bf16[64,3072]{1,0:T(8,128)(2,1)S(1)} %collective-permute-done.4.got_ref, bf16[64,3072]{1,0:T(8,128)(2,1)S(1)} %copy-done, f32[8,3072]{1,0:T(8,128)S(1)} %copy-done.2), custom_call_target="tpu_custom_call" | custom-call | tf_op jit(solution)/shard_map/finish/pallas_call | solution.py:127
Async XLA Ops:
  1.1 5.8 %copy-start.1 = (bf16[256,384]{1,0:T(8,128)(2,1)S(1)}, bf16[256,384]{1,0:T(8,128)(2,1)}, u32[]{:S(2)}) copy-start(bf16[256,384]{1,0:T(8,128)(2,1)} %q0.1) | copy-start | bytes 589828
  1.1 26.5 %copy-start.3 = (s32[8,16]{1,0:T(8,128)S(1)}, s32[8,16]{1,0:T(8,128)}, u32[]{:S(2)}) copy-start(s32[8,16]{1,0:T(8,128)} %split_ref.3) | copy-start | bytes 1540
  2.4 25.2 %all-to-all-start = ((bf16[4,2,256,384]{3,2,1,0:T(8,128)(2,1)}), bf16[4,2,256,384]{3,2,1,0:T(8,128)(2,1)S(1)}, u32[]{:S(2)}, u32[]{:S(2)}) async-start(bf16[4,2,256,384]{3,2,1,0:T(8,128)(2,1)} %broadcast_in_dim.2), calls=%async_computation | async-start | bytes 3145728 | tf_op jit(solution)/shard_map/all_to_all | solution.py:151
  6.9 10.7 %collective-permute-start.1 = (bf16[256,384]{1,0:T(8,128)(2,1)S(1)}, bf16[256,384]{1,0:T(8,128)(2,1)S(1)}, u32[]{:S(2)}, u32[]{:S(2)}) collective-permute-start(bf16[256,384]{1,0:T(8,128)(2,1)S(1)} %copy-done.1), channel_id=1, source_target_pairs={{0,32},{16,48},{32,0},{48,16},{1,33},{17,49},{33,1},{49,17},{2,34}... | collective-permute-start | bytes 589832 | tf_op jit(solution)/shard_map/ppermute | solution.py:148
  10.7 12.7 %collective-permute-start = (bf16[256,384]{1,0:T(8,128)(2,1)S(1)}, bf16[256,384]{1,0:T(8,128)(2,1)S(1)}, u32[]{:S(2)}, u32[]{:S(2)}) collective-permute-start(bf16[256,384]{1,0:T(8,128)(2,1)S(1)} %copy-done.1), channel_id=1, source_target_pairs={{0,16},{16,0},{32,48},{48,32},{1,17},{17,1},{33,49},{49,33},{2,18}... | collective-permute-start | bytes 589832 | tf_op jit(solution)/shard_map/ppermute | solution.py:148
  15.6 10.1 %collective-permute-start.2 = (bf16[256,384]{1,0:T(8,128)(2,1)S(1)}, bf16[256,384]{1,0:T(8,128)(2,1)S(1)}, u32[]{:S(2)}, u32[]{:S(2)}) collective-permute-start(bf16[256,384]{1,0:T(8,128)(2,1)S(1)} %copy-done.1), channel_id=1, source_target_pairs={{0,48},{16,32},{32,16},{48,0},{1,49},{17,33},{33,17},{49,1},{2,50}... | collective-permute-start | bytes 589832 | tf_op jit(solution)/shard_map/ppermute | solution.py:148
  34.2 19.9 %all-to-all-start.1 = ((bf16[8,144,384]{2,1,0:T(8,128)(2,1)}), bf16[8,144,384]{2,1,0:T(8,128)(2,1)S(1)}, u32[]{:S(2)}, u32[]{:S(2)}) async-start(bf16[8,144,384]{2,1,0:T(8,128)(2,1)} %attend.1), calls=%async_computation.1 | async-start | bytes 1769472 | tf_op jit(solution)/shard_map/all_to_all | solution.py:159
  39.9 6.8 %collective-permute-start.3 = (bf16[384,3072]{1,0:T(8,128)(2,1)}, bf16[384,3072]{1,0:T(8,128)(2,1)S(1)}, u32[]{:S(2)}, u32[]{:S(2)}) collective-permute-start(bf16[384,3072]{1,0:T(8,128)(2,1)} %w_any.3), channel_id=1, source_target_pairs={{0,1},{1,0},{2,3},{3,2},{4,5},{5,4},{6,7},{7,6},{8,9},{9,8},{10,11... | collective-permute-start | bytes 7077896 | tf_op jit(solution)/shard_map/ppermute | solution.py:154
  56.8 11.1 %copy-start = (bf16[64,3072]{1,0:T(8,128)(2,1)S(1)}, bf16[64,3072]{1,0:T(8,128)(2,1)}, u32[]{:S(2)}) copy-start(bf16[64,3072]{1,0:T(8,128)(2,1)} %latent_ref.1) | copy-start | bytes 1179652
  56.8 11.0 %copy-start.2 = (f32[8,3072]{1,0:T(8,128)S(1)}, f32[8,3072]{1,0:T(8,128)}, u32[]{:S(2)}) copy-start(f32[8,3072]{1,0:T(8,128)} %gate_ref.1) | copy-start | bytes 294916
  56.8 11.0 %copy-start.4 = (s32[8]{0:T(128)S(1)}, s32[8]{0:T(128)}, u32[]{:S(2)}) copy-start(s32[8]{0:T(128)} %text_ref.1) | copy-start | bytes 100
  56.8 11.0 %collective-permute-start.4 = (bf16[64,3072]{1,0:T(8,128)(2,1)S(1)}, bf16[64,3072]{1,0:T(8,128)(2,1)S(1)}, u32[]{:S(2)}, u32[]{:S(2)}) collective-permute-start(bf16[64,3072]{1,0:T(8,128)(2,1)S(1)} %project_given.1), channel_id=1, source_target_pairs={{0,2},{1,19},{2,16},{3,1},{16,18},{17,3},{18,0},{19,17},{4,6},{5,2... | collective-permute-start | bytes 1179656 | tf_op jit(solution)/shard_map/ppermute | solution.py:171
